TPU v7x, 256 devices: a whole 4x4x8 slice. The times are simulated.
256 devices in a mesh: row: 4 (over x), col: 16 (over z, core), depth: 4 (over y).
Axes of the slice: x: 4, y: 4, z: 8, core: 2. Of those that a mesh axis runs over, the one named last changes fastest.
Arguments:
- amplitudes: float32 [8, 768, 6144], P('depth', 'col', 'row'), may hold values from -6 to 6
- integrals: float32 [8, 768, 16, 768], P('depth', 'row', 'col'), may hold values from -0.21875 to 0.21875
- irrep_virtual: int32 [768], replicated, may hold values from 0 to 7, as said below
- irrep_first: int32 [8], replicated, may hold values from 0 to 7
- irrep_second: int32 [8], replicated, may hold values from 0 to 7
- irrep_target: int32 [16], replicated, may hold values from 0 to 7
Outputs:
- cycle_term: float32 [16, 768, 6144], P('col', 'depth', 'row')
Inputs may be any that keep to these rules, and one draw needn't show every extreme that they name: `irrep_virtual`: labels never fall along the virtual orbitals, so each irrep is one contiguous block, the blocks in rising order of irrep; every irrep holds 64 or more virtuals.
All inputs are finite; a program needn't handle non-finite values.
Results may differ from a plain program's by a relative error of at most 0.0001.
Values sent between devices are 32-bit elements; how exact they have to be, the bound alone decides.
No kernel may reach another device: no remote copies, remote signals or barrier semaphores. Data moves between devices by JAX's collectives and lax.ppermute only.
A program may use at most 64 MiB of HBM per device.

v0:
```python
import jax
import jax.numpy as jnp
from jax import lax
from jax.sharding import PartitionSpec as P


def amp_mask(labels_k, labels_c, labels_x):
    parity = jnp.bitwise_xor(
        jnp.bitwise_xor(labels_k[:, None, None], labels_c[None, :, None]), labels_x[None, None, :]
    )
    return (parity == 0).astype(jnp.float32)


def int_mask(labels_k, labels_c, labels_j, labels_b):
    parity = jnp.bitwise_xor(
        jnp.bitwise_xor(labels_k[:, None, None, None], labels_c[None, :, None, None]),
        jnp.bitwise_xor(labels_j[None, None, :, None], labels_b[None, None, None, :]),
    )
    return (parity == 0).astype(jnp.float32)


def contract(left_amp, right_int):
    return jnp.einsum(
        "kcjb,kcx->jbx",
        right_int,
        left_amp,
        precision=lax.Precision.HIGHEST,
        preferred_element_type=jnp.float32,
    )


def per_device(amplitudes, integrals, irrep_virtual, irrep_first, irrep_second, irrep_target):
    k_local = amplitudes.shape[0]
    x_local = amplitudes.shape[2]
    j_local = integrals.shape[2]
    all_x = jnp.bitwise_xor(irrep_virtual[:, None], irrep_first[None, :]).reshape(-1)
    labels_k = lax.dynamic_slice_in_dim(irrep_second, lax.axis_index("depth") * k_local, k_local)
    labels_x = lax.dynamic_slice_in_dim(all_x, lax.axis_index("row") * x_local, x_local)
    labels_j = lax.dynamic_slice_in_dim(irrep_target, lax.axis_index("col") * j_local, j_local)
    gathered = lax.all_gather(amplitudes, "col", axis=1, tiled=True)
    gathered = gathered * amp_mask(labels_k, irrep_virtual, labels_x)
    masked = lax.all_gather(integrals, "row", axis=1, tiled=True) * int_mask(
        labels_k, irrep_virtual, labels_j, irrep_virtual
    )
    partial_sum = contract(gathered, masked)
    return lax.psum_scatter(partial_sum, "depth", scatter_dimension=1, tiled=True)


def solution(mesh):
    return jax.shard_map(
        per_device,
        mesh=mesh,
        in_specs=(P("depth", "col", "row"), P("depth", "row", "col", None), P(), P(), P(), P()),
        out_specs=P("col", "depth", "row"),
        check_vma=False,
    )
```

profile of v0, /device:TPU:1, one launch (start us, length us, event | category | flops | bytes accessed | tf_op | source)
XLA Modules:
  0.0 219.6 jit_solution(11587721565921521954)
XLA Ops:
  6.5 0.0 all-gather.3.cloned.1.call-start
  6.5 0.7 all-gather.3.cloned.1.call-update
  7.3 0.0 all-gather.5.cloned.1.call-start
  7.3 0.7 all-gather.5.cloned.1.call-update
  8.0 0.0 reduce-scatter.2.cloned.1.call-start
  8.1 0.9 broadcast_xor_fusion
  8.9 0.2 xor.105
  9.1 1.2 dynamic_slice.10
  10.4 0.7 dynamic_slice.9
  11.1 0.1 dynamic_slice.11
  11.2 1.3 broadcast_xor_fusion.2
  12.5 0.8 broadcast_xor_fusion.1
  13.3 54.6 %all-gather.3.cloned.1.call-done = f32[2,768,1,768]{3,2,1,0:T(1,128)} async-done(((f32[2,192,1,768]{3,2,1,0:T(1,128)}), f32[2,768,1,768]{3,2,1,0:T(1,128)}) %all-gather.3.cloned.1.call-update) | async-done | bytes 4718608 | tf_op jit(solution)/shard_map/all_gather | solution.py:42
  67.9 8.2 %compare_select_fusion = f32[2,768,1,768]{3,2,1,0:T(1,128)} fusion(f32[2,768,1,768]{3,2,1,0:T(1,128)} %all-gather.3.cloned.1.call-done, s32[768]{0:T(1024)S(1)} %broadcast_xor_fusion.2, s32[2,768]{1,0:T(2,128)S(1)} %broadcast_xor_fusion.1), kind=kLoop, calls=%fused_computation | loop fusion | flops 3538944 | bytes 9446400 | tf_op jit(solution)/shard_map/mul | solution.py:42
  76.1 55.5 %all-gather.5.cloned.1.call-done = f32[2,768,1536]{2,1,0:T(8,128)} async-done(((f32[2,48,1536]{2,1,0:T(8,128)}), f32[2,768,1536]{2,1,0:T(8,128)}) %all-gather.5.cloned.1.call-update) | async-done | bytes 9437200 | tf_op jit(solution)/shard_map/all_gather | solution.py:40
  131.6 29.5 %fusion.8 = f32[1,768,1536]{2,1,0:T(8,128)} fusion(f32[2,768,1536]{2,1,0:T(8,128)} %all-gather.5.cloned.1.call-done, s32[1536]{0:T(1024)S(1)} %dynamic_slice.11, s32[2,768]{1,0:T(2,128)S(1)} %broadcast_xor_fusion.1, f32[2,768,1,768]{3,2,1,0:T(1,128)} %compare_select_fusion), kind=kOutput, calls=%fused_computation.10 | convolution fusion | flops 21750349824 | bytes 18886656 | tf_op jit(solution)/shard_map/kcjb,kcx->jbx/dot_general | solution.py:23
  161.1 0.0 reduce-scatter.2.cloned.1.call-update
  161.1 51.9 %reduce-scatter.2.cloned.1.call-done = f32[1,192,1536]{2,1,0:T(8,128)} async-done(((f32[1,768,1536]{2,1,0:T(8,128)}), f32[1,192,1536]{2,1,0:T(8,128)}) %reduce-scatter.2.cloned.1.call-update) | async-done | bytes 1179664 | tf_op jit(solution)/shard_map/reduce_scatter | solution.py:46
Async XLA Ops:
  6.5 61.4 %all-gather.3.cloned.1.call-start = ((), (), s32[]{:S(2)}) async-start(), calls=%async_computation.1 | async-start | bytes 5898240 | tf_op jit(solution)/shard_map/all_gather | solution.py:42
  7.3 124.3 %all-gather.5.cloned.1.call-start = ((), (), s32[]{:S(2)}) async-start(), calls=%async_computation.2 | async-start | bytes 10027008 | tf_op jit(solution)/shard_map/all_gather | solution.py:40
  8.0 205.0 %reduce-scatter.2.cloned.1.call-start = ((), (), s32[]{:S(2)}) async-start(), calls=%async_computation.3 | async-start | bytes 5898240 | tf_op jit(solution)/shard_map/reduce_scatter | solution.py:46
Sparse Core Ops, SparseCore 0:
  9.1 58.7 all-gather.2
  69.7 61.7 all-gather.4
  161.2 51.7 reduce-scatter.1
where the time goes:
time: 220 us
  waiting for transfers between devices  164 us (75%)
  matrix products  29.5 us (13%)
  between operations  13.1 us (6%)
  other arithmetic  11.1 us (5%)
  local copies, waits for them, and re-layouts  2.25 us (1%)
    all_gather x1, waiting for transfers between devices, per_device(): gathered = lax.all_gather(amplitudes, 'col', axis=1, tiled=True)  55.5 us
    all_gather x1, waiting for transfers between devices, per_device(): lax.all_gather(integrals, 'row', axis=1, tiled=True)  54.6 us
    reduce_scatter x1, waiting for transfers between devices, per_device(): lax.psum_scatter(partial_sum, 'depth', scatter_dimension=1, tiled=True)  51.9 us
    dot_general x1, matrix products, contract(): jnp.einsum('kcjb,kcx->jbx', right_int, left_amp, precision=lax.Precision....  29.5 us
    mul x1, other arithmetic, per_device(): lax.all_gather(integrals, 'row', axis=1, tiled=True)  8.17 us
  transfers between devices with their start and end apart: 3, of which 3 were waited for; matrix products, arithmetic and copies ran while one was open for 6% of the time, Pallas kernels for 0%

commit v1 on v0

v1 whole, which is shorter than its diff:
```python
import functools

import jax
import jax.numpy as jnp
from jax import lax
from jax.experimental import pallas as pl
from jax.experimental.pallas import tpu as pltpu
from jax.sharding import PartitionSpec as P

LANES = 512
BLOCK = 128
SMEM = pl.BlockSpec(memory_space=pltpu.SMEM)
VMEM = pl.BlockSpec(memory_space=pltpu.VMEM)
ANY = pl.BlockSpec(memory_space=pl.ANY)
F32, BF16, I32 = jnp.float32, jnp.bfloat16, jnp.int32


def label_of(place, starts):
    label = jnp.zeros_like(place)
    for irrep in range(1, 8):
        label = label + (place >= starts[irrep]).astype(I32)
    return label


def choose(index, scalars):
    out = jnp.full_like(index, scalars[0])
    for n in range(1, len(scalars)):
        out = jnp.where(index == n, scalars[n], out)
    return out


def two_terms(x):
    high = x.astype(BF16)
    return high, (x - high.astype(F32)).astype(BF16)


def nt(a, b):
    return lax.dot_general(a, b, (((1,), (1,)), ((), ())), preferred_element_type=F32)


def tn(a, b):
    return lax.dot_general(a, b, (((0,), (0,)), ((), ())), preferred_element_type=F32)


def x_places(pos, starts, first, x_local, oi):
    a_local = x_local // oi
    base = pos[0] * a_local
    x = lax.broadcasted_iota(I32, (1, x_local), 1)
    i = x % oi
    a = base + x // oi
    label = label_of(a, starts)
    firsts = [first[n] for n in range(oi)]
    s = label ^ choose(i, firsts)
    low = [jnp.maximum(starts[n], base) for n in range(8)]
    count = [jnp.maximum(jnp.minimum(starts[n + 1], base + a_local) - low[n], 0) for n in range(8)]
    place = a - choose(label, low)
    for n in range(oi - 1):
        place = place + jnp.where(n < i, choose(s ^ firsts[n], count), 0)
    return s, place - pos[3] * LANES


def pack_t_kernel(pos, starts, first, second, t_ref, out_ref, g_ref, s_ref):
    k_local, c_local, x_local = t_ref.shape
    s, place = x_places(pos, starts, first, x_local, first.shape[0])
    s_ref[...] = jnp.broadcast_to(s, s_ref.shape)
    for n in range(LANES // 128):
        rows = n * 128 + lax.broadcasted_iota(I32, (128, x_local), 0)
        g_ref[n * 128 : n * 128 + 128, :] = jnp.where(rows == place, 1.0, 0.0).astype(BF16)
    c = pos[1] * c_local + lax.broadcasted_iota(I32, (c_local, 1), 0)
    label = label_of(c, starts)
    parts = []
    for k in range(k_local):
        keep = (label ^ second[pos[2] * k_local + k]) == s
        parts.extend(two_terms(jnp.where(keep, t_ref[k], 0.0)))
    packed = nt(jnp.concatenate(parts, 0), g_ref[...])
    for k in range(k_local):
        n = 2 * k * c_local
        out_ref[k] = packed[n : n + c_local] + packed[n + c_local : n + 2 * c_local]


def pack_w_kernel(pos, starts, second, target, w_ref, out_ref):
    k_local, c_local, _ = out_ref.shape
    rows = k_local * c_local
    tiles = w_ref.shape[0] // rows
    row = lax.broadcasted_iota(I32, (c_local, 1), 0)
    label = label_of(pos[0] * c_local + row, starts) ^ target[pos[1]]
    wanted = jnp.concatenate([label ^ second[pos[2] * k_local + k] for k in range(k_local)], 0)
    firsts = [starts[n] // 8 * 8 for n in range(8)]
    total = jnp.zeros((2 * rows, BLOCK), F32)
    for q in range(tiles):
        b = q * 128 + lax.broadcasted_iota(I32, (1, 128), 1)
        label_b = label_of(b, starts)
        place = b - choose(label_b, firsts) - pos[4] * BLOCK
        hot = jnp.where(lax.broadcasted_iota(I32, (BLOCK, 128), 0) == place, 1.0, 0.0).astype(BF16)
        w = jnp.where(wanted == label_b, w_ref[pl.ds(q, rows, stride=tiles), :], 0.0)
        total = total + nt(jnp.concatenate(two_terms(w), 0), hot)
    for k in range(k_local):
        out_ref[k] = total[k * c_local : (k + 1) * c_local] + total[rows + k * c_local : rows + (k + 1) * c_local]


def product_kernel(plan, *refs):
    pos, starts, second, target = refs[:4]
    pieces = refs[4 : 4 + len(plan)]
    outs = refs[4 + len(plan) : 8 + len(plan)]
    t_all, w_all, total, sems = refs[8 + len(plan) :]
    k_local, c_all, _ = t_all.shape
    b_local = outs[0].shape[0]
    copies = []
    for n, (kind, k, shift, piece) in enumerate(zip(*zip(*plan), pieces)):
        size = piece.shape[-2]
        into = t_all if kind == "t" else w_all
        if kind == "t":
            chip = lax.rem(pos[1] // 2 + shift[0] + 8, 8)
            at = (chip * 2 + (pos[1] % 2 if shift[1] == 0 else 1 - pos[1] % 2)) * size
        else:
            at = lax.rem(pos[0] + shift + 4, 4) * size
        at = pl.multiple_of(at, 8)
        if k is None:
            copy = pltpu.make_async_copy(piece, into.at[:, pl.ds(at, size), :], sems.at[n])
        else:
            copy = pltpu.make_async_copy(piece, into.at[pl.ds(k, 1), pl.ds(at, size), :], sems.at[n])
        copy.start()
        copies.append(copy)
    total[...] = jnp.zeros_like(total)
    for copy in copies:
        copy.wait()
    row = lax.broadcasted_iota(I32, (128, 1), 0)
    for irrep in range(8):
        s = target[pos[1]] ^ irrep
        sums = jnp.zeros((BLOCK, LANES), F32)
        for k in range(k_local):
            p = s ^ second[pos[2] * k_local + k]
            begin, end = starts[p], starts[p + 1]
            aligned = begin // 8 * 8

            def step(n, acc, k=k, begin=begin, end=end, aligned=aligned):
                nominal = aligned + n * 128
                at = pl.multiple_of(jnp.minimum(nominal, c_all - 128), 8)
                c = at + row
                keep = (c >= jnp.maximum(begin, nominal)) & (c < end)
                w_high, w_low = two_terms(jnp.where(keep, w_all[k, pl.ds(at, 128), :], 0.0))
                t_high, t_low = two_terms(t_all[k, pl.ds(at, 128), :])
                return acc + tn(w_high, t_high) + tn(w_high, t_low) + tn(w_low, t_high)

            sums = lax.fori_loop(0, (end - aligned + 127) // 128, step, sums)
        at = starts[irrep] // 8 * 8 + pos[4] * BLOCK

        @pl.when(at < starts[irrep + 1])
        def _(at=pl.multiple_of(at, 8), sums=sums):
            total[pl.ds(at, BLOCK), :] += sums

    copies = []
    for n, out in enumerate(outs):
        at = pl.multiple_of(lax.rem(pos[2] + n, 4) * b_local, 8)
        copy = pltpu.make_async_copy(total.at[pl.ds(at, b_local), :], out, sems.at[n])
        copy.start()
        copies.append(copy)
    for copy in copies:
        copy.wait()


def expand_kernel(pos, starts, target, g_ref, s_ref, *refs):
    out_ref = refs[-1]
    b_local = refs[0].shape[0]
    sums = refs[0][...] + refs[1][...] + (refs[2][...] + refs[3][...])
    both = jnp.dot(jnp.concatenate(two_terms(sums), 0), g_ref[...], preferred_element_type=F32)
    b = pos[2] * b_local + lax.broadcasted_iota(I32, (b_local, 1), 0)
    keep = (label_of(b, starts) ^ target[pos[1]]) == s_ref[:1, :]
    value = jnp.where(keep, both[:b_local] + both[b_local:], 0.0)
    out_ref[0] = value + refs[4][0] if len(refs) > 5 else value


def params():
    return pltpu.CompilerParams(vmem_limit_bytes=48 * 1024 * 1024)


def one_pass(pos, starts, first, second, target, amplitudes, integrals, before):
    k_local, c_local, x_local = amplitudes.shape
    w_rows = integrals.shape[1]
    v = integrals.shape[3]
    b_local = v // 4
    shape = jax.ShapeDtypeStruct
    t0, hot, s_of = pl.pallas_call(
        pack_t_kernel,
        out_shape=(shape((k_local, c_local, LANES), F32), shape((LANES, x_local), BF16), shape((8, x_local), I32)),
        in_specs=[SMEM] * 4 + [VMEM],
        out_specs=(VMEM,) * 3,
        compiler_params=params(),
        name="pack_t",
    )(pos, starts, first, second, amplitudes)
    w0 = pl.pallas_call(
        pack_w_kernel,
        out_shape=shape((k_local, w_rows, BLOCK), F32),
        in_specs=[SMEM] * 4 + [VMEM],
        out_specs=VMEM,
        compiler_params=params(),
        name="pack_w",
    )(pos, starts, second, target, integrals.reshape(k_local * w_rows * (v // 128), 128))

    def along(x, axis, n, step):
        return lax.ppermute(x, axis, [(i, (i + step) % n) for i in range(n)])

    def swap(x):
        return lax.ppermute(x, "col", [(i, i ^ 1) for i in range(16)])

    got = [(None, (0, 0), t0)]
    right = left = t0
    for n in range(1, 4):
        right, left = along(right, "col", 16, 2), along(left, "col", 16, -2)
        got += [(None, (-n, 0), right), (None, (n, 0), left)]
    got += [(0, (4, 0), along(right[:1], "col", 16, 2)), (1, (4, 0), along(left[1:], "col", 16, -2))]
    got += [(k, (shift[0], 1), swap(piece)) for k, shift, piece in got]
    plan = [("t", k, shift) for k, shift, _ in got]
    pieces = [piece for _, _, piece in got]
    plan += [("w", None, -n) for n in range(4)]
    pieces += [w0] + [along(w0, "row", 4, n) for n in range(1, 4)]
    sums = pl.pallas_call(
        functools.partial(product_kernel, plan),
        out_shape=(shape((b_local, LANES), F32),) * 4,
        in_specs=[SMEM] * 4 + [ANY] * len(pieces),
        out_specs=(ANY,) * 4,
        scratch_shapes=[
            pltpu.VMEM((k_local, v, LANES), F32),
            pltpu.VMEM((k_local, v, BLOCK), F32),
            pltpu.VMEM((v + BLOCK, LANES), F32),
            pltpu.SemaphoreType.DMA((len(pieces),)),
        ],
        compiler_params=params(),
        name="product",
    )(pos, starts, second, target, *pieces)
    sums = [sums[0]] + [along(sums[n], "depth", 4, n) for n in range(1, 4)]
    more = [] if before is None else [before]
    return pl.pallas_call(
        expand_kernel,
        out_shape=shape((1, b_local, x_local), F32),
        in_specs=[SMEM] * 3 + [VMEM] * (6 + len(more)),
        out_specs=VMEM,
        compiler_params=params(),
        name="expand",
    )(pos, starts, target, hot, s_of, *sums, *more)


def per_device(amplitudes, integrals, irrep_virtual, irrep_first, irrep_second, irrep_target):
    v = irrep_virtual.shape[0]
    a_local = amplitudes.shape[2] // irrep_first.shape[0]
    starts = jnp.sum((irrep_virtual[None, :] < jnp.arange(16, dtype=I32)[:, None]).astype(I32), axis=1)
    where = [lax.axis_index(n).astype(I32) for n in ("row", "col", "depth")]

    def position(n_lane, n_block):
        return jnp.stack(where + [n_lane, n_block, 0, 0, 0]).astype(I32)

    def run(n_lane, n_block, before):
        return one_pass(
            position(n_lane, n_block), starts, irrep_first, irrep_second, irrep_target, amplitudes, integrals, before
        )

    out = run(jnp.int32(0), jnp.int32(0), None)
    edges = jnp.arange(0, v, a_local, dtype=I32)
    low, high = starts[:8], starts[1:9]
    count = jnp.maximum(jnp.minimum(high, edges[:, None] + a_local) - jnp.maximum(low, edges[:, None]), 0)
    same = (jnp.arange(8)[:, None, None] ^ irrep_first[None, None, :]) == jnp.arange(8)[None, :, None]
    most = jnp.max(jnp.sum(count[:, None, :, None] * same[None].astype(I32), axis=(2, 3)))
    n_lanes = (most + LANES - 1) // LANES
    n_blocks = (jnp.max(high - low // 8 * 8) + BLOCK - 1) // BLOCK
    return lax.fori_loop(1, n_lanes * n_blocks, lambda n, acc: run(n % n_lanes, n // n_lanes, acc), out)


def solution(mesh):
    return jax.shard_map(
        per_device,
        mesh=mesh,
        in_specs=(P("depth", "col", "row"), P("depth", "row", "col", None), P(), P(), P(), P()),
        out_specs=P("col", "depth", "row"),
        check_vma=False,
    )
```

time: 220 us -> 82.4 us (0.37)
  waiting for transfers between devices: 164 us -> 15.6 us
  starting transfers between devices: 0.08 us -> 34.9 us
  matrix products: 29.5 us -> 0 us
  Pallas kernels: 0 us -> 17.8 us
  between operations: 13.1 us -> 1.43 us
  other arithmetic: 11.1 us -> 6.79 us
  local copies, waits for them, and re-layouts: 2.25 us -> 5.49 us
    all_gather x2 -> x0, waiting for transfers between devices: 110 us -> none  [the longest x1 55.5 us: per_device(): gathered = lax.all_gather(amplitudes, 'col', axis=1, tiled=True)]
    reduce_scatter x1 -> x0, waiting for transfers between devices: 51.9 us -> none  [per_device(): lax.psum_scatter(partial_sum, 'depth', scatter_dimension=1, tiled=True)]
    ppermute x0 -> x23, starting transfers between devices: none -> 34.9 us  [the longest x14 24 us: along(): return lax.ppermute(x, axis, [(i, (i + step) % n) for i in range(n)])]
    dot_general x1 -> x0, matrix products: 29.5 us -> none  [contract(): jnp.einsum('kcjb,kcx->jbx', right_int, left_amp, precision=lax.Precision....]
    pallas_call x0 -> x4, Pallas kernels: none -> 17.8 us  [the longest x1 11.4 us: one_pass(): pl.pallas_call(functools.partial(product_kernel, plan), out_shape=(shape(...]
    ppermute x0 -> x23, waiting for transfers between devices: none -> 15.6 us  [the longest x14 14.7 us: along(): return lax.ppermute(x, axis, [(i, (i + step) % n) for i in range(n)])]
    mul x1, other arithmetic: 8.17 us -> 0.01 us  [per_device(): edges = jnp.arange(0, v, a_local, dtype=I32)]
    reduce_sum x0 -> x2, other arithmetic: none -> 2.79 us  [the longest x1 1.97 us: per_device(): jnp.sum(count[:, None, :, None] * same[None].astype(I32), axis=(2, 3))]
  transfers between devices with their start and end apart: 3 -> 23, of which waited for: 3 -> 6; matrix products, arithmetic and copies ran while one was open for 6% -> 12% of each run, Pallas kernels for 0% -> 2%
where the time goes in v1:
time: 82.4 us; the launch traced here: 82 us
  starting transfers between devices  34.9 us (42%)
  Pallas kernels  17.8 us (22%)
  waiting for transfers between devices  15.6 us (19%)
  other arithmetic  6.79 us (8%)
  local copies, waits for them, and re-layouts  5.49 us (7%)
  between operations  1.43 us (2%)
    ppermute x14, starting transfers between devices, along(): return lax.ppermute(x, axis, [(i, (i + step) % n) for i in range(n)])  24 us
    ppermute x14, waiting for transfers between devices, along(): return lax.ppermute(x, axis, [(i, (i + step) % n) for i in range(n)])  14.7 us
    pallas_call x1, Pallas kernels, one_pass(): pl.pallas_call(functools.partial(product_kernel, plan), out_shape=(shape(...  11.4 us
    ppermute x9, starting transfers between devices, swap(): return lax.ppermute(x, 'col', [(i, i ^ 1) for i in range(16)])  11 us
    pallas_call x1, Pallas kernels, one_pass(): pl.pallas_call(expand_kernel, out_shape=shape((1, b_local, x_local), F32)...  2.97 us
    reshape x1, local copies, waits for them, and re-layouts, one_pass(): integrals.reshape(k_local * w_rows * (v // 128), 128)  2.35 us
    pallas_call x1, Pallas kernels, one_pass(): pl.pallas_call(pack_t_kernel, out_shape=(shape((k_local, c_local, LANES),...  2.05 us
    reduce_sum x1, other arithmetic, per_device(): jnp.sum(count[:, None, :, None] * same[None].astype(I32), axis=(2, 3))  1.97 us
  transfers between devices with their start and end apart: 23, of which 6 were waited for; matrix products, arithmetic and copies ran while one was open for 12% of the time, Pallas kernels for 2%

profile of v1, /device:TPU:1, one launch (start us, length us, event | category | flops | bytes accessed | tf_op | source)
XLA Modules:
  0.0 82.0 jit_solution(15249018228345440193)
XLA Ops:
  0.0 0.8 convert_reduce_fusion.starts.refs_1_
  0.8 0.1 stack.48.pos.refs_0_
  0.9 2.0 %pack_t.5 = (f32[2,48,512]{2,1,0:T(8,128)S(1)}, bf16[512,1536]{1,0:T(8,128)(2,1)S(1)}, s32[8,1536]{1,0:T(8,128)S(1)}) custom-call(s32[8]{0:T(128)S(1)} %stack.48.pos.refs_0_, s32[16]{0:T(128)S(1)} %convert_reduce_fusion.starts.refs_1_, s32[8]{0:T(128)} %first.1, s32[8]{0:T(128)} %refs_2_.1, f32[2,48,1536]{2,1,0:T(8,128)} %t_ref.1), custom_call_target="tpu_custom_call" | custom-call | tf_op jit(solution)/shard_map/pack_t/pallas_call | solution.py:183
  3.0 0.6 copy-done.2
  3.6 6.4 %collective-permute-start.24 = (f32[2,48,512]{2,1,0:T(8,128)S(1)}, f32[2,48,512]{2,1,0:T(8,128)S(1)}, u32[]{:S(2)}, u32[]{:S(2)}) collective-permute-start(f32[2,48,512]{2,1,0:T(8,128)S(1)} %get-tuple-element.195.refs_4_), channel_id=1, source_target_pairs={{0,56},{4,60},{8,0},{12,4},{16,8},{20,12},{24,16},{28,20},{32,24},... | collective-permute-start | bytes 589832 | tf_op jit(solution)/shard_map/ppermute | solution.py:201
  10.0 0.0 collective-permute-start.23
  10.0 3.6 %collective-permute-done.24.refs_6_ = f32[2,48,512]{2,1,0:T(8,128)S(1)} collective-permute-done((f32[2,48,512]{2,1,0:T(8,128)S(1)}, f32[2,48,512]{2,1,0:T(8,128)S(1)}, u32[]{:S(2)}, u32[]{:S(2)}) %collective-permute-start.24) | collective-permute-done | bytes 196640 | tf_op jit(solution)/shard_map/ppermute | solution.py:201
  13.6 3.4 %collective-permute-start.26 = (f32[2,48,512]{2,1,0:T(8,128)S(1)}, f32[2,48,512]{2,1,0:T(8,128)S(1)}, u32[]{:S(2)}, u32[]{:S(2)}) collective-permute-start(f32[2,48,512]{2,1,0:T(8,128)S(1)} %collective-permute-done.24.refs_6_), channel_id=1, source_target_pairs={{0,56},{4,60},{8,0},{12,4},{16,8},{20,12},{24,16},{28,20},{32,24},... | collective-permute-start | bytes 589832 | tf_op jit(solution)/shard_map/ppermute | solution.py:201
  17.0 1.3 %copy-done = f32[2,192,1,768]{3,2,1,0:T(1,128)S(1)} copy-done((f32[2,192,1,768]{3,2,1,0:T(1,128)S(1)}, f32[2,192,1,768]{3,2,1,0:T(1,128)}, u32[]{:S(2)}) %copy-start) | copy-done | bytes 1179672
  18.3 1.4 %pack_w.2.refs_22_ = f32[2,192,128]{2,1,0:T(8,128)S(1)} custom-call(s32[8]{0:T(128)S(1)} %stack.48.pos.refs_0_, s32[16]{0:T(128)S(1)} %convert_reduce_fusion.starts.refs_1_, s32[8]{0:T(128)} %refs_2_.1, s32[16]{0:T(128)} %target.3, f32[2304,128]{1,0:T(8,128)S(1)} %bitcast.28), custom_call_target="tpu_custom_call" | custom-call | tf_op jit(solution)/shard_map/pack_w/pallas_call | solution.py:191
  19.6 2.6 %collective-permute-start.42 = (f32[2,192,128]{2,1,0:T(8,128)S(1)}, f32[2,192,128]{2,1,0:T(8,128)S(1)}, u32[]{:S(2)}, u32[]{:S(2)}) collective-permute-start(f32[2,192,128]{2,1,0:T(8,128)S(1)} %pack_w.2.refs_22_), channel_id=1, source_target_pairs={{0,192},{64,0},{128,64},{192,128},{1,193},{65,1},{129,65},{193,129... | collective-permute-start | bytes 589832 | tf_op jit(solution)/shard_map/ppermute | solution.py:201
  22.2 0.5 collective-permute-start.41
  22.7 0.0 collective-permute-done.26.refs_8_
  22.7 2.7 %collective-permute-start.28 = (f32[2,48,512]{2,1,0:T(8,128)S(1)}, f32[2,48,512]{2,1,0:T(8,128)S(1)}, u32[]{:S(2)}, u32[]{:S(2)}) collective-permute-start(f32[2,48,512]{2,1,0:T(8,128)S(1)} %collective-permute-done.26.refs_8_), channel_id=1, source_target_pairs={{0,56},{4,60},{8,0},{12,4},{16,8},{20,12},{24,16},{28,20},{32,24},... | collective-permute-start | bytes 589832 | tf_op jit(solution)/shard_map/ppermute | solution.py:201
  25.4 0.6 collective-permute-start.40
  26.0 0.9 %collective-permute-done.42.refs_25_ = f32[2,192,128]{2,1,0:T(8,128)S(1)} collective-permute-done((f32[2,192,128]{2,1,0:T(8,128)S(1)}, f32[2,192,128]{2,1,0:T(8,128)S(1)}, u32[]{:S(2)}, u32[]{:S(2)}) %collective-permute-start.42) | collective-permute-done | bytes 196640 | tf_op jit(solution)/shard_map/ppermute | solution.py:201
  26.9 4.6 %collective-permute-start.31 = (f32[2,48,512]{2,1,0:T(8,128)S(1)}, f32[2,48,512]{2,1,0:T(8,128)S(1)}, u32[]{:S(2)}, u32[]{:S(2)}) collective-permute-start(f32[2,48,512]{2,1,0:T(8,128)S(1)} %get-tuple-element.195.refs_4_), channel_id=1, source_target_pairs={{0,4},{4,0},{8,12},{12,8},{16,20},{20,16},{24,28},{28,24},{32,36},... | collective-permute-start | bytes 589832 | tf_op jit(solution)/shard_map/ppermute | solution.py:204
  31.5 0.0 collective-permute-done.41.refs_24_
  31.5 1.9 %collective-permute-start.33 = (f32[2,48,512]{2,1,0:T(8,128)S(1)}, f32[2,48,512]{2,1,0:T(8,128)S(1)}, u32[]{:S(2)}, u32[]{:S(2)}) collective-permute-start(f32[2,48,512]{2,1,0:T(8,128)S(1)} %collective-permute-done.24.refs_6_), channel_id=1, source_target_pairs={{0,4},{4,0},{8,12},{12,8},{16,20},{20,16},{24,28},{28,24},{32,36},... | collective-permute-start | bytes 589832 | tf_op jit(solution)/shard_map/ppermute | solution.py:204
  33.4 0.0 collective-permute-done.28.refs_10_
  33.4 0.0 collective-permute-start.32
  33.4 1.8 %collective-permute-start.35 = (f32[2,48,512]{2,1,0:T(8,128)S(1)}, f32[2,48,512]{2,1,0:T(8,128)S(1)}, u32[]{:S(2)}, u32[]{:S(2)}) collective-permute-start(f32[2,48,512]{2,1,0:T(8,128)S(1)} %collective-permute-done.26.refs_8_), channel_id=1, source_target_pairs={{0,4},{4,0},{8,12},{12,8},{16,20},{20,16},{24,28},{28,24},{32,36},... | collective-permute-start | bytes 589832 | tf_op jit(solution)/shard_map/ppermute | solution.py:204
  35.2 0.6 iota_xor_fusion
  35.8 0.0 collective-permute-done.40.refs_23_
  35.8 0.1 collective-permute-start.34
  35.9 0.0 collective-permute-done.31.refs_13_
  35.9 2.7 %collective-permute-start.30 = (f32[1,48,512]{2,1,0:T(8,128)S(1)}, f32[1,48,512]{2,1,0:T(8,128)S(1)}, u32[]{:S(2)}, u32[]{:S(2)}) collective-permute-start(f32[1,48,512]{2,1,0:T(8,128)S(1)} %slice.31), channel_id=1, source_target_pairs={{0,56},{4,60},{8,0},{12,4},{16,8},{20,12},{24,16},{28,20},{32,24},... | collective-permute-start | bytes 294920 | tf_op jit(solution)/shard_map/ppermute | solution.py:201
  38.7 0.0 collective-permute-start.29
  38.7 0.4 collective-permute-start.37
  39.1 0.2 collective-permute-start.36
  39.3 0.7 subtract_reduce_fusion
  40.0 0.8 collective-permute-done.30.refs_12_
  40.8 0.9 %collective-permute-start.39 = (f32[1,48,512]{2,1,0:T(8,128)S(1)}, f32[1,48,512]{2,1,0:T(8,128)S(1)}, u32[]{:S(2)}, u32[]{:S(2)}) collective-permute-start(f32[1,48,512]{2,1,0:T(8,128)S(1)} %collective-permute-done.30.refs_12_), channel_id=1, source_target_pairs={{0,4},{4,0},{8,12},{12,8},{16,20},{20,16},{24,28},{28,24},{32,36},... | collective-permute-start | bytes 294920 | tf_op jit(solution)/shard_map/ppermute | solution.py:204
  41.7 2.3 %collective-permute-done.29.refs_11_ = f32[1,48,512]{2,1,0:T(8,128)S(1)} collective-permute-done((f32[1,48,512]{2,1,0:T(8,128)S(1)}, f32[1,48,512]{2,1,0:T(8,128)S(1)}, u32[]{:S(2)}, u32[]{:S(2)}) %collective-permute-start.29) | collective-permute-done | bytes 98336 | tf_op jit(solution)/shard_map/ppermute | solution.py:201
  43.9 1.1 %collective-permute-start.38 = (f32[1,48,512]{2,1,0:T(8,128)S(1)}, f32[1,48,512]{2,1,0:T(8,128)S(1)}, u32[]{:S(2)}, u32[]{:S(2)}) collective-permute-start(f32[1,48,512]{2,1,0:T(8,128)S(1)} %collective-permute-done.29.refs_11_), channel_id=1, source_target_pairs={{0,4},{4,0},{8,12},{12,8},{16,20},{20,16},{24,28},{28,24},{32,36},... | collective-permute-start | bytes 294920 | tf_op jit(solution)/shard_map/ppermute | solution.py:204
  45.1 0.9 %collective-permute-done.38.refs_20_ = f32[1,48,512]{2,1,0:T(8,128)S(1)} collective-permute-done((f32[1,48,512]{2,1,0:T(8,128)S(1)}, f32[1,48,512]{2,1,0:T(8,128)S(1)}, u32[]{:S(2)}, u32[]{:S(2)}) %collective-permute-start.38) | collective-permute-done | bytes 98336 | tf_op jit(solution)/shard_map/ppermute | solution.py:204
  46.0 11.4 %product.5 = (f32[192,512]{1,0:T(8,128)S(1)}, f32[192,512]{1,0:T(8,128)}, f32[192,512]{1,0:T(8,128)}, f32[192,512]{1,0:T(8,128)}) custom-call(s32[8]{0:T(128)S(1)} %stack.48.pos.refs_0_, s32[16]{0:T(128)S(1)} %convert_reduce_fusion.starts.refs_1_, s32[8]{0:T(128)S(1)} %copy-done.5, s32[16]{0:T(128)S(1)} %copy-done.4, ...), custom_call_target="tpu_custom_call" | custom-call | tf_op jit(solution)/shard_map/product/pallas_call | solution.py:217
  57.5 1.4 %collective-permute-start.43 = (f32[192,512]{1,0:T(8,128)}, f32[192,512]{1,0:T(8,128)S(1)}, u32[]{:S(2)}, u32[]{:S(2)}) collective-permute-start(f32[192,512]{1,0:T(8,128)} %get-tuple-element.197), channel_id=1, source_target_pairs={{0,1},{1,2},{2,3},{3,0},{4,5},{5,6},{6,7},{7,4},{8,9},{9,10},{10,1... | collective-permute-start | bytes 1179656 | tf_op jit(solution)/shard_map/ppermute | solution.py:201
  58.9 2.6 %collective-permute-start.44 = (f32[192,512]{1,0:T(8,128)}, f32[192,512]{1,0:T(8,128)}, u32[]{:S(2)}, u32[]{:S(2)}) collective-permute-start(f32[192,512]{1,0:T(8,128)} %get-tuple-element.198), channel_id=1, source_target_pairs={{0,2},{1,3},{2,0},{3,1},{4,6},{5,7},{6,4},{7,5},{8,10},{9,11},{10,... | collective-permute-start | bytes 1179656 | tf_op jit(solution)/shard_map/ppermute | solution.py:201
  61.5 1.1 %collective-permute-start.45 = (f32[192,512]{1,0:T(8,128)}, f32[192,512]{1,0:T(8,128)}, u32[]{:S(2)}, u32[]{:S(2)}) collective-permute-start(f32[192,512]{1,0:T(8,128)} %get-tuple-element.199), channel_id=1, source_target_pairs={{0,3},{1,0},{2,1},{3,2},{4,7},{5,4},{6,5},{7,6},{8,11},{9,8},{10,9... | collective-permute-start | bytes 1179656 | tf_op jit(solution)/shard_map/ppermute | solution.py:201
  62.6 0.6 subtract_maximum_fusion
  63.9 0.7 fusion
  64.5 2.0 %multiply_reduce_fusion = s32[4,8]{1,0:T(4,128)} fusion(s32[8,8,8]{2,1,0:T(8,128)S(1)} %fusion, s32[4,8]{1,0:T(4,128)} %subtract_maximum_fusion), kind=kLoop, calls=%fused_computation | loop fusion | flops 4064 | bytes 2304 | tf_op jit(solution)/shard_map/reduce_sum | solution.py:262
  66.5 1.4 %reduce_max.18 = s32[]{:T(128)} reduce(s32[4,8]{1,0:T(4,128)} %multiply_reduce_fusion, s32[]{:T(128)} %constant.89.clone.1), dimensions={0,1}, to_apply=%region_2.0 | reduce | flops 31 | bytes 136 | tf_op jit(solution)/shard_map/reduce_max | solution.py:262
  68.5 1.1 %copy.8 = f32[2,192,1,768]{3,1,0,2:T(8,128)} copy(f32[2,192,1,768]{3,2,1,0:T(1,128)S(1)} %copy-done.1) | data formatting | bytes 2359296 | tf_op jit(solution)/shard_map/while | solution.py:265
  69.7 2.4 %reshape.96 = f32[2304,128]{1,0:T(8,128)} reshape(f32[2,192,1,768]{3,1,0,2:T(8,128)} %copy.8) | data formatting | bytes 2359296 | tf_op jit(solution)/shard_map/while/body/reshape | solution.py:198
  72.0 7.0 %collective-permute-done.44.refs_2_ = f32[192,512]{1,0:T(8,128)} collective-permute-done((f32[192,512]{1,0:T(8,128)}, f32[192,512]{1,0:T(8,128)}, u32[]{:S(2)}, u32[]{:S(2)}) %collective-permute-start.44) | collective-permute-done | bytes 393248 | tf_op jit(solution)/shard_map/ppermute | solution.py:201
  79.1 3.0 %expand.5 = f32[1,192,1536]{2,1,0:T(8,128)} custom-call(s32[8]{0:T(128)S(1)} %stack.48.pos.refs_0_, s32[16]{0:T(128)S(1)} %convert_reduce_fusion.starts.refs_1_, s32[16]{0:T(128)S(1)} %copy-done.4, bf16[512,1536]{1,0:T(8,128)(2,1)S(1)} %get-tuple-element.193.g_ref, s32[8,1536]{1,0:T(8,128)S(1)} %copy-done.3, f32[192,512]{1,0:T(8,128)S(1)} %get-tuple-element.196.refs_0_, ...), custom_call_target="tpu_custom_call" | custom-call | tf_op jit(solution)/shard_map/expand/pallas_call | solution.py:233
  (33 shorter events, 0.1 us)
Async XLA Ops:
  0.0 35.2 %copy-start.6 = (s32[8]{0:T(128)S(1)}, s32[8]{0:T(128)}, u32[]{:S(2)}) copy-start(s32[8]{0:T(128)} %first.1) | copy-start | bytes 100
  0.9 45.1 %copy-start.4 = (s32[16]{0:T(128)S(1)}, s32[16]{0:T(128)}, u32[]{:S(2)}) copy-start(s32[16]{0:T(128)} %target.3) | copy-start | bytes 196
  0.9 45.1 %copy-start.5 = (s32[8]{0:T(128)S(1)}, s32[8]{0:T(128)}, u32[]{:S(2)}) copy-start(s32[8]{0:T(128)} %refs_2_.1) | copy-start | bytes 100
  3.0 0.6 copy-start.2
  3.6 10.0 %collective-permute-start.24 = (f32[2,48,512]{2,1,0:T(8,128)S(1)}, f32[2,48,512]{2,1,0:T(8,128)S(1)}, u32[]{:S(2)}, u32[]{:S(2)}) collective-permute-start(f32[2,48,512]{2,1,0:T(8,128)S(1)} %get-tuple-element.195.refs_4_), channel_id=1, source_target_pairs={{0,56},{4,60},{8,0},{12,4},{16,8},{20,12},{24,16},{28,20},{32,24},... | collective-permute-start | bytes 589832 | tf_op jit(solution)/shard_map/ppermute | solution.py:201
  10.0 7.0 %collective-permute-start.23 = (f32[2,48,512]{2,1,0:T(8,128)S(1)}, f32[2,48,512]{2,1,0:T(8,128)S(1)}, u32[]{:S(2)}, u32[]{:S(2)}) collective-permute-start(f32[2,48,512]{2,1,0:T(8,128)S(1)} %get-tuple-element.195.refs_4_), channel_id=1, source_target_pairs={{0,8},{4,12},{8,16},{12,20},{16,24},{20,28},{24,32},{28,36},{32,40... | collective-permute-start | bytes 589832 | tf_op jit(solution)/shard_map/ppermute | solution.py:201
  13.6 9.1 %collective-permute-start.26 = (f32[2,48,512]{2,1,0:T(8,128)S(1)}, f32[2,48,512]{2,1,0:T(8,128)S(1)}, u32[]{:S(2)}, u32[]{:S(2)}) collective-permute-start(f32[2,48,512]{2,1,0:T(8,128)S(1)} %collective-permute-done.24.refs_6_), channel_id=1, source_target_pairs={{0,56},{4,60},{8,0},{12,4},{16,8},{20,12},{24,16},{28,20},{32,24},... | collective-permute-start | bytes 589832 | tf_op jit(solution)/shard_map/ppermute | solution.py:201
  17.0 8.4 %collective-permute-start.25 = (f32[2,48,512]{2,1,0:T(8,128)S(1)}, f32[2,48,512]{2,1,0:T(8,128)S(1)}, u32[]{:S(2)}, u32[]{:S(2)}) collective-permute-start(f32[2,48,512]{2,1,0:T(8,128)S(1)} %collective-permute-done.23.refs_5_), channel_id=1, source_target_pairs={{0,8},{4,12},{8,16},{12,20},{16,24},{20,28},{24,32},{28,36},{32,40... | collective-permute-start | bytes 589832 | tf_op jit(solution)/shard_map/ppermute | solution.py:201
  17.0 1.3 %copy-start = (f32[2,192,1,768]{3,2,1,0:T(1,128)S(1)}, f32[2,192,1,768]{3,2,1,0:T(1,128)}, u32[]{:S(2)}) copy-start(f32[2,192,1,768]{3,2,1,0:T(1,128)} %param.9) | copy-start | bytes 3538948
  19.6 7.3 %collective-permute-start.42 = (f32[2,192,128]{2,1,0:T(8,128)S(1)}, f32[2,192,128]{2,1,0:T(8,128)S(1)}, u32[]{:S(2)}, u32[]{:S(2)}) collective-permute-start(f32[2,192,128]{2,1,0:T(8,128)S(1)} %pack_w.2.refs_22_), channel_id=1, source_target_pairs={{0,192},{64,0},{128,64},{192,128},{1,193},{65,1},{129,65},{193,129... | collective-permute-start | bytes 589832 | tf_op jit(solution)/shard_map/ppermute | solution.py:201
  22.2 9.3 %collective-permute-start.41 = (f32[2,192,128]{2,1,0:T(8,128)S(1)}, f32[2,192,128]{2,1,0:T(8,128)S(1)}, u32[]{:S(2)}, u32[]{:S(2)}) collective-permute-start(f32[2,192,128]{2,1,0:T(8,128)S(1)} %pack_w.2.refs_22_), channel_id=1, source_target_pairs={{0,128},{64,192},{128,0},{192,64},{1,129},{65,193},{129,1},{193,65... | collective-permute-start | bytes 589832 | tf_op jit(solution)/shard_map/ppermute | solution.py:201
  22.7 10.7 %collective-permute-start.28 = (f32[2,48,512]{2,1,0:T(8,128)S(1)}, f32[2,48,512]{2,1,0:T(8,128)S(1)}, u32[]{:S(2)}, u32[]{:S(2)}) collective-permute-start(f32[2,48,512]{2,1,0:T(8,128)S(1)} %collective-permute-done.26.refs_8_), channel_id=1, source_target_pairs={{0,56},{4,60},{8,0},{12,4},{16,8},{20,12},{24,16},{28,20},{32,24},... | collective-permute-start | bytes 589832 | tf_op jit(solution)/shard_map/ppermute | solution.py:201
  25.4 8.0 %collective-permute-start.27 = (f32[2,48,512]{2,1,0:T(8,128)S(1)}, f32[2,48,512]{2,1,0:T(8,128)S(1)}, u32[]{:S(2)}, u32[]{:S(2)}) collective-permute-start(f32[2,48,512]{2,1,0:T(8,128)S(1)} %collective-permute-done.25.refs_7_), channel_id=1, source_target_pairs={{0,8},{4,12},{8,16},{12,20},{16,24},{20,28},{24,32},{28,36},{32,40... | collective-permute-start | bytes 589832 | tf_op jit(solution)/shard_map/ppermute | solution.py:201
  25.4 10.4 %collective-permute-start.40 = (f32[2,192,128]{2,1,0:T(8,128)S(1)}, f32[2,192,128]{2,1,0:T(8,128)S(1)}, u32[]{:S(2)}, u32[]{:S(2)}) collective-permute-start(f32[2,192,128]{2,1,0:T(8,128)S(1)} %pack_w.2.refs_22_), channel_id=1, source_target_pairs={{0,64},{64,128},{128,192},{192,0},{1,65},{65,129},{129,193},{193,1... | collective-permute-start | bytes 589832 | tf_op jit(solution)/shard_map/ppermute | solution.py:201
  26.9 9.0 %collective-permute-start.31 = (f32[2,48,512]{2,1,0:T(8,128)S(1)}, f32[2,48,512]{2,1,0:T(8,128)S(1)}, u32[]{:S(2)}, u32[]{:S(2)}) collective-permute-start(f32[2,48,512]{2,1,0:T(8,128)S(1)} %get-tuple-element.195.refs_4_), channel_id=1, source_target_pairs={{0,4},{4,0},{8,12},{12,8},{16,20},{20,16},{24,28},{28,24},{32,36},... | collective-permute-start | bytes 589832 | tf_op jit(solution)/shard_map/ppermute | solution.py:204
  31.5 7.2 %collective-permute-start.33 = (f32[2,48,512]{2,1,0:T(8,128)S(1)}, f32[2,48,512]{2,1,0:T(8,128)S(1)}, u32[]{:S(2)}, u32[]{:S(2)}) collective-permute-start(f32[2,48,512]{2,1,0:T(8,128)S(1)} %collective-permute-done.24.refs_6_), channel_id=1, source_target_pairs={{0,4},{4,0},{8,12},{12,8},{16,20},{20,16},{24,28},{28,24},{32,36},... | collective-permute-start | bytes 589832 | tf_op jit(solution)/shard_map/ppermute | solution.py:204
  33.4 5.2 %collective-permute-start.32 = (f32[2,48,512]{2,1,0:T(8,128)S(1)}, f32[2,48,512]{2,1,0:T(8,128)S(1)}, u32[]{:S(2)}, u32[]{:S(2)}) collective-permute-start(f32[2,48,512]{2,1,0:T(8,128)S(1)} %collective-permute-done.23.refs_5_), channel_id=1, source_target_pairs={{0,4},{4,0},{8,12},{12,8},{16,20},{20,16},{24,28},{28,24},{32,36},... | collective-permute-start | bytes 589832 | tf_op jit(solution)/shard_map/ppermute | solution.py:204
  33.4 5.6 %collective-permute-start.35 = (f32[2,48,512]{2,1,0:T(8,128)S(1)}, f32[2,48,512]{2,1,0:T(8,128)S(1)}, u32[]{:S(2)}, u32[]{:S(2)}) collective-permute-start(f32[2,48,512]{2,1,0:T(8,128)S(1)} %collective-permute-done.26.refs_8_), channel_id=1, source_target_pairs={{0,4},{4,0},{8,12},{12,8},{16,20},{20,16},{24,28},{28,24},{32,36},... | collective-permute-start | bytes 589832 | tf_op jit(solution)/shard_map/ppermute | solution.py:204
  35.8 9.3 %collective-permute-start.34 = (f32[2,48,512]{2,1,0:T(8,128)S(1)}, f32[2,48,512]{2,1,0:T(8,128)S(1)}, u32[]{:S(2)}, u32[]{:S(2)}) collective-permute-start(f32[2,48,512]{2,1,0:T(8,128)S(1)} %collective-permute-done.25.refs_7_), channel_id=1, source_target_pairs={{0,4},{4,0},{8,12},{12,8},{16,20},{20,16},{24,28},{28,24},{32,36},... | collective-permute-start | bytes 589832 | tf_op jit(solution)/shard_map/ppermute | solution.py:204
  35.9 4.9 %collective-permute-start.30 = (f32[1,48,512]{2,1,0:T(8,128)S(1)}, f32[1,48,512]{2,1,0:T(8,128)S(1)}, u32[]{:S(2)}, u32[]{:S(2)}) collective-permute-start(f32[1,48,512]{2,1,0:T(8,128)S(1)} %slice.31), channel_id=1, source_target_pairs={{0,56},{4,60},{8,0},{12,4},{16,8},{20,12},{24,16},{28,20},{32,24},... | collective-permute-start | bytes 294920 | tf_op jit(solution)/shard_map/ppermute | solution.py:201
  38.7 5.3 %collective-permute-start.29 = (f32[1,48,512]{2,1,0:T(8,128)S(1)}, f32[1,48,512]{2,1,0:T(8,128)S(1)}, u32[]{:S(2)}, u32[]{:S(2)}) collective-permute-start(f32[1,48,512]{2,1,0:T(8,128)S(1)} %slice.30), channel_id=1, source_target_pairs={{0,8},{4,12},{8,16},{12,20},{16,24},{20,28},{24,32},{28,36},{32,40... | collective-permute-start | bytes 294920 | tf_op jit(solution)/shard_map/ppermute | solution.py:201
  38.7 6.4 %collective-permute-start.37 = (f32[2,48,512]{2,1,0:T(8,128)S(1)}, f32[2,48,512]{2,1,0:T(8,128)S(1)}, u32[]{:S(2)}, u32[]{:S(2)}) collective-permute-start(f32[2,48,512]{2,1,0:T(8,128)S(1)} %collective-permute-done.28.refs_10_), channel_id=1, source_target_pairs={{0,4},{4,0},{8,12},{12,8},{16,20},{20,16},{24,28},{28,24},{32,36},... | collective-permute-start | bytes 589832 | tf_op jit(solution)/shard_map/ppermute | solution.py:204
  39.1 7.0 %collective-permute-start.36 = (f32[2,48,512]{2,1,0:T(8,128)S(1)}, f32[2,48,512]{2,1,0:T(8,128)S(1)}, u32[]{:S(2)}, u32[]{:S(2)}) collective-permute-start(f32[2,48,512]{2,1,0:T(8,128)S(1)} %collective-permute-done.27.refs_9_), channel_id=1, source_target_pairs={{0,4},{4,0},{8,12},{12,8},{16,20},{20,16},{24,28},{28,24},{32,36},... | collective-permute-start | bytes 589832 | tf_op jit(solution)/shard_map/ppermute | solution.py:204
  40.8 4.3 %collective-permute-start.39 = (f32[1,48,512]{2,1,0:T(8,128)S(1)}, f32[1,48,512]{2,1,0:T(8,128)S(1)}, u32[]{:S(2)}, u32[]{:S(2)}) collective-permute-start(f32[1,48,512]{2,1,0:T(8,128)S(1)} %collective-permute-done.30.refs_12_), channel_id=1, source_target_pairs={{0,4},{4,0},{8,12},{12,8},{16,20},{20,16},{24,28},{28,24},{32,36},... | collective-permute-start | bytes 294920 | tf_op jit(solution)/shard_map/ppermute | solution.py:204
  43.9 2.1 %collective-permute-start.38 = (f32[1,48,512]{2,1,0:T(8,128)S(1)}, f32[1,48,512]{2,1,0:T(8,128)S(1)}, u32[]{:S(2)}, u32[]{:S(2)}) collective-permute-start(f32[1,48,512]{2,1,0:T(8,128)S(1)} %collective-permute-done.29.refs_11_), channel_id=1, source_target_pairs={{0,4},{4,0},{8,12},{12,8},{16,20},{20,16},{24,28},{28,24},{32,36},... | collective-permute-start | bytes 294920 | tf_op jit(solution)/shard_map/ppermute | solution.py:204
  45.1 23.4 %copy-start.1 = (f32[2,192,1,768]{3,2,1,0:T(1,128)S(1)}, f32[2,192,1,768]{3,2,1,0:T(1,128)}, u32[]{:S(2)}) copy-start(f32[2,192,1,768]{3,2,1,0:T(1,128)} %param.9) | copy-start | bytes 3538948
  57.5 14.5 %collective-permute-start.43 = (f32[192,512]{1,0:T(8,128)}, f32[192,512]{1,0:T(8,128)S(1)}, u32[]{:S(2)}, u32[]{:S(2)}) collective-permute-start(f32[192,512]{1,0:T(8,128)} %get-tuple-element.197), channel_id=1, source_target_pairs={{0,1},{1,2},{2,3},{3,0},{4,5},{5,6},{6,7},{7,4},{8,9},{9,10},{10,1... | collective-permute-start | bytes 1179656 | tf_op jit(solution)/shard_map/ppermute | solution.py:201
  58.9 20.2 %collective-permute-start.44 = (f32[192,512]{1,0:T(8,128)}, f32[192,512]{1,0:T(8,128)}, u32[]{:S(2)}, u32[]{:S(2)}) collective-permute-start(f32[192,512]{1,0:T(8,128)} %get-tuple-element.198), channel_id=1, source_target_pairs={{0,2},{1,3},{2,0},{3,1},{4,6},{5,7},{6,4},{7,5},{8,10},{9,11},{10,... | collective-permute-start | bytes 1179656 | tf_op jit(solution)/shard_map/ppermute | solution.py:201
  61.5 17.6 %collective-permute-start.45 = (f32[192,512]{1,0:T(8,128)}, f32[192,512]{1,0:T(8,128)}, u32[]{:S(2)}, u32[]{:S(2)}) collective-permute-start(f32[192,512]{1,0:T(8,128)} %get-tuple-element.199), channel_id=1, source_target_pairs={{0,3},{1,0},{2,1},{3,2},{4,7},{5,4},{6,5},{7,6},{8,11},{9,8},{10,9... | collective-permute-start | bytes 1179656 | tf_op jit(solution)/shard_map/ppermute | solution.py:201
  69.7 9.4 %copy-start.3 = (s32[8,1536]{1,0:T(8,128)S(1)}, s32[8,1536]{1,0:T(8,128)}, u32[]{:S(2)}) copy-start(s32[8,1536]{1,0:T(8,128)} %copy-done.2) | copy-start | bytes 147460
  79.0 3.0 %copy-start.7 = (s32[8]{0:T(128)S(1)}, s32[8]{0:T(128)}, u32[]{:S(2)}) copy-start(s32[8]{0:T(128)} %first.1) | copy-start | bytes 100

commit v2 on v1

v2 whole, which is shorter than its diff:
```python
import functools

import jax
import jax.numpy as jnp
from jax import lax
from jax.experimental import pallas as pl
from jax.experimental.pallas import tpu as pltpu
from jax.sharding import PartitionSpec as P


LANES = 512
BLOCK = 128
SMEM = pl.BlockSpec(memory_space=pltpu.SMEM)
VMEM = pl.BlockSpec(memory_space=pltpu.VMEM)
ANY = pl.BlockSpec(memory_space=pl.ANY)
F32, BF16, I32 = jnp.float32, jnp.bfloat16, jnp.int32


def label_of(place, starts):
    label = jnp.zeros_like(place)
    for irrep in range(1, 8):
        label = label + (place >= starts[irrep]).astype(I32)
    return label


def choose(index, scalars):
    out = jnp.full_like(index, scalars[0])
    for n in range(1, len(scalars)):
        out = jnp.where(index == n, scalars[n], out)
    return out


def two_terms(x):
    high = x.astype(BF16)
    return high, (x - high.astype(F32)).astype(BF16)


def nt(a, b):
    return lax.dot_general(a, b, (((1,), (1,)), ((), ())), preferred_element_type=F32)


def tn(a, b):
    return lax.dot_general(a, b, (((0,), (0,)), ((), ())), preferred_element_type=F32)


def x_places(pos, starts, first, x_local, oi):
    a_local = x_local // oi
    base = pos[0] * a_local
    x = lax.broadcasted_iota(I32, (1, x_local), 1)
    i = x % oi
    a = base + x // oi
    label = label_of(a, starts)
    firsts = [first[n] for n in range(oi)]
    s = label ^ choose(i, firsts)
    low = [jnp.maximum(starts[n], base) for n in range(8)]
    count = [jnp.maximum(jnp.minimum(starts[n + 1], base + a_local) - low[n], 0) for n in range(8)]
    place = a - choose(label, low)
    for n in range(oi - 1):
        place = place + jnp.where(n < i, choose(s ^ firsts[n], count), 0)
    return s, place - pos[3] * LANES


def pack_t_kernel(pos, starts, first, second, t_ref, out_ref, g_ref):
    k_local, c_local, x_local = t_ref.shape
    s, place = x_places(pos, starts, first, x_local, first.shape[0])
    c = pos[1] * c_local + lax.broadcasted_iota(I32, (c_local, 1), 0)
    label = label_of(c, starts)
    parts = []
    for k in range(k_local):
        keep = (label ^ second[pos[2] * k_local + k]) == s
        parts.extend(two_terms(jnp.where(keep, t_ref[k], 0.0)))
    stacked = jnp.concatenate(parts, 0)
    for n in range(LANES // 128):
        lanes = slice(n * 128, n * 128 + 128)
        rows = n * 128 + lax.broadcasted_iota(I32, (128, x_local), 0)
        hot = jnp.where(rows == place, 1.0, 0.0).astype(BF16)
        g_ref[lanes, :] = hot
        packed = nt(stacked, hot)
        for k in range(k_local):
            at = 2 * k * c_local
            out_ref[k, :, lanes] = packed[at : at + c_local] + packed[at + c_local : at + 2 * c_local]


def pack_w_kernel(pos, starts, second, target, w_ref, out_ref):
    k_local, c_local, _ = out_ref.shape
    rows = k_local * c_local
    tiles = w_ref.shape[0] // rows
    row = lax.broadcasted_iota(I32, (c_local, 1), 0)
    label = label_of(pos[0] * c_local + row, starts) ^ target[pos[1]]
    wanted = jnp.concatenate([label ^ second[pos[2] * k_local + k] for k in range(k_local)], 0)
    firsts = [starts[n] // 8 * 8 for n in range(8)]
    total = jnp.zeros((2 * rows, BLOCK), F32)
    for q in range(tiles):
        b = q * 128 + lax.broadcasted_iota(I32, (1, 128), 1)
        label_b = label_of(b, starts)
        place = b - choose(label_b, firsts) - pos[4] * BLOCK
        hot = jnp.where(lax.broadcasted_iota(I32, (BLOCK, 128), 0) == place, 1.0, 0.0).astype(BF16)
        w = jnp.where(wanted == label_b, w_ref[pl.ds(q, rows, stride=tiles), :], 0.0)
        total = total + nt(jnp.concatenate(two_terms(w), 0), hot)
    for k in range(k_local):
        out_ref[k] = total[k * c_local : (k + 1) * c_local] + total[rows + k * c_local : rows + (k + 1) * c_local]


def place_piece(pos, kind, shift, size):
    if kind == "t":
        chip = lax.rem(pos[1] // 2 + shift[0] + 8, 8)
        at = (chip * 2 + (pos[1] % 2 if shift[1] == 0 else 1 - pos[1] % 2)) * size
    else:
        at = lax.rem(pos[0] + shift + 4, 4) * size
    return pl.multiple_of(at, 8)


def stacks(w, t):
    w_high, w_low = two_terms(w)
    t_high, t_low = two_terms(t)
    return [w_high, w_high, w_low], [t_high, t_low, t_high]


def early_kernel(plan, *refs):
    pos, starts, second, target = refs[:4]
    pieces = refs[4 : 4 + len(plan)]
    total, w_out, t_all, w_all, sems = refs[4 + len(plan) :]
    k_local, c_all, _ = t_all.shape
    copies = []
    for n, (kind, shift, piece) in enumerate(zip(*zip(*plan), pieces)):
        size = piece.shape[-2]
        into = t_all if kind == "t" else w_all
        at = place_piece(pos, kind, shift, size)
        copies.append(pltpu.make_async_copy(piece, into.at[:, pl.ds(at, size), :], sems.at[n]))
        copies[-1].start()
    missing = c_all // 8
    at = pl.multiple_of(lax.rem(pos[1] // 2 + 4, 8) * missing, 8)
    for k in range(k_local):
        t_all[k, pl.ds(at, missing), :] = jnp.zeros((missing, LANES), F32)
    total[...] = jnp.zeros_like(total)
    for copy in copies:
        copy.wait()
    late = pl.ds(at, missing)
    w_out[...] = w_all[:, late, :]
    row = lax.broadcasted_iota(I32, (128, 1), 0)

    def one_irrep(irrep, _):
        s = target[pos[1]] ^ irrep
        spans = []
        for k in range(k_local):
            p = s ^ second[pos[2] * k_local + k]
            spans.append((starts[p], starts[p + 1], starts[p] // 8 * 8))
        trips = [(end - aligned + 127) // 128 for _, end, aligned in spans]

        def step(n, acc):
            ws, ts = [], []
            for k, (begin, end, aligned) in enumerate(spans):
                nominal = aligned + n * 128
                at = pl.multiple_of(jnp.minimum(nominal, c_all - 128), 8)
                c = at + row
                keep = (c >= jnp.maximum(begin, nominal)) & (c < end)
                w, t = stacks(jnp.where(keep, w_all[k, pl.ds(at, 128), :], 0.0), t_all[k, pl.ds(at, 128), :])
                ws, ts = ws + w, ts + t
            return acc + tn(jnp.concatenate(ws, 0), jnp.concatenate(ts, 0))

        sums = lax.fori_loop(0, jnp.maximum(*trips), step, jnp.zeros((BLOCK, LANES), F32))
        to = starts[irrep] // 8 * 8 + pos[4] * BLOCK

        @pl.when(to < starts[irrep + 1])
        def _():
            total[pl.ds(pl.multiple_of(to, 8), BLOCK), :] += sums

        return 0

    lax.fori_loop(0, 8, one_irrep, 0)


def late_kernel(pos, starts, second, target, total, w, t0, t1, u0, u1, *refs):
    outs, (t_all, sums, sems) = refs[:-3], refs[-3:]
    half = t0.shape[1]
    c_late = 2 * half
    copies = []
    for n, (k, shift, piece) in enumerate(((0, 0, t0), (1, 0, t1), (0, 1, u0), (1, 1, u1))):
        at = pl.multiple_of((pos[1] % 2 if shift == 0 else 1 - pos[1] % 2) * half, 8)
        copies.append(pltpu.make_async_copy(piece, t_all.at[pl.ds(k, 1), pl.ds(at, half), :], sems.at[n]))
        copies[-1].start()
    whole = pltpu.make_async_copy(total, sums, sems.at[4])
    whole.start()
    for copy in copies:
        copy.wait()
    whole.wait()
    base = lax.rem(pos[1] // 2 + 4, 8) * c_late
    c = base + lax.broadcasted_iota(I32, (c_late, 1), 0)
    label = label_of(c, starts)
    first_p = last_p = 0
    for irrep in range(1, 8):
        first_p = first_p + (base >= starts[irrep]).astype(I32)
        last_p = last_p + (base + c_late - 1 >= starts[irrep]).astype(I32)

    def one_p(p, _):
        for k in range(2):
            irrep = p ^ second[pos[2] * 2 + k] ^ target[pos[1]]
            ws, ts = stacks(jnp.where(label == p, w[k], 0.0), t_all[k])
            term = tn(jnp.concatenate(ws, 0), jnp.concatenate(ts, 0))
            to = starts[irrep] // 8 * 8 + pos[4] * BLOCK

            @pl.when(to < starts[irrep + 1])
            def _(term=term, to=to):
                sums[pl.ds(pl.multiple_of(to, 8), BLOCK), :] += term

        return 0

    lax.fori_loop(first_p, last_p + 1, one_p, 0)
    b_local = outs[-1].shape[0]
    copies = []
    for n, (step, skip) in enumerate(((2, 0), (2, b_local // 2), (1, 0), (3, 0), (0, 0))):
        at = pl.multiple_of(lax.rem(pos[2] + step, 4) * b_local + skip, 8)
        copies.append(pltpu.make_async_copy(sums.at[pl.ds(at, outs[n].shape[0]), :], outs[n], sems.at[n]))
        copies[-1].start()
    for copy in copies:
        copy.wait()


def join_kernel(one, three, relay_up, relay_down, out_one, out_three):
    half = relay_up.shape[0]
    out_one[:half] = one[:half] + relay_up[...]
    out_one[half:] = one[half:]
    out_three[:half] = three[:half]
    out_three[half:] = three[half:] + relay_down[...]


def expand_kernel(pos, starts, first, target, g_ref, *refs):
    out_ref = refs[-1]
    b_local = refs[0].shape[0]
    x_local, oi, width = out_ref.shape[2], first.shape[0], 256
    sums = jnp.concatenate(two_terms(refs[0][...] + refs[1][...] + refs[2][...]), 0)
    b = pos[2] * b_local + lax.broadcasted_iota(I32, (b_local, 1), 0)
    wanted = label_of(b, starts) ^ target[pos[1]]

    def tile(n, _):
        x = n * width + lax.broadcasted_iota(I32, (1, width), 1)
        lanes = pl.ds(pl.multiple_of(n * width, width), width)
        a = pos[0] * (x_local // oi) + x // oi
        s = label_of(a, starts) ^ choose(x % oi, [first[i] for i in range(oi)])
        both = jnp.dot(sums, g_ref[:, lanes], preferred_element_type=F32)
        value = jnp.where(wanted == s, both[:b_local] + both[b_local:], 0.0)
        out_ref[0, :, lanes] = value + refs[3][0, :, lanes] if len(refs) > 4 else value
        return 0

    lax.fori_loop(0, x_local // width, tile, 0)


def params():
    return pltpu.CompilerParams(vmem_limit_bytes=48 * 1024 * 1024)


def one_pass(pos, starts, first, second, target, amplitudes, integrals, w_rows, before):
    k_local, c_local, x_local = amplitudes.shape
    v = c_local * 16
    b_local = v // 4
    shape = jax.ShapeDtypeStruct
    t0, hot = pl.pallas_call(
        pack_t_kernel,
        out_shape=(shape((k_local, c_local, LANES), F32), shape((LANES, x_local), BF16)),
        in_specs=[SMEM] * 4 + [VMEM],
        out_specs=(VMEM,) * 2,
        compiler_params=params(),
        name="pack_t",
    )(pos, starts, first, second, amplitudes)
    w0 = pl.pallas_call(
        pack_w_kernel,
        out_shape=shape((k_local, w_rows, BLOCK), F32),
        in_specs=[SMEM] * 4 + [VMEM],
        out_specs=VMEM,
        compiler_params=params(),
        cost_estimate=pl.CostEstimate(flops=10**9, bytes_accessed=4 * 10**6, transcendentals=0),
        name="pack_w",
    )(pos, starts, second, target, integrals)

    def along(x, axis, n, step):
        return lax.ppermute(x, axis, [(i, (i + step) % n) for i in range(n)])

    def swap(x):
        return lax.ppermute(x, "col", [(i, i ^ 1) for i in range(16)])

    got = [((0, 0), t0)]
    right = left = t0
    for n in range(1, 4):
        right = along(right, "col", 16, 2)
        left = along(left, "col", 16, -2)
        got += [((-n, 0), right), ((n, 0), left)]
    got += [((shift[0], 1), swap(piece)) for shift, piece in got]
    plan = [("t", shift) for shift, _ in got] + [("w", -n) for n in range(4)]
    pieces = [piece for _, piece in got] + [w0] + [along(w0, "row", 4, n) for n in range(1, 4)]
    late = [along(right[:1], "col", 16, 2), along(left[1:], "col", 16, -2)]
    total, w_late = pl.pallas_call(
        functools.partial(early_kernel, plan),
        out_shape=(shape((v + BLOCK, LANES), F32), shape((k_local, v // 8, BLOCK), F32)),
        in_specs=[SMEM] * 4 + [ANY] * len(pieces),
        out_specs=(VMEM,) * 2,
        scratch_shapes=[
            pltpu.VMEM((k_local, v, LANES), F32),
            pltpu.VMEM((k_local, v, BLOCK), F32),
            pltpu.SemaphoreType.DMA((len(pieces),)),
        ],
        compiler_params=params(),
        cost_estimate=pl.CostEstimate(flops=4 * 10**9, bytes_accessed=12 * 10**6, transcendentals=0),
        name="early",
    )(pos, starts, second, target, *pieces)
    late += [swap(piece) for piece in late]
    up, down, one, three, own = pl.pallas_call(
        late_kernel,
        out_shape=(shape((b_local // 2, LANES), F32),) * 2 + (shape((b_local, LANES), F32),) * 3,
        in_specs=[SMEM] * 4 + [ANY, VMEM] + [ANY] * 4,
        out_specs=(ANY,) * 5,
        scratch_shapes=[
            pltpu.VMEM((k_local, v // 8, LANES), F32),
            pltpu.VMEM((v + BLOCK, LANES), F32),
            pltpu.SemaphoreType.DMA((5,)),
        ],
        compiler_params=params(),
        name="late",
    )(pos, starts, second, target, total, w_late, *late)
    one, three = pl.pallas_call(
        join_kernel,
        out_shape=(shape((b_local, LANES), F32),) * 2,
        in_specs=[VMEM] * 4,
        out_specs=(VMEM,) * 2,
        compiler_params=params(),
        name="join",
    )(one, three, along(up, "depth", 4, 1), along(down, "depth", 4, -1))
    sums = [own, along(one, "depth", 4, 1), along(three, "depth", 4, -1)]
    more = [] if before is None else [before]
    return pl.pallas_call(
        expand_kernel,
        out_shape=shape((1, b_local, x_local), F32),
        in_specs=[SMEM] * 4 + [VMEM] * (4 + len(more)),
        out_specs=VMEM,
        compiler_params=params(),
        name="expand",
    )(pos, starts, first, target, hot, *sums, *more)


def per_device(amplitudes, integrals, irrep_virtual, irrep_first, irrep_second, irrep_target):
    v = irrep_virtual.shape[0]
    a_local = amplitudes.shape[2] // irrep_first.shape[0]
    starts = jnp.sum((irrep_virtual[None, :] < jnp.arange(16, dtype=I32)[:, None]).astype(I32), axis=1)
    where = [lax.axis_index(n).astype(I32) for n in ("row", "col", "depth")]

    def position(n_lane, n_block):
        return jnp.stack(where + [n_lane, n_block, 0, 0, 0]).astype(I32)

    w_rows = integrals.shape[1]
    flat = integrals.reshape(-1, 128)

    def run(n_lane, n_block, before):
        labels = (starts, irrep_first, irrep_second, irrep_target)
        return one_pass(position(n_lane, n_block), *labels, amplitudes, flat, w_rows, before)

    out = run(jnp.int32(0), jnp.int32(0), None)
    edges = jnp.arange(0, v, a_local, dtype=I32)
    low, high = starts[:8], starts[1:9]
    count = jnp.maximum(jnp.minimum(high, edges[:, None] + a_local) - jnp.maximum(low, edges[:, None]), 0)
    same = (jnp.arange(8)[:, None, None] ^ irrep_first[None, None, :]) == jnp.arange(8)[None, :, None]
    most = jnp.max(jnp.sum(count[:, None, :, None] * same[None].astype(I32), axis=(2, 3)))
    n_lanes = (most + LANES - 1) // LANES
    n_blocks = (jnp.max(high - low // 8 * 8) + BLOCK - 1) // BLOCK
    return lax.fori_loop(1, n_lanes * n_blocks, lambda n, acc: run(n % n_lanes, n // n_lanes, acc), out)


def solution(mesh):
    return jax.shard_map(
        per_device,
        mesh=mesh,
        in_specs=(P("depth", "col", "row"), P("depth", "row", "col", None), P(), P(), P(), P()),
        out_specs=P("col", "depth", "row"),
        check_vma=False,
    )
```

time: 82.4 us -> 72 us (0.87)
  the two profiles are of different devices: /device:TPU:1 before, /device:TPU:32 now
where the time goes in v2:
time: 72 us; the launch traced here: 71.8 us
  starting transfers between devices  25.9 us (36%)
  waiting for transfers between devices  21.7 us (30%)
  Pallas kernels  18.2 us (25%)
  other arithmetic  4.32 us (6%)
  between operations  1.48 us (2%)
    ppermute x15, starting transfers between devices, along(): return lax.ppermute(x, axis, [(i, (i + step) % n) for i in range(n)])  25.2 us
    ppermute x15, waiting for transfers between devices, along(): return lax.ppermute(x, axis, [(i, (i + step) % n) for i in range(n)])  21.7 us
    pallas_call x1, Pallas kernels, one_pass(): pl.pallas_call(functools.partial(early_kernel, plan), out_shape=(shape((v...  7.04 us
    pallas_call x1, Pallas kernels, one_pass(): pl.pallas_call(late_kernel, out_shape=(shape((b_local // 2, LANES), F32),...  3.54 us
    pallas_call x1, Pallas kernels, one_pass(): pl.pallas_call(expand_kernel, out_shape=shape((1, b_local, x_local), F32)...  3.35 us
    pallas_call x1, Pallas kernels, one_pass(): pl.pallas_call(pack_t_kernel, out_shape=(shape((k_local, c_local, LANES),...  2.25 us
    pallas_call x1, Pallas kernels, one_pass(): pl.pallas_call(pack_w_kernel, out_shape=shape((k_local, w_rows, BLOCK), F...  1.97 us
  transfers between devices with their start and end apart: 24, of which 9 were waited for; matrix products, arithmetic and copies ran while one was open for 5% of the time, Pallas kernels for 13%

profile of v2, /device:TPU:32, one launch (start us, length us, event | category | flops | bytes accessed | tf_op | source)
XLA Modules:
  0.0 71.8 jit_solution(14880148180970043577)
XLA Ops:
  0.0 0.8 %convert_reduce_fusion.starts.refs_1_ = s32[16]{0:T(128)S(1)} fusion(s32[768]{0:T(1024)} %param.10), kind=kLoop, calls=%fused_computation.1 | loop fusion | flops 36848 | bytes 3136 | tf_op jit(solution)/shard_map/reduce_sum | solution.py:342
  0.8 0.1 stack.48.pos.refs_0_
  0.9 2.3 %pack_t.5 = (f32[2,48,512]{2,1,0:T(8,128)S(1)}, bf16[512,1536]{1,0:T(8,128)(2,1)S(1)}) custom-call(s32[8]{0:T(128)S(1)} %stack.48.pos.refs_0_, s32[16]{0:T(128)S(1)} %convert_reduce_fusion.starts.refs_1_, s32[8]{0:T(128)} %first.3, s32[8]{0:T(128)} %second.5, f32[2,48,1536]{2,1,0:T(8,128)} %t_ref.1), custom_call_target="tpu_custom_call" | custom-call | tf_op jit(solution)/shard_map/pack_t/pallas_call | solution.py:257
  3.2 2.0 %collective-permute-start.24 = (f32[2,48,512]{2,1,0:T(8,128)S(1)}, f32[2,48,512]{2,1,0:T(8,128)S(1)}, u32[]{:S(2)}, u32[]{:S(2)}) collective-permute-start(f32[2,48,512]{2,1,0:T(8,128)S(1)} %get-tuple-element.201.refs_4_), channel_id=1, source_target_pairs={{0,8},{4,12},{8,16},{12,20},{16,24},{20,28},{24,32},{28,36},{32,40... | collective-permute-start | bytes 589832 | tf_op jit(solution)/shard_map/ppermute | solution.py:276
  5.2 0.1 collective-permute-start.25
  5.3 2.0 %pack_w.2.refs_18_ = f32[2,192,128]{2,1,0:T(8,128)S(1)} custom-call(s32[8]{0:T(128)S(1)} %stack.48.pos.refs_0_, s32[16]{0:T(128)S(1)} %convert_reduce_fusion.starts.refs_1_, s32[8]{0:T(128)} %second.5, s32[16]{0:T(128)} %target.5, f32[2304,128]{1,0:T(8,128)} %bitcast.19), custom_call_target="tpu_custom_call" | custom-call | flops 1000000000 | bytes 4000000 | tf_op jit(solution)/shard_map/pack_w/pallas_call | solution.py:265
  7.3 1.6 %collective-permute-start.37 = (f32[2,192,128]{2,1,0:T(8,128)S(1)}, f32[2,192,128]{2,1,0:T(8,128)S(1)}, u32[]{:S(2)}, u32[]{:S(2)}) collective-permute-start(f32[2,192,128]{2,1,0:T(8,128)S(1)} %pack_w.2.refs_18_), channel_id=1, source_target_pairs={{0,64},{64,128},{128,192},{192,0},{1,65},{65,129},{129,193},{193,1... | collective-permute-start | bytes 589832 | tf_op jit(solution)/shard_map/ppermute | solution.py:276
  8.8 1.1 %collective-permute-done.24.refs_5_ = f32[2,48,512]{2,1,0:T(8,128)S(1)} collective-permute-done((f32[2,48,512]{2,1,0:T(8,128)S(1)}, f32[2,48,512]{2,1,0:T(8,128)S(1)}, u32[]{:S(2)}, u32[]{:S(2)}) %collective-permute-start.24) | collective-permute-done | bytes 196640 | tf_op jit(solution)/shard_map/ppermute | solution.py:276
  9.9 1.9 %collective-permute-start.26 = (f32[2,48,512]{2,1,0:T(8,128)S(1)}, f32[2,48,512]{2,1,0:T(8,128)S(1)}, u32[]{:S(2)}, u32[]{:S(2)}) collective-permute-start(f32[2,48,512]{2,1,0:T(8,128)S(1)} %collective-permute-done.24.refs_5_), channel_id=1, source_target_pairs={{0,8},{4,12},{8,16},{12,20},{16,24},{20,28},{24,32},{28,36},{32,40... | collective-permute-start | bytes 589832 | tf_op jit(solution)/shard_map/ppermute | solution.py:276
  11.8 0.0 collective-permute-done.25.refs_6_
  11.8 2.3 %collective-permute-start.27 = (f32[2,48,512]{2,1,0:T(8,128)S(1)}, f32[2,48,512]{2,1,0:T(8,128)S(1)}, u32[]{:S(2)}, u32[]{:S(2)}) collective-permute-start(f32[2,48,512]{2,1,0:T(8,128)S(1)} %collective-permute-done.25.refs_6_), channel_id=1, source_target_pairs={{0,56},{4,60},{8,0},{12,4},{16,8},{20,12},{24,16},{28,20},{32,24},... | collective-permute-start | bytes 589832 | tf_op jit(solution)/shard_map/ppermute | solution.py:276
  14.1 3.0 %collective-permute-start.38 = (f32[2,192,128]{2,1,0:T(8,128)S(1)}, f32[2,192,128]{2,1,0:T(8,128)S(1)}, u32[]{:S(2)}, u32[]{:S(2)}) collective-permute-start(f32[2,192,128]{2,1,0:T(8,128)S(1)} %pack_w.2.refs_18_), channel_id=1, source_target_pairs={{0,128},{64,192},{128,0},{192,64},{1,129},{65,193},{129,1},{193,65... | collective-permute-start | bytes 589832 | tf_op jit(solution)/shard_map/ppermute | solution.py:276
  17.1 0.0 collective-permute-done.30.refs_11_
  17.1 1.1 %collective-permute-start.39 = (f32[2,192,128]{2,1,0:T(8,128)S(1)}, f32[2,192,128]{2,1,0:T(8,128)S(1)}, u32[]{:S(2)}, u32[]{:S(2)}) collective-permute-start(f32[2,192,128]{2,1,0:T(8,128)S(1)} %pack_w.2.refs_18_), channel_id=1, source_target_pairs={{0,192},{64,0},{128,64},{192,128},{1,193},{65,1},{129,65},{193,129... | collective-permute-start | bytes 589832 | tf_op jit(solution)/shard_map/ppermute | solution.py:276
  18.3 0.1 collective-permute-done.26.refs_7_
  18.4 0.7 collective-permute-start.28
  19.1 0.0 collective-permute-done.27.refs_8_
  19.1 2.6 %collective-permute-start.29 = (f32[2,48,512]{2,1,0:T(8,128)S(1)}, f32[2,48,512]{2,1,0:T(8,128)S(1)}, u32[]{:S(2)}, u32[]{:S(2)}) collective-permute-start(f32[2,48,512]{2,1,0:T(8,128)S(1)} %collective-permute-done.27.refs_8_), channel_id=1, source_target_pairs={{0,56},{4,60},{8,0},{12,4},{16,8},{20,12},{24,16},{28,20},{32,24},... | collective-permute-start | bytes 589832 | tf_op jit(solution)/shard_map/ppermute | solution.py:276
  21.7 0.0 collective-permute-done.38.refs_20_
  21.7 0.1 collective-permute-start.32
  21.8 3.9 %collective-permute-done.39.refs_21_ = f32[2,192,128]{2,1,0:T(8,128)S(1)} collective-permute-done((f32[2,192,128]{2,1,0:T(8,128)S(1)}, f32[2,192,128]{2,1,0:T(8,128)S(1)}, u32[]{:S(2)}, u32[]{:S(2)}) %collective-permute-start.39) | collective-permute-done | bytes 196640 | tf_op jit(solution)/shard_map/ppermute | solution.py:276
  25.7 0.5 collective-permute-start.34
  26.2 0.9 %collective-permute-done.28.refs_9_ = f32[2,48,512]{2,1,0:T(8,128)S(1)} collective-permute-done((f32[2,48,512]{2,1,0:T(8,128)S(1)}, f32[2,48,512]{2,1,0:T(8,128)S(1)}, u32[]{:S(2)}, u32[]{:S(2)}) %collective-permute-start.28) | collective-permute-done | bytes 196640 | tf_op jit(solution)/shard_map/ppermute | solution.py:276
  27.1 0.0 collective-permute-start.35
  27.1 0.4 collective-permute-done.29.refs_10_
  27.5 0.1 collective-permute-start.36
  27.6 0.0 collective-permute-done.32.refs_13_
  27.7 3.2 %collective-permute-start.40 = (f32[1,48,512]{2,1,0:T(8,128)S(1)}, f32[1,48,512]{2,1,0:T(8,128)S(1)}, u32[]{:S(2)}, u32[]{:S(2)}) collective-permute-start(f32[1,48,512]{2,1,0:T(8,128)S(1)} %slice.30), channel_id=1, source_target_pairs={{0,8},{4,12},{8,16},{12,20},{16,24},{20,28},{24,32},{28,36},{32,40... | collective-permute-start | bytes 294920 | tf_op jit(solution)/shard_map/ppermute | solution.py:276
  30.9 0.0 collective-permute-done.33.refs_14_
  30.9 0.0 collective-permute-start.41
  30.9 2.7 %collective-permute-done.40.t0 = f32[1,48,512]{2,1,0:T(8,128)S(1)} collective-permute-done((f32[1,48,512]{2,1,0:T(8,128)S(1)}, f32[1,48,512]{2,1,0:T(8,128)S(1)}, u32[]{:S(2)}, u32[]{:S(2)}) %collective-permute-start.40) | collective-permute-done | bytes 98336 | tf_op jit(solution)/shard_map/ppermute | solution.py:276
  33.7 0.0 collective-permute-start.42
  33.7 3.4 %collective-permute-done.41.t1 = f32[1,48,512]{2,1,0:T(8,128)S(1)} collective-permute-done((f32[1,48,512]{2,1,0:T(8,128)S(1)}, f32[1,48,512]{2,1,0:T(8,128)S(1)}, u32[]{:S(2)}, u32[]{:S(2)}) %collective-permute-start.41) | collective-permute-done | bytes 98336 | tf_op jit(solution)/shard_map/ppermute | solution.py:276
  37.1 7.0 %early.5 = (f32[896,512]{1,0:T(8,128)S(1)}, f32[2,96,128]{2,1,0:T(8,128)S(1)}) custom-call(s32[8]{0:T(128)S(1)} %stack.48.pos.refs_0_, s32[16]{0:T(128)S(1)} %convert_reduce_fusion.starts.refs_1_, s32[8]{0:T(128)S(1)} %copy-done.2, s32[16]{0:T(128)S(1)} %copy-done.1, f32[2,48,512]{2,1,0:T(8,128)S(1)} %get-tuple-element.201.refs_4_, ...), custom_call_target="tpu_custom_call" | custom-call | flops 4000000000 | bytes 12000000 | tf_op jit(solution)/shard_map/early/pallas_call | solution.py:291
  44.1 3.5 %late.5 = (f32[96,512]{1,0:T(8,128)S(1)}, f32[96,512]{1,0:T(8,128)S(1)}, f32[192,512]{1,0:T(8,128)S(1)}, f32[192,512]{1,0:T(8,128)S(1)}, f32[192,512]{1,0:T(8,128)S(1)}) custom-call(s32[8]{0:T(128)S(1)} %stack.48.pos.refs_0_, s32[16]{0:T(128)S(1)} %convert_reduce_fusion.starts.refs_1_, s32[8]{0:T(128)S(1)} %copy-done.2, s32[16]{0:T(128)S(1)} %copy-done.1, ...), custom_call_target="tpu_custom_call" | custom-call | tf_op jit(solution)/shard_map/late/pallas_call | solution.py:306
  47.7 1.7 %collective-permute-start.44 = (f32[96,512]{1,0:T(8,128)S(1)}, f32[96,512]{1,0:T(8,128)S(1)}, u32[]{:S(2)}, u32[]{:S(2)}) collective-permute-start(f32[96,512]{1,0:T(8,128)S(1)} %get-tuple-element.207), channel_id=1, source_target_pairs={{0,1},{1,2},{2,3},{3,0},{4,5},{5,6},{6,7},{7,4},{8,9},{9,10},{10,1... | collective-permute-start | bytes 589832 | tf_op jit(solution)/shard_map/ppermute | solution.py:276
  49.3 1.7 %collective-permute-start.45 = (f32[96,512]{1,0:T(8,128)S(1)}, f32[96,512]{1,0:T(8,128)S(1)}, u32[]{:S(2)}, u32[]{:S(2)}) collective-permute-start(f32[96,512]{1,0:T(8,128)S(1)} %get-tuple-element.208), channel_id=1, source_target_pairs={{0,3},{1,0},{2,1},{3,2},{4,7},{5,4},{6,5},{7,6},{8,11},{9,8},{10,9... | collective-permute-start | bytes 589832 | tf_op jit(solution)/shard_map/ppermute | solution.py:276
  51.0 0.7 %subtract_reduce_fusion = (s32[]{:T(128)}, s32[8]{0:T(128)S(1)}, s32[8]{0:T(128)S(1)}) fusion(s32[16]{0:T(128)S(1)} %convert_reduce_fusion.starts.refs_1_), kind=kLoop, calls=%fused_computation.11 | loop fusion | flops 143 | bytes 132 | tf_op jit(solution)/shard_map/reduce_max | solution.py:362
  51.7 4.6 %collective-permute-done.44.relay_up = f32[96,512]{1,0:T(8,128)S(1)} collective-permute-done((f32[96,512]{1,0:T(8,128)S(1)}, f32[96,512]{1,0:T(8,128)S(1)}, u32[]{:S(2)}, u32[]{:S(2)}) %collective-permute-start.44) | collective-permute-done | bytes 196640 | tf_op jit(solution)/shard_map/ppermute | solution.py:276
  56.4 0.0 collective-permute-done.45.relay_down
  56.4 0.1 join.5
  56.4 1.7 %collective-permute-start.46 = (f32[192,512]{1,0:T(8,128)S(1)}, f32[192,512]{1,0:T(8,128)S(1)}, u32[]{:S(2)}, u32[]{:S(2)}) collective-permute-start(f32[192,512]{1,0:T(8,128)S(1)} %get-tuple-element.209), channel_id=1, source_target_pairs={{0,1},{1,2},{2,3},{3,0},{4,5},{5,6},{6,7},{7,4},{8,9},{9,10},{10,1... | collective-permute-start | bytes 1179656 | tf_op jit(solution)/shard_map/ppermute | solution.py:276
  58.1 1.7 %collective-permute-start.47 = (f32[192,512]{1,0:T(8,128)S(1)}, f32[192,512]{1,0:T(8,128)S(1)}, u32[]{:S(2)}, u32[]{:S(2)}) collective-permute-start(f32[192,512]{1,0:T(8,128)S(1)} %get-tuple-element.210), channel_id=1, source_target_pairs={{0,3},{1,0},{2,1},{3,2},{4,7},{5,4},{6,5},{7,6},{8,11},{9,8},{10,9... | collective-permute-start | bytes 1179656 | tf_op jit(solution)/shard_map/ppermute | solution.py:276
  59.8 0.1 subtract_maximum_fusion
  59.8 1.3 %multiply_reduce_fusion = s32[4,8]{1,0:T(4,128)} fusion(s32[8,8,8]{2,1,0:T(8,128)S(1)} %fusion, s32[4,8]{1,0:T(4,128)S(1)} %subtract_maximum_fusion), kind=kLoop, calls=%fused_computation | loop fusion | flops 4064 | bytes 2304 | tf_op jit(solution)/shard_map/reduce_sum | solution.py:360
  61.2 1.4 %reduce_max.18 = s32[]{:T(128)} reduce(s32[4,8]{1,0:T(4,128)} %multiply_reduce_fusion, s32[]{:T(128)} %constant.89.clone.1), dimensions={0,1}, to_apply=%region_2.0 | reduce | flops 31 | bytes 136 | tf_op jit(solution)/shard_map/reduce_max | solution.py:360
  63.9 4.6 %collective-permute-done.46.refs_1_ = f32[192,512]{1,0:T(8,128)S(1)} collective-permute-done((f32[192,512]{1,0:T(8,128)S(1)}, f32[192,512]{1,0:T(8,128)S(1)}, u32[]{:S(2)}, u32[]{:S(2)}) %collective-permute-start.46) | collective-permute-done | bytes 393248 | tf_op jit(solution)/shard_map/ppermute | solution.py:276
  68.5 3.4 %expand.5 = f32[1,192,1536]{2,1,0:T(8,128)} custom-call(s32[8]{0:T(128)S(1)} %stack.48.pos.refs_0_, s32[16]{0:T(128)S(1)} %convert_reduce_fusion.starts.refs_1_, s32[8]{0:T(128)S(1)} %copy-done, s32[16]{0:T(128)S(1)} %copy-done.1, bf16[512,1536]{1,0:T(8,128)(2,1)S(1)} %get-tuple-element.200.g_ref, f32[192,512]{1,0:T(8,128)S(1)} %get-tuple-element.204.refs_0_, ...), custom_call_target="tpu_custom_call" | custom-call | tf_op jit(solution)/shard_map/expand/pallas_call | solution.py:329
  (27 shorter events, 0.1 us)
Async XLA Ops:
  3.2 6.7 %collective-permute-start.24 = (f32[2,48,512]{2,1,0:T(8,128)S(1)}, f32[2,48,512]{2,1,0:T(8,128)S(1)}, u32[]{:S(2)}, u32[]{:S(2)}) collective-permute-start(f32[2,48,512]{2,1,0:T(8,128)S(1)} %get-tuple-element.201.refs_4_), channel_id=1, source_target_pairs={{0,8},{4,12},{8,16},{12,20},{16,24},{20,28},{24,32},{28,36},{32,40... | collective-permute-start | bytes 589832 | tf_op jit(solution)/shard_map/ppermute | solution.py:276
  5.2 6.6 %collective-permute-start.25 = (f32[2,48,512]{2,1,0:T(8,128)S(1)}, f32[2,48,512]{2,1,0:T(8,128)S(1)}, u32[]{:S(2)}, u32[]{:S(2)}) collective-permute-start(f32[2,48,512]{2,1,0:T(8,128)S(1)} %get-tuple-element.201.refs_4_), channel_id=1, source_target_pairs={{0,56},{4,60},{8,0},{12,4},{16,8},{20,12},{24,16},{28,20},{32,24},... | collective-permute-start | bytes 589832 | tf_op jit(solution)/shard_map/ppermute | solution.py:276
  5.3 11.9 %collective-permute-start.30 = (f32[2,48,512]{2,1,0:T(8,128)S(1)}, f32[2,48,512]{2,1,0:T(8,128)S(1)}, u32[]{:S(2)}, u32[]{:S(2)}) collective-permute-start(f32[2,48,512]{2,1,0:T(8,128)S(1)} %get-tuple-element.201.refs_4_), channel_id=1, source_target_pairs={{0,4},{4,0},{8,12},{12,8},{16,20},{20,16},{24,28},{28,24},{32,36},... | collective-permute-start | bytes 589832 | tf_op jit(solution)/shard_map/ppermute | solution.py:279
  5.3 22.3 %copy-start = (s32[8]{0:T(128)S(1)}, s32[8]{0:T(128)}, u32[]{:S(2)}) copy-start(s32[8]{0:T(128)} %first.3) | copy-start | bytes 100
  5.3 31.8 %copy-start.1 = (s32[16]{0:T(128)S(1)}, s32[16]{0:T(128)}, u32[]{:S(2)}) copy-start(s32[16]{0:T(128)} %target.5) | copy-start | bytes 196
  5.3 31.8 %copy-start.2 = (s32[8]{0:T(128)S(1)}, s32[8]{0:T(128)}, u32[]{:S(2)}) copy-start(s32[8]{0:T(128)} %second.5) | copy-start | bytes 100
  7.3 11.0 %collective-permute-start.37 = (f32[2,192,128]{2,1,0:T(8,128)S(1)}, f32[2,192,128]{2,1,0:T(8,128)S(1)}, u32[]{:S(2)}, u32[]{:S(2)}) collective-permute-start(f32[2,192,128]{2,1,0:T(8,128)S(1)} %pack_w.2.refs_18_), channel_id=1, source_target_pairs={{0,64},{64,128},{128,192},{192,0},{1,65},{65,129},{129,193},{193,1... | collective-permute-start | bytes 589832 | tf_op jit(solution)/shard_map/ppermute | solution.py:276
  9.9 8.5 %collective-permute-start.26 = (f32[2,48,512]{2,1,0:T(8,128)S(1)}, f32[2,48,512]{2,1,0:T(8,128)S(1)}, u32[]{:S(2)}, u32[]{:S(2)}) collective-permute-start(f32[2,48,512]{2,1,0:T(8,128)S(1)} %collective-permute-done.24.refs_5_), channel_id=1, source_target_pairs={{0,8},{4,12},{8,16},{12,20},{16,24},{20,28},{24,32},{28,36},{32,40... | collective-permute-start | bytes 589832 | tf_op jit(solution)/shard_map/ppermute | solution.py:276
  11.8 7.3 %collective-permute-start.27 = (f32[2,48,512]{2,1,0:T(8,128)S(1)}, f32[2,48,512]{2,1,0:T(8,128)S(1)}, u32[]{:S(2)}, u32[]{:S(2)}) collective-permute-start(f32[2,48,512]{2,1,0:T(8,128)S(1)} %collective-permute-done.25.refs_6_), channel_id=1, source_target_pairs={{0,56},{4,60},{8,0},{12,4},{16,8},{20,12},{24,16},{28,20},{32,24},... | collective-permute-start | bytes 589832 | tf_op jit(solution)/shard_map/ppermute | solution.py:276
  14.1 7.6 %collective-permute-start.38 = (f32[2,192,128]{2,1,0:T(8,128)S(1)}, f32[2,192,128]{2,1,0:T(8,128)S(1)}, u32[]{:S(2)}, u32[]{:S(2)}) collective-permute-start(f32[2,192,128]{2,1,0:T(8,128)S(1)} %pack_w.2.refs_18_), channel_id=1, source_target_pairs={{0,128},{64,192},{128,0},{192,64},{1,129},{65,193},{129,1},{193,65... | collective-permute-start | bytes 589832 | tf_op jit(solution)/shard_map/ppermute | solution.py:276
  17.1 8.6 %collective-permute-start.39 = (f32[2,192,128]{2,1,0:T(8,128)S(1)}, f32[2,192,128]{2,1,0:T(8,128)S(1)}, u32[]{:S(2)}, u32[]{:S(2)}) collective-permute-start(f32[2,192,128]{2,1,0:T(8,128)S(1)} %pack_w.2.refs_18_), channel_id=1, source_target_pairs={{0,192},{64,0},{128,64},{192,128},{1,193},{65,1},{129,65},{193,129... | collective-permute-start | bytes 589832 | tf_op jit(solution)/shard_map/ppermute | solution.py:276
  18.3 7.4 %collective-permute-start.31 = (f32[2,48,512]{2,1,0:T(8,128)S(1)}, f32[2,48,512]{2,1,0:T(8,128)S(1)}, u32[]{:S(2)}, u32[]{:S(2)}) collective-permute-start(f32[2,48,512]{2,1,0:T(8,128)S(1)} %collective-permute-done.24.refs_5_), channel_id=1, source_target_pairs={{0,4},{4,0},{8,12},{12,8},{16,20},{20,16},{24,28},{28,24},{32,36},... | collective-permute-start | bytes 589832 | tf_op jit(solution)/shard_map/ppermute | solution.py:279
  18.4 8.7 %collective-permute-start.28 = (f32[2,48,512]{2,1,0:T(8,128)S(1)}, f32[2,48,512]{2,1,0:T(8,128)S(1)}, u32[]{:S(2)}, u32[]{:S(2)}) collective-permute-start(f32[2,48,512]{2,1,0:T(8,128)S(1)} %collective-permute-done.26.refs_7_), channel_id=1, source_target_pairs={{0,8},{4,12},{8,16},{12,20},{16,24},{20,28},{24,32},{28,36},{32,40... | collective-permute-start | bytes 589832 | tf_op jit(solution)/shard_map/ppermute | solution.py:276
  19.1 8.5 %collective-permute-start.29 = (f32[2,48,512]{2,1,0:T(8,128)S(1)}, f32[2,48,512]{2,1,0:T(8,128)S(1)}, u32[]{:S(2)}, u32[]{:S(2)}) collective-permute-start(f32[2,48,512]{2,1,0:T(8,128)S(1)} %collective-permute-done.27.refs_8_), channel_id=1, source_target_pairs={{0,56},{4,60},{8,0},{12,4},{16,8},{20,12},{24,16},{28,20},{32,24},... | collective-permute-start | bytes 589832 | tf_op jit(solution)/shard_map/ppermute | solution.py:276
  21.7 5.9 %collective-permute-start.32 = (f32[2,48,512]{2,1,0:T(8,128)S(1)}, f32[2,48,512]{2,1,0:T(8,128)S(1)}, u32[]{:S(2)}, u32[]{:S(2)}) collective-permute-start(f32[2,48,512]{2,1,0:T(8,128)S(1)} %collective-permute-done.25.refs_6_), channel_id=1, source_target_pairs={{0,4},{4,0},{8,12},{12,8},{16,20},{20,16},{24,28},{28,24},{32,36},... | collective-permute-start | bytes 589832 | tf_op jit(solution)/shard_map/ppermute | solution.py:279
  25.7 5.2 %collective-permute-start.33 = (f32[2,48,512]{2,1,0:T(8,128)S(1)}, f32[2,48,512]{2,1,0:T(8,128)S(1)}, u32[]{:S(2)}, u32[]{:S(2)}) collective-permute-start(f32[2,48,512]{2,1,0:T(8,128)S(1)} %collective-permute-done.26.refs_7_), channel_id=1, source_target_pairs={{0,4},{4,0},{8,12},{12,8},{16,20},{20,16},{24,28},{28,24},{32,36},... | collective-permute-start | bytes 589832 | tf_op jit(solution)/shard_map/ppermute | solution.py:279
  25.7 11.3 %collective-permute-start.34 = (f32[2,48,512]{2,1,0:T(8,128)S(1)}, f32[2,48,512]{2,1,0:T(8,128)S(1)}, u32[]{:S(2)}, u32[]{:S(2)}) collective-permute-start(f32[2,48,512]{2,1,0:T(8,128)S(1)} %collective-permute-done.27.refs_8_), channel_id=1, source_target_pairs={{0,4},{4,0},{8,12},{12,8},{16,20},{20,16},{24,28},{28,24},{32,36},... | collective-permute-start | bytes 589832 | tf_op jit(solution)/shard_map/ppermute | solution.py:279
  27.1 9.9 %collective-permute-start.35 = (f32[2,48,512]{2,1,0:T(8,128)S(1)}, f32[2,48,512]{2,1,0:T(8,128)S(1)}, u32[]{:S(2)}, u32[]{:S(2)}) collective-permute-start(f32[2,48,512]{2,1,0:T(8,128)S(1)} %collective-permute-done.28.refs_9_), channel_id=1, source_target_pairs={{0,4},{4,0},{8,12},{12,8},{16,20},{20,16},{24,28},{28,24},{32,36},... | collective-permute-start | bytes 589832 | tf_op jit(solution)/shard_map/ppermute | solution.py:279
  27.5 9.5 %collective-permute-start.36 = (f32[2,48,512]{2,1,0:T(8,128)S(1)}, f32[2,48,512]{2,1,0:T(8,128)S(1)}, u32[]{:S(2)}, u32[]{:S(2)}) collective-permute-start(f32[2,48,512]{2,1,0:T(8,128)S(1)} %collective-permute-done.29.refs_10_), channel_id=1, source_target_pairs={{0,4},{4,0},{8,12},{12,8},{16,20},{20,16},{24,28},{28,24},{32,36},... | collective-permute-start | bytes 589832 | tf_op jit(solution)/shard_map/ppermute | solution.py:279
  27.7 6.0 %collective-permute-start.40 = (f32[1,48,512]{2,1,0:T(8,128)S(1)}, f32[1,48,512]{2,1,0:T(8,128)S(1)}, u32[]{:S(2)}, u32[]{:S(2)}) collective-permute-start(f32[1,48,512]{2,1,0:T(8,128)S(1)} %slice.30), channel_id=1, source_target_pairs={{0,8},{4,12},{8,16},{12,20},{16,24},{20,28},{24,32},{28,36},{32,40... | collective-permute-start | bytes 294920 | tf_op jit(solution)/shard_map/ppermute | solution.py:276
  30.9 6.1 %collective-permute-start.41 = (f32[1,48,512]{2,1,0:T(8,128)S(1)}, f32[1,48,512]{2,1,0:T(8,128)S(1)}, u32[]{:S(2)}, u32[]{:S(2)}) collective-permute-start(f32[1,48,512]{2,1,0:T(8,128)S(1)} %slice.31), channel_id=1, source_target_pairs={{0,56},{4,60},{8,0},{12,4},{16,8},{20,12},{24,16},{28,20},{32,24},... | collective-permute-start | bytes 294920 | tf_op jit(solution)/shard_map/ppermute | solution.py:276
  33.7 10.5 %collective-permute-start.42 = (f32[1,48,512]{2,1,0:T(8,128)S(1)}, f32[1,48,512]{2,1,0:T(8,128)S(1)}, u32[]{:S(2)}, u32[]{:S(2)}) collective-permute-start(f32[1,48,512]{2,1,0:T(8,128)S(1)} %collective-permute-done.40.t0), channel_id=1, source_target_pairs={{0,4},{4,0},{8,12},{12,8},{16,20},{20,16},{24,28},{28,24},{32,36},... | collective-permute-start | bytes 294920 | tf_op jit(solution)/shard_map/ppermute | solution.py:279
  37.0 7.1 %collective-permute-start.43 = (f32[1,48,512]{2,1,0:T(8,128)S(1)}, f32[1,48,512]{2,1,0:T(8,128)S(1)}, u32[]{:S(2)}, u32[]{:S(2)}) collective-permute-start(f32[1,48,512]{2,1,0:T(8,128)S(1)} %collective-permute-done.41.t1), channel_id=1, source_target_pairs={{0,4},{4,0},{8,12},{12,8},{16,20},{20,16},{24,28},{28,24},{32,36},... | collective-permute-start | bytes 294920 | tf_op jit(solution)/shard_map/ppermute | solution.py:279
  47.7 8.7 %collective-permute-start.44 = (f32[96,512]{1,0:T(8,128)S(1)}, f32[96,512]{1,0:T(8,128)S(1)}, u32[]{:S(2)}, u32[]{:S(2)}) collective-permute-start(f32[96,512]{1,0:T(8,128)S(1)} %get-tuple-element.207), channel_id=1, source_target_pairs={{0,1},{1,2},{2,3},{3,0},{4,5},{5,6},{6,7},{7,4},{8,9},{9,10},{10,1... | collective-permute-start | bytes 589832 | tf_op jit(solution)/shard_map/ppermute | solution.py:276
  49.3 7.0 %collective-permute-start.45 = (f32[96,512]{1,0:T(8,128)S(1)}, f32[96,512]{1,0:T(8,128)S(1)}, u32[]{:S(2)}, u32[]{:S(2)}) collective-permute-start(f32[96,512]{1,0:T(8,128)S(1)} %get-tuple-element.208), channel_id=1, source_target_pairs={{0,3},{1,0},{2,1},{3,2},{4,7},{5,4},{6,5},{7,6},{8,11},{9,8},{10,9... | collective-permute-start | bytes 589832 | tf_op jit(solution)/shard_map/ppermute | solution.py:276
  56.4 12.0 %collective-permute-start.46 = (f32[192,512]{1,0:T(8,128)S(1)}, f32[192,512]{1,0:T(8,128)S(1)}, u32[]{:S(2)}, u32[]{:S(2)}) collective-permute-start(f32[192,512]{1,0:T(8,128)S(1)} %get-tuple-element.209), channel_id=1, source_target_pairs={{0,1},{1,2},{2,3},{3,0},{4,5},{5,6},{6,7},{7,4},{8,9},{9,10},{10,1... | collective-permute-start | bytes 1179656 | tf_op jit(solution)/shard_map/ppermute | solution.py:276
  58.1 10.3 %collective-permute-start.47 = (f32[192,512]{1,0:T(8,128)S(1)}, f32[192,512]{1,0:T(8,128)S(1)}, u32[]{:S(2)}, u32[]{:S(2)}) collective-permute-start(f32[192,512]{1,0:T(8,128)S(1)} %get-tuple-element.210), channel_id=1, source_target_pairs={{0,3},{1,0},{2,1},{3,2},{4,7},{5,4},{6,5},{7,6},{8,11},{9,8},{10,9... | collective-permute-start | bytes 1179656 | tf_op jit(solution)/shard_map/ppermute | solution.py:276
  68.5 3.4 %copy-start.3 = (s32[8]{0:T(128)S(1)}, s32[8]{0:T(128)}, u32[]{:S(2)}) copy-start(s32[8]{0:T(128)} %second.5) | copy-start | bytes 100

commit v3 on v2

--- a/solution.py
+++ b/solution.py
@@ -1,5 +1,3 @@
-import functools
-
 import jax
 import jax.numpy as jnp
 from jax import lax
@@ -101,42 +99,42 @@
         out_ref[k] = total[k * c_local : (k + 1) * c_local] + total[rows + k * c_local : rows + (k + 1) * c_local]
 
 
-def place_piece(pos, kind, shift, size):
-    if kind == "t":
-        chip = lax.rem(pos[1] // 2 + shift[0] + 8, 8)
-        at = (chip * 2 + (pos[1] % 2 if shift[1] == 0 else 1 - pos[1] % 2)) * size
-    else:
-        at = lax.rem(pos[0] + shift + 4, 4) * size
-    return pl.multiple_of(at, 8)
-
-
-def stacks(w, t):
+def three_terms(w, t):
     w_high, w_low = two_terms(w)
     t_high, t_low = two_terms(t)
-    return [w_high, w_high, w_low], [t_high, t_low, t_high]
-
-
-def early_kernel(plan, *refs):
-    pos, starts, second, target = refs[:4]
-    pieces = refs[4 : 4 + len(plan)]
-    total, w_out, t_all, w_all, sems = refs[4 + len(plan) :]
+    both = tn(jnp.concatenate([w_high, w_low], 1), t_high)
+    return both[: w.shape[1]] + both[w.shape[1] :] + tn(w_high, t_low)
+
+
+def early_kernel(pos, starts, second, target, *refs):
+    blocks, ws, (total, w_out, t_all, w_all, sems) = refs[:7], refs[7:11], refs[11:]
     k_local, c_all, _ = t_all.shape
+    chip, core = pos[1] // 2, pos[1] % 2
+    missing = c_all // 8
+    half = missing // 2
     copies = []
-    for n, (kind, shift, piece) in enumerate(zip(*zip(*plan), pieces)):
+
+    def fetch(piece, into, at):
         size = piece.shape[-2]
-        into = t_all if kind == "t" else w_all
-        at = place_piece(pos, kind, shift, size)
-        copies.append(pltpu.make_async_copy(piece, into.at[:, pl.ds(at, size), :], sems.at[n]))
+        there = into.at[:, pl.ds(pl.multiple_of(at, 8), size), :]
+        copies.append(pltpu.make_async_copy(piece, there, sems.at[len(copies)]))
         copies[-1].start()
-    missing = c_all // 8
-    at = pl.multiple_of(lax.rem(pos[1] // 2 + 4, 8) * missing, 8)
+
+    for n, block in enumerate(blocks):
+        far = n if n < 4 else 3 - n
+        base = lax.rem(chip + (2 * core - 1) * far + 8, 8) * missing
+        for window in range(2):
+            of_core = core if (window == 0) == (n < 4) else 1 - core
+            fetch(block.at[window], t_all, base + of_core * half)
+    for n, w in enumerate(ws):
+        fetch(w, w_all, lax.rem(pos[0] - n + 4, 4) * w.shape[1])
+    at = pl.multiple_of(lax.rem(chip + 4, 8) * missing, 8)
     for k in range(k_local):
         t_all[k, pl.ds(at, missing), :] = jnp.zeros((missing, LANES), F32)
     total[...] = jnp.zeros_like(total)
     for copy in copies:
         copy.wait()
-    late = pl.ds(at, missing)
-    w_out[...] = w_all[:, late, :]
+    w_out[...] = w_all[:, pl.ds(at, missing), :]
     row = lax.broadcasted_iota(I32, (128, 1), 0)
 
     def one_irrep(irrep, _):
@@ -148,15 +146,15 @@
         trips = [(end - aligned + 127) // 128 for _, end, aligned in spans]
 
         def step(n, acc):
-            ws, ts = [], []
+            w_rows, t_rows = [], []
             for k, (begin, end, aligned) in enumerate(spans):
                 nominal = aligned + n * 128
                 at = pl.multiple_of(jnp.minimum(nominal, c_all - 128), 8)
                 c = at + row
                 keep = (c >= jnp.maximum(begin, nominal)) & (c < end)
-                w, t = stacks(jnp.where(keep, w_all[k, pl.ds(at, 128), :], 0.0), t_all[k, pl.ds(at, 128), :])
-                ws, ts = ws + w, ts + t
-            return acc + tn(jnp.concatenate(ws, 0), jnp.concatenate(ts, 0))
+                w_rows.append(jnp.where(keep, w_all[k, pl.ds(at, 128), :], 0.0))
+                t_rows.append(t_all[k, pl.ds(at, 128), :])
+            return acc + three_terms(jnp.concatenate(w_rows, 0), jnp.concatenate(t_rows, 0))
 
         sums = lax.fori_loop(0, jnp.maximum(*trips), step, jnp.zeros((BLOCK, LANES), F32))
         to = starts[irrep] // 8 * 8 + pos[4] * BLOCK
@@ -170,23 +168,22 @@
     lax.fori_loop(0, 8, one_irrep, 0)
 
 
-def late_kernel(pos, starts, second, target, total, w, t0, t1, u0, u1, *refs):
-    outs, (t_all, sums, sems) = refs[:-3], refs[-3:]
-    half = t0.shape[1]
+def rows_for(pos, total, step, part):
+    b_local = (total.shape[0] - BLOCK) // 4
+    at = lax.rem(pos[2] + step, 4) * b_local + part * (b_local // 2)
+    return total[pl.ds(pl.multiple_of(at, 8), b_local // 2), :]
+
+
+def late_kernel(pos, starts, second, target, given, w, mine, other, total, up, down, one, three, t_all):
+    half = mine.shape[2]
     c_late = 2 * half
-    copies = []
-    for n, (k, shift, piece) in enumerate(((0, 0, t0), (1, 0, t1), (0, 1, u0), (1, 1, u1))):
-        at = pl.multiple_of((pos[1] % 2 if shift == 0 else 1 - pos[1] % 2) * half, 8)
-        copies.append(pltpu.make_async_copy(piece, t_all.at[pl.ds(k, 1), pl.ds(at, half), :], sems.at[n]))
-        copies[-1].start()
-    whole = pltpu.make_async_copy(total, sums, sems.at[4])
-    whole.start()
-    for copy in copies:
-        copy.wait()
-    whole.wait()
-    base = lax.rem(pos[1] // 2 + 4, 8) * c_late
-    c = base + lax.broadcasted_iota(I32, (c_late, 1), 0)
-    label = label_of(c, starts)
+    chip, core = pos[1] // 2, pos[1] % 2
+    for window in range(2):
+        for piece, k in ((mine, core), (other, 1 - core)):
+            of_core = core if (window == 0) == (piece is mine) else 1 - core
+            t_all[k, pl.ds(pl.multiple_of(of_core * half, 8), half), :] = piece[window, 0]
+    base = lax.rem(chip + 4, 8) * c_late
+    label = label_of(base + lax.broadcasted_iota(I32, (c_late, 1), 0), starts)
     first_p = last_p = 0
     for irrep in range(1, 8):
         first_p = first_p + (base >= starts[irrep]).astype(I32)
@@ -195,40 +192,33 @@
     def one_p(p, _):
         for k in range(2):
             irrep = p ^ second[pos[2] * 2 + k] ^ target[pos[1]]
-            ws, ts = stacks(jnp.where(label == p, w[k], 0.0), t_all[k])
-            term = tn(jnp.concatenate(ws, 0), jnp.concatenate(ts, 0))
+            term = three_terms(jnp.where(label == p, w[k], 0.0), t_all[k])
             to = starts[irrep] // 8 * 8 + pos[4] * BLOCK
 
             @pl.when(to < starts[irrep + 1])
             def _(term=term, to=to):
-                sums[pl.ds(pl.multiple_of(to, 8), BLOCK), :] += term
+                total[pl.ds(pl.multiple_of(to, 8), BLOCK), :] += term
 
         return 0
 
     lax.fori_loop(first_p, last_p + 1, one_p, 0)
-    b_local = outs[-1].shape[0]
-    copies = []
-    for n, (step, skip) in enumerate(((2, 0), (2, b_local // 2), (1, 0), (3, 0), (0, 0))):
-        at = pl.multiple_of(lax.rem(pos[2] + step, 4) * b_local + skip, 8)
-        copies.append(pltpu.make_async_copy(sums.at[pl.ds(at, outs[n].shape[0]), :], outs[n], sems.at[n]))
-        copies[-1].start()
-    for copy in copies:
-        copy.wait()
-
-
-def join_kernel(one, three, relay_up, relay_down, out_one, out_three):
-    half = relay_up.shape[0]
-    out_one[:half] = one[:half] + relay_up[...]
-    out_one[half:] = one[half:]
-    out_three[:half] = three[:half]
-    out_three[half:] = three[half:] + relay_down[...]
+    for out, step, part in ((up, 2, 0), (down, 2, 1), (one, 1, 1), (three, 3, 0)):
+        out[...] = rows_for(pos, total, step, part)
+
+
+def join_kernel(pos, total, relay_up, relay_down, one, three):
+    one[...] = rows_for(pos, total, 1, 0) + relay_up[...]
+    three[...] = rows_for(pos, total, 3, 1) + relay_down[...]
 
 
 def expand_kernel(pos, starts, first, target, g_ref, *refs):
+    total, one_0, one_1, three_0, three_1 = refs[:5]
     out_ref = refs[-1]
-    b_local = refs[0].shape[0]
+    b_local = out_ref.shape[1]
     x_local, oi, width = out_ref.shape[2], first.shape[0], 256
-    sums = jnp.concatenate(two_terms(refs[0][...] + refs[1][...] + refs[2][...]), 0)
+    upper = rows_for(pos, total, 0, 0) + one_0[...] + three_0[...]
+    lower = rows_for(pos, total, 0, 1) + one_1[...] + three_1[...]
+    sums = jnp.concatenate(two_terms(jnp.concatenate([upper, lower], 0)), 0)
     b = pos[2] * b_local + lax.broadcasted_iota(I32, (b_local, 1), 0)
     wanted = label_of(b, starts) ^ target[pos[1]]
 
@@ -239,7 +229,7 @@
         s = label_of(a, starts) ^ choose(x % oi, [first[i] for i in range(oi)])
         both = jnp.dot(sums, g_ref[:, lanes], preferred_element_type=F32)
         value = jnp.where(wanted == s, both[:b_local] + both[b_local:], 0.0)
-        out_ref[0, :, lanes] = value + refs[3][0, :, lanes] if len(refs) > 4 else value
+        out_ref[0, :, lanes] = value + refs[5][0, :, lanes] if len(refs) > 6 else value
         return 0
 
     lax.fori_loop(0, x_local // width, tile, 0)
@@ -272,64 +262,65 @@
         name="pack_w",
     )(pos, starts, second, target, integrals)
 
-    def along(x, axis, n, step):
-        return lax.ppermute(x, axis, [(i, (i + step) % n) for i in range(n)])
+    def along(x, axis, step):
+        return lax.ppermute(x, axis, [(i, (i + step) % 4) for i in range(4)])
 
     def swap(x):
         return lax.ppermute(x, "col", [(i, i ^ 1) for i in range(16)])
 
-    got = [((0, 0), t0)]
-    right = left = t0
-    for n in range(1, 4):
-        right = along(right, "col", 16, 2)
-        left = along(left, "col", 16, -2)
-        got += [((-n, 0), right), ((n, 0), left)]
-    got += [((shift[0], 1), swap(piece)) for shift, piece in got]
-    plan = [("t", shift) for shift, _ in got] + [("w", -n) for n in range(4)]
-    pieces = [piece for _, piece in got] + [w0] + [along(w0, "row", 4, n) for n in range(1, 4)]
-    late = [along(right[:1], "col", 16, 2), along(left[1:], "col", 16, -2)]
+    def ring(x):
+        pairs = [(2 * z + core, 2 * ((z + 1 - 2 * core) % 8) + core) for z in range(8) for core in range(2)]
+        return lax.ppermute(x, "col", pairs)
+
+    got = [jnp.stack([t0, swap(t0)])]
+    for _ in range(1, 4):
+        got.append(ring(got[-1]))
+    core = lax.axis_index("col") % 2
+    mine = ring(lax.dynamic_slice_in_dim(got[3], core, 1, axis=1))
+    got += [swap(got[n]) for n in range(1, 4)]
+    ws = [w0] + [along(w0, "row", n) for n in range(1, 4)]
     total, w_late = pl.pallas_call(
-        functools.partial(early_kernel, plan),
+        early_kernel,
         out_shape=(shape((v + BLOCK, LANES), F32), shape((k_local, v // 8, BLOCK), F32)),
-        in_specs=[SMEM] * 4 + [ANY] * len(pieces),
+        in_specs=[SMEM] * 4 + [ANY] * 11,
         out_specs=(VMEM,) * 2,
         scratch_shapes=[
             pltpu.VMEM((k_local, v, LANES), F32),
             pltpu.VMEM((k_local, v, BLOCK), F32),
-            pltpu.SemaphoreType.DMA((len(pieces),)),
+            pltpu.SemaphoreType.DMA((18,)),
         ],
         compiler_params=params(),
         cost_estimate=pl.CostEstimate(flops=4 * 10**9, bytes_accessed=12 * 10**6, transcendentals=0),
         name="early",
-    )(pos, starts, second, target, *pieces)
-    late += [swap(piece) for piece in late]
-    up, down, one, three, own = pl.pallas_call(
+    )(pos, starts, second, target, *got, *ws)
+    part = shape((b_local // 2, LANES), F32)
+    total, up, down, one_1, three_0 = pl.pallas_call(
         late_kernel,
-        out_shape=(shape((b_local // 2, LANES), F32),) * 2 + (shape((b_local, LANES), F32),) * 3,
-        in_specs=[SMEM] * 4 + [ANY, VMEM] + [ANY] * 4,
-        out_specs=(ANY,) * 5,
-        scratch_shapes=[
-            pltpu.VMEM((k_local, v // 8, LANES), F32),
-            pltpu.VMEM((v + BLOCK, LANES), F32),
-            pltpu.SemaphoreType.DMA((5,)),
-        ],
+        out_shape=(shape(total.shape, F32),) + (part,) * 4,
+        in_specs=[SMEM] * 4 + [VMEM] * 4,
+        out_specs=(VMEM,) * 5,
+        scratch_shapes=[pltpu.VMEM((k_local, v // 8, LANES), F32)],
+        input_output_aliases={4: 0},
         compiler_params=params(),
         name="late",
-    )(pos, starts, second, target, total, w_late, *late)
-    one, three = pl.pallas_call(
+    )(pos, starts, second, target, total, w_late, mine, swap(mine))
+    up, down = along(up, "depth", 1), along(down, "depth", -1)
+    one_1, three_0 = along(one_1, "depth", 1), along(three_0, "depth", -1)
+    one_0, three_1 = pl.pallas_call(
         join_kernel,
-        out_shape=(shape((b_local, LANES), F32),) * 2,
-        in_specs=[VMEM] * 4,
+        out_shape=(part,) * 2,
+        in_specs=[SMEM] + [VMEM] * 3,
         out_specs=(VMEM,) * 2,
         compiler_params=params(),
         name="join",
-    )(one, three, along(up, "depth", 4, 1), along(down, "depth", 4, -1))
-    sums = [own, along(one, "depth", 4, 1), along(three, "depth", 4, -1)]
+    )(pos, total, up, down)
+    one_0, three_1 = along(one_0, "depth", 1), along(three_1, "depth", -1)
+    sums = [total, one_0, one_1, three_0, three_1]
     more = [] if before is None else [before]
     return pl.pallas_call(
         expand_kernel,
         out_shape=shape((1, b_local, x_local), F32),
-        in_specs=[SMEM] * 4 + [VMEM] * (4 + len(more)),
+        in_specs=[SMEM] * 4 + [VMEM] * (6 + len(more)),
         out_specs=VMEM,
         compiler_params=params(),
         name="expand",

time: 72 us -> 86.7 us (1.20)
  the two profiles are of different devices: /device:TPU:32 before, /device:TPU:1 now
where the time goes in v3:
time: 86.7 us; the launch traced here: 85.2 us
  starting transfers between devices  33.9 us (39%)
  waiting for transfers between devices  20 us (23%)
  Pallas kernels  18.5 us (21%)
  local copies, waits for them, and re-layouts  8.21 us (9%)
  other arithmetic  3.11 us (4%)
  between operations  1.44 us (2%)
    ppermute x9, starting transfers between devices, along(): return lax.ppermute(x, axis, [(i, (i + step) % 4) for i in range(4)])  13.8 us
    ppermute x4, waiting for transfers between devices, ring(): return lax.ppermute(x, 'col', pairs)  13.2 us
    ppermute x4, starting transfers between devices, ring(): return lax.ppermute(x, 'col', pairs)  10.2 us
    ppermute x5, starting transfers between devices, swap(): return lax.ppermute(x, 'col', [(i, i ^ 1) for i in range(16)])  9.95 us
    unnamed x32, local copies, waits for them, and re-layouts  8.1 us
    pallas_call x1, Pallas kernels, one_pass(): pl.pallas_call(early_kernel, out_shape=(shape((v + BLOCK, LANES), F32), s...  6.85 us
    ppermute x9, waiting for transfers between devices, along(): return lax.ppermute(x, axis, [(i, (i + step) % 4) for i in range(4)])  5.75 us
    pallas_call x1, Pallas kernels, one_pass(): pl.pallas_call(expand_kernel, out_shape=shape((1, b_local, x_local), F32)...  4 us
  transfers between devices with their start and end apart: 18, of which 8 were waited for; matrix products, arithmetic and copies ran while one was open for 3% of the time, Pallas kernels for 11%

profile of v3, /device:TPU:1, one launch (start us, length us, event | category | flops | bytes accessed | tf_op | source)
XLA Modules:
  0.0 85.2 jit_solution(5098619711716829128)
XLA Ops:
  0.0 0.8 convert_reduce_fusion.starts
  0.8 0.1 stack.72.pos
  0.9 2.4 %pack_t.5 = (f32[2,48,512]{2,1,0:T(8,128)S(1)}, bf16[512,1536]{1,0:T(8,128)(2,1)S(1)}) custom-call(s32[8]{0:T(128)S(1)} %stack.72.pos, s32[16]{0:T(128)S(1)} %convert_reduce_fusion.starts, s32[8]{0:T(128)} %first.3, s32[8]{0:T(128)} %second.7, f32[2,48,1536]{2,1,0:T(8,128)} %t_ref.1), custom_call_target="tpu_custom_call" | custom-call | tf_op jit(solution)/shard_map/pack_t/pallas_call | solution.py:247
  3.3 3.3 %collective-permute-start.18 = (f32[2,48,512]{2,1,0:T(8,128)S(1)}, f32[2,48,512]{2,1,0:T(8,128)S(1)}, u32[]{:S(2)}, u32[]{:S(2)}) collective-permute-start(f32[2,48,512]{2,1,0:T(8,128)S(1)} %get-tuple-element.203), channel_id=1, source_target_pairs={{0,4},{4,0},{8,12},{12,8},{16,20},{20,16},{24,28},{28,24},{32,36},... | collective-permute-start | bytes 589832 | tf_op jit(solution)/shard_map/ppermute | solution.py:269
  6.6 1.1 %collective-permute-done.18 = f32[2,48,512]{2,1,0:T(8,128)S(1)} collective-permute-done((f32[2,48,512]{2,1,0:T(8,128)S(1)}, f32[2,48,512]{2,1,0:T(8,128)S(1)}, u32[]{:S(2)}, u32[]{:S(2)}) %collective-permute-start.18) | collective-permute-done | bytes 196640 | tf_op jit(solution)/shard_map/ppermute | solution.py:269
  7.7 3.9 %collective-permute-start.19 = (f32[2,2,48,512]{3,2,1,0:T(8,128)S(1)}, f32[2,2,48,512]{3,2,1,0:T(8,128)S(1)}, u32[]{:S(2)}, u32[]{:S(2)}) collective-permute-start(f32[2,2,48,512]{3,2,1,0:T(8,128)S(1)} %pad_maximum_fusion.1.refs_0_), channel_id=1, source_target_pairs={{0,8},{4,60},{8,16},{12,4},{16,24},{20,12},{24,32},{28,20},{32,40}... | collective-permute-start | bytes 1179656 | tf_op jit(solution)/shard_map/ppermute | solution.py:273
  11.6 0.7 copy-done.4
  12.4 4.0 %collective-permute-done.19.refs_1_ = f32[2,2,48,512]{3,2,1,0:T(8,128)S(1)} collective-permute-done((f32[2,2,48,512]{3,2,1,0:T(8,128)S(1)}, f32[2,2,48,512]{3,2,1,0:T(8,128)S(1)}, u32[]{:S(2)}, u32[]{:S(2)}) %collective-permute-start.19) | collective-permute-done | bytes 393248 | tf_op jit(solution)/shard_map/ppermute | solution.py:273
  16.3 3.1 %collective-permute-start.20 = (f32[2,2,48,512]{3,2,1,0:T(8,128)S(1)}, f32[2,2,48,512]{3,2,1,0:T(8,128)S(1)}, u32[]{:S(2)}, u32[]{:S(2)}) collective-permute-start(f32[2,2,48,512]{3,2,1,0:T(8,128)S(1)} %collective-permute-done.19.refs_1_), channel_id=1, source_target_pairs={{0,8},{4,60},{8,16},{12,4},{16,24},{20,12},{24,32},{28,20},{32,40}... | collective-permute-start | bytes 1179656 | tf_op jit(solution)/shard_map/ppermute | solution.py:273
  19.5 4.7 %collective-permute-done.20.refs_2_ = f32[2,2,48,512]{3,2,1,0:T(8,128)S(1)} collective-permute-done((f32[2,2,48,512]{3,2,1,0:T(8,128)S(1)}, f32[2,2,48,512]{3,2,1,0:T(8,128)S(1)}, u32[]{:S(2)}, u32[]{:S(2)}) %collective-permute-start.20) | collective-permute-done | bytes 393248 | tf_op jit(solution)/shard_map/ppermute | solution.py:273
  24.2 3.1 %collective-permute-start.21 = (f32[2,2,48,512]{3,2,1,0:T(8,128)S(1)}, f32[2,2,48,512]{3,2,1,0:T(8,128)S(1)}, u32[]{:S(2)}, u32[]{:S(2)}) collective-permute-start(f32[2,2,48,512]{3,2,1,0:T(8,128)S(1)} %collective-permute-done.20.refs_2_), channel_id=1, source_target_pairs={{0,8},{4,60},{8,16},{12,4},{16,24},{20,12},{24,32},{28,20},{32,40}... | collective-permute-start | bytes 1179656 | tf_op jit(solution)/shard_map/ppermute | solution.py:273
  27.3 1.2 %pack_w.2.refs_7_ = f32[2,192,128]{2,1,0:T(8,128)S(1)} custom-call(s32[8]{0:T(128)S(1)} %stack.72.pos, s32[16]{0:T(128)S(1)} %convert_reduce_fusion.starts, s32[8]{0:T(128)S(1)} %copy-done.26, s32[16]{0:T(128)S(1)} %copy-done.25, f32[2304,128]{1,0:T(8,128)S(1)} %bitcast.32), custom_call_target="tpu_custom_call" | custom-call | flops 1000000000 | bytes 4000000 | tf_op jit(solution)/shard_map/pack_w/pallas_call | solution.py:255
  28.5 1.3 %collective-permute-start.25 = (f32[2,192,128]{2,1,0:T(8,128)S(1)}, f32[2,192,128]{2,1,0:T(8,128)}, u32[]{:S(2)}, u32[]{:S(2)}) collective-permute-start(f32[2,192,128]{2,1,0:T(8,128)S(1)} %pack_w.2.refs_7_), channel_id=1, source_target_pairs={{0,64},{64,128},{128,192},{192,0},{1,65},{65,129},{129,193},{193,1... | collective-permute-start | bytes 589832 | tf_op jit(solution)/shard_map/ppermute | solution.py:266
  29.8 2.5 %collective-permute-start.26 = (f32[2,192,128]{2,1,0:T(8,128)S(1)}, f32[2,192,128]{2,1,0:T(8,128)}, u32[]{:S(2)}, u32[]{:S(2)}) collective-permute-start(f32[2,192,128]{2,1,0:T(8,128)S(1)} %pack_w.2.refs_7_), channel_id=1, source_target_pairs={{0,128},{64,192},{128,0},{192,64},{1,129},{65,193},{129,1},{193,65... | collective-permute-start | bytes 589832 | tf_op jit(solution)/shard_map/ppermute | solution.py:266
  32.3 0.4 collective-permute-start.22
  32.7 0.2 collective-permute-start.23
  32.9 3.1 %collective-permute-start.24 = (f32[2,2,48,512]{3,2,1,0:T(8,128)S(1)}, f32[2,2,48,512]{3,2,1,0:T(8,128)}, u32[]{:S(2)}, u32[]{:S(2)}) collective-permute-start(f32[2,2,48,512]{3,2,1,0:T(8,128)S(1)} %collective-permute-done.21.refs_3_), channel_id=1, source_target_pairs={{0,4},{4,0},{8,12},{12,8},{16,20},{20,16},{24,28},{28,24},{32,36},... | collective-permute-start | bytes 1179656 | tf_op jit(solution)/shard_map/ppermute | solution.py:269
  36.0 0.6 collective-permute-done.25.refs_8_
  36.7 1.9 %collective-permute-start.27 = (f32[2,192,128]{2,1,0:T(8,128)S(1)}, f32[2,192,128]{2,1,0:T(8,128)S(1)}, u32[]{:S(2)}, u32[]{:S(2)}) collective-permute-start(f32[2,192,128]{2,1,0:T(8,128)S(1)} %pack_w.2.refs_7_), channel_id=1, source_target_pairs={{0,192},{64,0},{128,64},{192,128},{1,193},{65,1},{129,65},{193,129... | collective-permute-start | bytes 589832 | tf_op jit(solution)/shard_map/ppermute | solution.py:266
  38.6 0.7 copy-done.22
  39.3 2.6 %collective-permute-done.26.refs_9_ = f32[2,192,128]{2,1,0:T(8,128)} collective-permute-done((f32[2,192,128]{2,1,0:T(8,128)S(1)}, f32[2,192,128]{2,1,0:T(8,128)}, u32[]{:S(2)}, u32[]{:S(2)}) %collective-permute-start.26) | collective-permute-done | bytes 196640 | tf_op jit(solution)/shard_map/ppermute | solution.py:266
  41.9 4.5 %collective-permute-done.28.mine = f32[2,1,48,512]{3,2,1,0:T(8,128)S(1)} collective-permute-done((f32[2,1,48,512]{3,2,1,0:T(8,128)S(1)}, f32[2,1,48,512]{3,2,1,0:T(8,128)S(1)}, u32[]{:S(2)}, u32[]{:S(2)}) %collective-permute-start.28) | collective-permute-done | bytes 196640 | tf_op jit(solution)/shard_map/ppermute | solution.py:273
  46.4 3.0 %collective-permute-start.29 = (f32[2,1,48,512]{3,2,1,0:T(8,128)S(1)}, f32[2,1,48,512]{3,2,1,0:T(8,128)S(1)}, u32[]{:S(2)}, u32[]{:S(2)}) collective-permute-start(f32[2,1,48,512]{3,2,1,0:T(8,128)S(1)} %collective-permute-done.28.mine), channel_id=1, source_target_pairs={{0,4},{4,0},{8,12},{12,8},{16,20},{20,16},{24,28},{28,24},{32,36},... | collective-permute-start | bytes 589832 | tf_op jit(solution)/shard_map/ppermute | solution.py:269
  49.4 0.8 copy-done.18
  50.1 0.0 collective-permute-done.23.refs_5_
  50.1 0.0 copy-start.5
  50.1 1.0 %copy-done.5 = f32[2,2,48,512]{3,2,1,0:T(8,128)S(1)} copy-done((f32[2,2,48,512]{3,2,1,0:T(8,128)S(1)}, f32[2,2,48,512]{3,2,1,0:T(8,128)}, u32[]{:S(2)}) %copy-start.5) | copy-done | bytes 393240
  51.1 1.0 %copy-done.7 = f32[2,2,48,512]{3,2,1,0:T(8,128)S(1)} copy-done((f32[2,2,48,512]{3,2,1,0:T(8,128)S(1)}, f32[2,2,48,512]{3,2,1,0:T(8,128)}, u32[]{:S(2)}) %copy-start.7) | copy-done | bytes 393240
  52.1 1.0 %copy-done.11 = f32[2,2,48,512]{3,2,1,0:T(8,128)S(1)} copy-done((f32[2,2,48,512]{3,2,1,0:T(8,128)S(1)}, f32[2,2,48,512]{3,2,1,0:T(8,128)}, u32[]{:S(2)}) %copy-start.11) | copy-done | bytes 393240
  53.1 1.0 %copy-done.15 = f32[2,2,48,512]{3,2,1,0:T(8,128)S(1)} copy-done((f32[2,2,48,512]{3,2,1,0:T(8,128)S(1)}, f32[2,2,48,512]{3,2,1,0:T(8,128)}, u32[]{:S(2)}) %copy-start.15) | copy-done | bytes 393240
  54.1 1.0 %copy-done.19 = f32[2,2,48,512]{3,2,1,0:T(8,128)S(1)} copy-done((f32[2,2,48,512]{3,2,1,0:T(8,128)S(1)}, f32[2,2,48,512]{3,2,1,0:T(8,128)}, u32[]{:S(2)}) %copy-start.19) | copy-done | bytes 393240
  55.1 0.9 %copy-done.23 = f32[2,192,128]{2,1,0:T(8,128)S(1)} copy-done((f32[2,192,128]{2,1,0:T(8,128)S(1)}, f32[2,192,128]{2,1,0:T(8,128)}, u32[]{:S(2)}) %copy-start.23) | copy-done | bytes 196632
  56.0 6.9 %early.5 = (f32[896,512]{1,0:T(8,128)S(1)}, f32[2,96,128]{2,1,0:T(8,128)S(1)}) custom-call(s32[8]{0:T(128)S(1)} %stack.72.pos, s32[16]{0:T(128)S(1)} %convert_reduce_fusion.starts, s32[8]{0:T(128)S(1)} %copy-done.26, s32[16]{0:T(128)S(1)} %copy-done.25, f32[2,2,48,512]{3,2,1,0:T(8,128)S(1)} %copy-done.5, f32[2,2,48,512]{3,2,1,0:T(8,128)S(1)} %copy-done.11, ...), custom_call_target="tpu_custom_call" | custom-call | flops 4000000000 | bytes 12000000 | tf_op jit(solution)/shard_map/early/pallas_call | solution.py:282
  62.9 2.7 %late.5 = (f32[896,512]{1,0:T(8,128)S(1)}, f32[96,512]{1,0:T(8,128)S(1)}, f32[96,512]{1,0:T(8,128)S(1)}, f32[96,512]{1,0:T(8,128)}, f32[96,512]{1,0:T(8,128)}) custom-call(s32[8]{0:T(128)S(1)} %stack.72.pos, s32[16]{0:T(128)S(1)} %convert_reduce_fusion.starts, s32[8]{0:T(128)S(1)} %copy-done.26, s32[16]{0:T(128)S(1)} %copy-done.25, ...), custom_call_target="tpu_custom_call", output_to_operand_aliasing={{0}: (4, {})} | custom-call | tf_op jit(solution)/shard_map/late/pallas_call | solution.py:297
  65.6 1.3 %collective-permute-start.30 = (f32[96,512]{1,0:T(8,128)S(1)}, f32[96,512]{1,0:T(8,128)S(1)}, u32[]{:S(2)}, u32[]{:S(2)}) collective-permute-start(f32[96,512]{1,0:T(8,128)S(1)} %get-tuple-element.207), channel_id=1, source_target_pairs={{0,1},{1,2},{2,3},{3,0},{4,5},{5,6},{6,7},{7,4},{8,9},{9,10},{10,1... | collective-permute-start | bytes 589832 | tf_op jit(solution)/shard_map/ppermute | solution.py:266
  66.9 1.4 %collective-permute-start.31 = (f32[96,512]{1,0:T(8,128)S(1)}, f32[96,512]{1,0:T(8,128)S(1)}, u32[]{:S(2)}, u32[]{:S(2)}) collective-permute-start(f32[96,512]{1,0:T(8,128)S(1)} %get-tuple-element.208), channel_id=1, source_target_pairs={{0,3},{1,0},{2,1},{3,2},{4,7},{5,4},{6,5},{7,6},{8,11},{9,8},{10,9... | collective-permute-start | bytes 589832 | tf_op jit(solution)/shard_map/ppermute | solution.py:266
  68.3 0.7 subtract_reduce_fusion
  69.0 0.0 collective-permute-start.33
  69.0 2.6 %collective-permute-start.34 = (f32[96,512]{1,0:T(8,128)}, f32[96,512]{1,0:T(8,128)}, u32[]{:S(2)}, u32[]{:S(2)}) collective-permute-start(f32[96,512]{1,0:T(8,128)} %get-tuple-element.211), channel_id=1, source_target_pairs={{0,3},{1,0},{2,1},{3,2},{4,7},{5,4},{6,5},{7,6},{8,11},{9,8},{10,9... | collective-permute-start | bytes 589832 | tf_op jit(solution)/shard_map/ppermute | solution.py:266
  71.7 1.7 %collective-permute-done.30.relay_up = f32[96,512]{1,0:T(8,128)S(1)} collective-permute-done((f32[96,512]{1,0:T(8,128)S(1)}, f32[96,512]{1,0:T(8,128)S(1)}, u32[]{:S(2)}, u32[]{:S(2)}) %collective-permute-start.30) | collective-permute-done | bytes 196640 | tf_op jit(solution)/shard_map/ppermute | solution.py:266
  73.4 1.4 %join.5 = (f32[96,512]{1,0:T(8,128)}, f32[96,512]{1,0:T(8,128)}) custom-call(s32[8]{0:T(128)S(1)} %stack.72.pos, f32[896,512]{1,0:T(8,128)S(1)} %get-tuple-element.206.total.refs_0_, f32[96,512]{1,0:T(8,128)S(1)} %collective-permute-done.30.relay_up, f32[96,512]{1,0:T(8,128)S(1)} %collective-permute-done.31.relay_down), custom_call_target="tpu_custom_call" | custom-call | tf_op jit(solution)/shard_map/join/pallas_call | solution.py:309
  74.7 1.1 %collective-permute-start.32 = (f32[96,512]{1,0:T(8,128)}, f32[96,512]{1,0:T(8,128)}, u32[]{:S(2)}, u32[]{:S(2)}) collective-permute-start(f32[96,512]{1,0:T(8,128)} %get-tuple-element.209), channel_id=1, source_target_pairs={{0,1},{1,2},{2,3},{3,0},{4,5},{5,6},{6,7},{7,4},{8,9},{9,10},{10,1... | collective-permute-start | bytes 589832 | tf_op jit(solution)/shard_map/ppermute | solution.py:266
  75.8 1.6 %collective-permute-start.35 = (f32[96,512]{1,0:T(8,128)}, f32[96,512]{1,0:T(8,128)}, u32[]{:S(2)}, u32[]{:S(2)}) collective-permute-start(f32[96,512]{1,0:T(8,128)} %get-tuple-element.212), channel_id=1, source_target_pairs={{0,3},{1,0},{2,1},{3,2},{4,7},{5,4},{6,5},{7,6},{8,11},{9,8},{10,9... | collective-permute-start | bytes 589832 | tf_op jit(solution)/shard_map/ppermute | solution.py:266
  77.4 0.1 subtract_maximum_fusion
  77.5 0.7 multiply_reduce_fusion
  78.2 0.7 reduce_max.18
  80.3 0.9 %collective-permute-done.32.refs_1_ = f32[96,512]{1,0:T(8,128)} collective-permute-done((f32[96,512]{1,0:T(8,128)}, f32[96,512]{1,0:T(8,128)}, u32[]{:S(2)}, u32[]{:S(2)}) %collective-permute-start.32) | collective-permute-done | bytes 196640 | tf_op jit(solution)/shard_map/ppermute | solution.py:266
  81.2 4.0 %expand.5 = f32[1,192,1536]{2,1,0:T(8,128)} custom-call(s32[8]{0:T(128)S(1)} %stack.72.pos, s32[16]{0:T(128)S(1)} %convert_reduce_fusion.starts, s32[8]{0:T(128)S(1)} %copy-done.24, s32[16]{0:T(128)S(1)} %copy-done.25, bf16[512,1536]{1,0:T(8,128)(2,1)S(1)} %get-tuple-element.202.g_ref, f32[896,512]{1,0:T(8,128)S(1)} %get-tuple-element.206.total.refs_0_, ...), custom_call_target="tpu_custom_call" | custom-call | tf_op jit(solution)/shard_map/expand/pallas_call | solution.py:320
  (39 shorter events, 0.1 us)
Async XLA Ops:
  0.0 27.3 %copy-start.26 = (s32[8]{0:T(128)S(1)}, s32[8]{0:T(128)}, u32[]{:S(2)}) copy-start(s32[8]{0:T(128)} %second.7) | copy-start | bytes 100
  0.0 27.3 %copy-start.25 = (s32[16]{0:T(128)S(1)}, s32[16]{0:T(128)}, u32[]{:S(2)}) copy-start(s32[16]{0:T(128)} %target.7) | copy-start | bytes 196
  0.9 26.4 %copy-start.27 = (f32[2,192,1,768]{3,2,1,0:T(1,128)S(1)}, f32[2,192,1,768]{3,2,1,0:T(1,128)}, u32[]{:S(2)}) copy-start(f32[2,192,1,768]{3,2,1,0:T(1,128)} %param.9) | copy-start | bytes 3538948
  3.3 4.4 %collective-permute-start.18 = (f32[2,48,512]{2,1,0:T(8,128)S(1)}, f32[2,48,512]{2,1,0:T(8,128)S(1)}, u32[]{:S(2)}, u32[]{:S(2)}) collective-permute-start(f32[2,48,512]{2,1,0:T(8,128)S(1)} %get-tuple-element.203), channel_id=1, source_target_pairs={{0,4},{4,0},{8,12},{12,8},{16,20},{20,16},{24,28},{28,24},{32,36},... | collective-permute-start | bytes 589832 | tf_op jit(solution)/shard_map/ppermute | solution.py:269
  7.7 8.7 %collective-permute-start.19 = (f32[2,2,48,512]{3,2,1,0:T(8,128)S(1)}, f32[2,2,48,512]{3,2,1,0:T(8,128)S(1)}, u32[]{:S(2)}, u32[]{:S(2)}) collective-permute-start(f32[2,2,48,512]{3,2,1,0:T(8,128)S(1)} %pad_maximum_fusion.1.refs_0_), channel_id=1, source_target_pairs={{0,8},{4,60},{8,16},{12,4},{16,24},{20,12},{24,32},{28,20},{32,40}... | collective-permute-start | bytes 1179656 | tf_op jit(solution)/shard_map/ppermute | solution.py:273
  11.6 0.7 copy-start.4
  16.3 16.0 %copy-start.10 = (f32[2,2,48,512]{3,2,1,0:T(8,128)}, f32[2,2,48,512]{3,2,1,0:T(8,128)S(1)}, u32[]{:S(2)}) copy-start(f32[2,2,48,512]{3,2,1,0:T(8,128)S(1)} %collective-permute-done.19.refs_1_) | copy-start | bytes 1179652
  16.3 7.8 %collective-permute-start.20 = (f32[2,2,48,512]{3,2,1,0:T(8,128)S(1)}, f32[2,2,48,512]{3,2,1,0:T(8,128)S(1)}, u32[]{:S(2)}, u32[]{:S(2)}) collective-permute-start(f32[2,2,48,512]{3,2,1,0:T(8,128)S(1)} %collective-permute-done.19.refs_1_), channel_id=1, source_target_pairs={{0,8},{4,60},{8,16},{12,4},{16,24},{20,12},{24,32},{28,20},{32,40}... | collective-permute-start | bytes 1179656 | tf_op jit(solution)/shard_map/ppermute | solution.py:273
  24.2 8.5 %copy-start.14 = (f32[2,2,48,512]{3,2,1,0:T(8,128)}, f32[2,2,48,512]{3,2,1,0:T(8,128)S(1)}, u32[]{:S(2)}) copy-start(f32[2,2,48,512]{3,2,1,0:T(8,128)S(1)} %collective-permute-done.20.refs_2_) | copy-start | bytes 1179652
  24.2 8.7 %collective-permute-start.21 = (f32[2,2,48,512]{3,2,1,0:T(8,128)S(1)}, f32[2,2,48,512]{3,2,1,0:T(8,128)S(1)}, u32[]{:S(2)}, u32[]{:S(2)}) collective-permute-start(f32[2,2,48,512]{3,2,1,0:T(8,128)S(1)} %collective-permute-done.20.refs_2_), channel_id=1, source_target_pairs={{0,8},{4,60},{8,16},{12,4},{16,24},{20,12},{24,32},{28,20},{32,40}... | collective-permute-start | bytes 1179656 | tf_op jit(solution)/shard_map/ppermute | solution.py:273
  27.3 5.0 %copy-start.24 = (s32[8]{0:T(128)S(1)}, s32[8]{0:T(128)}, u32[]{:S(2)}) copy-start(s32[8]{0:T(128)} %first.3) | copy-start | bytes 100
  28.5 8.1 %collective-permute-start.25 = (f32[2,192,128]{2,1,0:T(8,128)S(1)}, f32[2,192,128]{2,1,0:T(8,128)}, u32[]{:S(2)}, u32[]{:S(2)}) collective-permute-start(f32[2,192,128]{2,1,0:T(8,128)S(1)} %pack_w.2.refs_7_), channel_id=1, source_target_pairs={{0,64},{64,128},{128,192},{192,0},{1,65},{65,129},{129,193},{193,1... | collective-permute-start | bytes 589832 | tf_op jit(solution)/shard_map/ppermute | solution.py:266
  29.8 12.0 %collective-permute-start.26 = (f32[2,192,128]{2,1,0:T(8,128)S(1)}, f32[2,192,128]{2,1,0:T(8,128)}, u32[]{:S(2)}, u32[]{:S(2)}) collective-permute-start(f32[2,192,128]{2,1,0:T(8,128)S(1)} %pack_w.2.refs_7_), channel_id=1, source_target_pairs={{0,128},{64,192},{128,0},{192,64},{1,129},{65,193},{129,1},{193,65... | collective-permute-start | bytes 589832 | tf_op jit(solution)/shard_map/ppermute | solution.py:266
  32.3 17.0 %collective-permute-start.22 = (f32[2,2,48,512]{3,2,1,0:T(8,128)S(1)}, f32[2,2,48,512]{3,2,1,0:T(8,128)S(1)}, u32[]{:S(2)}, u32[]{:S(2)}) collective-permute-start(f32[2,2,48,512]{3,2,1,0:T(8,128)S(1)} %collective-permute-done.19.refs_1_), channel_id=1, source_target_pairs={{0,4},{4,0},{8,12},{12,8},{16,20},{20,16},{24,28},{28,24},{32,36},... | collective-permute-start | bytes 1179656 | tf_op jit(solution)/shard_map/ppermute | solution.py:269
  32.7 17.4 %collective-permute-start.23 = (f32[2,2,48,512]{3,2,1,0:T(8,128)S(1)}, f32[2,2,48,512]{3,2,1,0:T(8,128)}, u32[]{:S(2)}, u32[]{:S(2)}) collective-permute-start(f32[2,2,48,512]{3,2,1,0:T(8,128)S(1)} %collective-permute-done.20.refs_2_), channel_id=1, source_target_pairs={{0,4},{4,0},{8,12},{12,8},{16,20},{20,16},{24,28},{28,24},{32,36},... | collective-permute-start | bytes 1179656 | tf_op jit(solution)/shard_map/ppermute | solution.py:269
  32.9 17.2 %copy-start.6 = (f32[2,2,48,512]{3,2,1,0:T(8,128)}, f32[2,2,48,512]{3,2,1,0:T(8,128)S(1)}, u32[]{:S(2)}) copy-start(f32[2,2,48,512]{3,2,1,0:T(8,128)S(1)} %collective-permute-done.21.refs_3_) | copy-start | bytes 1179652
  32.9 17.2 %collective-permute-start.24 = (f32[2,2,48,512]{3,2,1,0:T(8,128)S(1)}, f32[2,2,48,512]{3,2,1,0:T(8,128)}, u32[]{:S(2)}, u32[]{:S(2)}) collective-permute-start(f32[2,2,48,512]{3,2,1,0:T(8,128)S(1)} %collective-permute-done.21.refs_3_), channel_id=1, source_target_pairs={{0,4},{4,0},{8,12},{12,8},{16,20},{20,16},{24,28},{28,24},{32,36},... | collective-permute-start | bytes 1179656 | tf_op jit(solution)/shard_map/ppermute | solution.py:269
  36.7 12.7 %collective-permute-start.27 = (f32[2,192,128]{2,1,0:T(8,128)S(1)}, f32[2,192,128]{2,1,0:T(8,128)S(1)}, u32[]{:S(2)}, u32[]{:S(2)}) collective-permute-start(f32[2,192,128]{2,1,0:T(8,128)S(1)} %pack_w.2.refs_7_), channel_id=1, source_target_pairs={{0,192},{64,0},{128,64},{192,128},{1,193},{65,1},{129,65},{193,129... | collective-permute-start | bytes 589832 | tf_op jit(solution)/shard_map/ppermute | solution.py:266
  38.6 0.7 copy-start.22
  41.9 4.5 %collective-permute-start.28 = (f32[2,1,48,512]{3,2,1,0:T(8,128)S(1)}, f32[2,1,48,512]{3,2,1,0:T(8,128)S(1)}, u32[]{:S(2)}, u32[]{:S(2)}) collective-permute-start(f32[2,1,48,512]{3,2,1,0:T(8,128)S(1)} %constant_dynamic-slice_fusion.1), channel_id=1, source_target_pairs={{0,8},{4,60},{8,16},{12,4},{16,24},{20,12},{24,32},{28,20},{32,40}... | collective-permute-start | bytes 589832 | tf_op jit(solution)/shard_map/ppermute | solution.py:273
  46.4 16.5 %collective-permute-start.29 = (f32[2,1,48,512]{3,2,1,0:T(8,128)S(1)}, f32[2,1,48,512]{3,2,1,0:T(8,128)S(1)}, u32[]{:S(2)}, u32[]{:S(2)}) collective-permute-start(f32[2,1,48,512]{3,2,1,0:T(8,128)S(1)} %collective-permute-done.28.mine), channel_id=1, source_target_pairs={{0,4},{4,0},{8,12},{12,8},{16,20},{20,16},{24,28},{28,24},{32,36},... | collective-permute-start | bytes 589832 | tf_op jit(solution)/shard_map/ppermute | solution.py:269
  49.3 0.8 copy-start.18
  50.1 1.0 %copy-start.5 = (f32[2,2,48,512]{3,2,1,0:T(8,128)S(1)}, f32[2,2,48,512]{3,2,1,0:T(8,128)}, u32[]{:S(2)}) copy-start(f32[2,2,48,512]{3,2,1,0:T(8,128)} %copy-done.4) | copy-start | bytes 1179652
  51.1 1.0 %copy-start.7 = (f32[2,2,48,512]{3,2,1,0:T(8,128)S(1)}, f32[2,2,48,512]{3,2,1,0:T(8,128)}, u32[]{:S(2)}) copy-start(f32[2,2,48,512]{3,2,1,0:T(8,128)} %copy-done.6) | copy-start | bytes 1179652
  52.1 1.0 %copy-start.11 = (f32[2,2,48,512]{3,2,1,0:T(8,128)S(1)}, f32[2,2,48,512]{3,2,1,0:T(8,128)}, u32[]{:S(2)}) copy-start(f32[2,2,48,512]{3,2,1,0:T(8,128)} %copy-done.10) | copy-start | bytes 1179652
  53.1 1.0 %copy-start.15 = (f32[2,2,48,512]{3,2,1,0:T(8,128)S(1)}, f32[2,2,48,512]{3,2,1,0:T(8,128)}, u32[]{:S(2)}) copy-start(f32[2,2,48,512]{3,2,1,0:T(8,128)} %copy-done.14) | copy-start | bytes 1179652
  54.1 1.0 %copy-start.19 = (f32[2,2,48,512]{3,2,1,0:T(8,128)S(1)}, f32[2,2,48,512]{3,2,1,0:T(8,128)}, u32[]{:S(2)}) copy-start(f32[2,2,48,512]{3,2,1,0:T(8,128)} %copy-done.18) | copy-start | bytes 1179652
  55.1 0.9 %copy-start.23 = (f32[2,192,128]{2,1,0:T(8,128)S(1)}, f32[2,192,128]{2,1,0:T(8,128)}, u32[]{:S(2)}) copy-start(f32[2,192,128]{2,1,0:T(8,128)} %copy-done.22) | copy-start | bytes 589828
  65.6 7.8 %collective-permute-start.30 = (f32[96,512]{1,0:T(8,128)S(1)}, f32[96,512]{1,0:T(8,128)S(1)}, u32[]{:S(2)}, u32[]{:S(2)}) collective-permute-start(f32[96,512]{1,0:T(8,128)S(1)} %get-tuple-element.207), channel_id=1, source_target_pairs={{0,1},{1,2},{2,3},{3,0},{4,5},{5,6},{6,7},{7,4},{8,9},{9,10},{10,1... | collective-permute-start | bytes 589832 | tf_op jit(solution)/shard_map/ppermute | solution.py:266
  66.9 6.5 %collective-permute-start.31 = (f32[96,512]{1,0:T(8,128)S(1)}, f32[96,512]{1,0:T(8,128)S(1)}, u32[]{:S(2)}, u32[]{:S(2)}) collective-permute-start(f32[96,512]{1,0:T(8,128)S(1)} %get-tuple-element.208), channel_id=1, source_target_pairs={{0,3},{1,0},{2,1},{3,2},{4,7},{5,4},{6,5},{7,6},{8,11},{9,8},{10,9... | collective-permute-start | bytes 589832 | tf_op jit(solution)/shard_map/ppermute | solution.py:266
  69.0 11.3 %collective-permute-start.33 = (f32[96,512]{1,0:T(8,128)}, f32[96,512]{1,0:T(8,128)}, u32[]{:S(2)}, u32[]{:S(2)}) collective-permute-start(f32[96,512]{1,0:T(8,128)} %get-tuple-element.210), channel_id=1, source_target_pairs={{0,1},{1,2},{2,3},{3,0},{4,5},{5,6},{6,7},{7,4},{8,9},{9,10},{10,1... | collective-permute-start | bytes 589832 | tf_op jit(solution)/shard_map/ppermute | solution.py:266
  69.0 11.2 %collective-permute-start.34 = (f32[96,512]{1,0:T(8,128)}, f32[96,512]{1,0:T(8,128)}, u32[]{:S(2)}, u32[]{:S(2)}) collective-permute-start(f32[96,512]{1,0:T(8,128)} %get-tuple-element.211), channel_id=1, source_target_pairs={{0,3},{1,0},{2,1},{3,2},{4,7},{5,4},{6,5},{7,6},{8,11},{9,8},{10,9... | collective-permute-start | bytes 589832 | tf_op jit(solution)/shard_map/ppermute | solution.py:266
  74.7 6.4 %collective-permute-start.32 = (f32[96,512]{1,0:T(8,128)}, f32[96,512]{1,0:T(8,128)}, u32[]{:S(2)}, u32[]{:S(2)}) collective-permute-start(f32[96,512]{1,0:T(8,128)} %get-tuple-element.209), channel_id=1, source_target_pairs={{0,1},{1,2},{2,3},{3,0},{4,5},{5,6},{6,7},{7,4},{8,9},{9,10},{10,1... | collective-permute-start | bytes 589832 | tf_op jit(solution)/shard_map/ppermute | solution.py:266
  75.8 5.3 %collective-permute-start.35 = (f32[96,512]{1,0:T(8,128)}, f32[96,512]{1,0:T(8,128)}, u32[]{:S(2)}, u32[]{:S(2)}) collective-permute-start(f32[96,512]{1,0:T(8,128)} %get-tuple-element.212), channel_id=1, source_target_pairs={{0,3},{1,0},{2,1},{3,2},{4,7},{5,4},{6,5},{7,6},{8,11},{9,8},{10,9... | collective-permute-start | bytes 589832 | tf_op jit(solution)/shard_map/ppermute | solution.py:266

commit v4 on v3

--- a/solution.py
+++ b/solution.py
@@ -1,3 +1,5 @@
+import functools
+
 import jax
 import jax.numpy as jnp
 from jax import lax
@@ -106,28 +108,33 @@
     return both[: w.shape[1]] + both[w.shape[1] :] + tn(w_high, t_low)
 
 
-def early_kernel(pos, starts, second, target, *refs):
-    blocks, ws, (total, w_out, t_all, w_all, sems) = refs[:7], refs[7:11], refs[11:]
+def fetch_windows(pos, windows, into, sems):
+    copies = []
+    for n, ((far, other), piece) in enumerate(windows):
+        core = 1 - pos[1] % 2 if other else pos[1] % 2
+        at = (lax.rem(pos[1] // 2 + far + 8, 8) * 2 + core) * piece.shape[1]
+        there = into.at[:, pl.ds(pl.multiple_of(at, 8), piece.shape[1]), :]
+        copies.append(pltpu.make_async_copy(piece, there, sems.at[n]))
+        copies[-1].start()
+    return copies
+
+
+def place_kernel(where, pos, *refs):
+    pieces, (t_all, sems) = refs[: len(where)], refs[len(where) :]
+    for copy in fetch_windows(pos, list(zip(where, pieces)), t_all, sems):
+        copy.wait()
+
+
+def early_kernel(where, pos, starts, second, target, given, *refs):
+    pieces, ws, (t_all, total, w_out, w_all, sems) = refs[: len(where)], refs[len(where) : len(where) + 4], refs[len(where) + 4 :]
     k_local, c_all, _ = t_all.shape
-    chip, core = pos[1] // 2, pos[1] % 2
+    chip = pos[1] // 2
     missing = c_all // 8
-    half = missing // 2
-    copies = []
-
-    def fetch(piece, into, at):
-        size = piece.shape[-2]
-        there = into.at[:, pl.ds(pl.multiple_of(at, 8), size), :]
-        copies.append(pltpu.make_async_copy(piece, there, sems.at[len(copies)]))
+    copies = fetch_windows(pos, list(zip(where, pieces)), t_all, sems)
+    for n, w in enumerate(ws):
+        at = pl.multiple_of(lax.rem(pos[0] - n + 4, 4) * w.shape[1], 8)
+        copies.append(pltpu.make_async_copy(w, w_all.at[:, pl.ds(at, w.shape[1]), :], sems.at[len(where) + n]))
         copies[-1].start()
-
-    for n, block in enumerate(blocks):
-        far = n if n < 4 else 3 - n
-        base = lax.rem(chip + (2 * core - 1) * far + 8, 8) * missing
-        for window in range(2):
-            of_core = core if (window == 0) == (n < 4) else 1 - core
-            fetch(block.at[window], t_all, base + of_core * half)
-    for n, w in enumerate(ws):
-        fetch(w, w_all, lax.rem(pos[0] - n + 4, 4) * w.shape[1])
     at = pl.multiple_of(lax.rem(chip + 4, 8) * missing, 8)
     for k in range(k_local):
         t_all[k, pl.ds(at, missing), :] = jnp.zeros((missing, LANES), F32)
@@ -174,14 +181,12 @@
     return total[pl.ds(pl.multiple_of(at, 8), b_local // 2), :]
 
 
-def late_kernel(pos, starts, second, target, given, w, mine, other, total, up, down, one, three, t_all):
-    half = mine.shape[2]
+def late_kernel(pos, starts, second, target, given, w, t0, t1, u0, u1, total, up, down, one, three, t_all):
+    half = t0.shape[1]
     c_late = 2 * half
     chip, core = pos[1] // 2, pos[1] % 2
-    for window in range(2):
-        for piece, k in ((mine, core), (other, 1 - core)):
-            of_core = core if (window == 0) == (piece is mine) else 1 - core
-            t_all[k, pl.ds(pl.multiple_of(of_core * half, 8), half), :] = piece[window, 0]
+    for k, of_core, piece in ((0, core, t0), (1, core, t1), (0, 1 - core, u0), (1, 1 - core, u1)):
+        t_all[k, pl.ds(pl.multiple_of(of_core * half, 8), half), :] = piece[0]
     base = lax.rem(chip + 4, 8) * c_late
     label = label_of(base + lax.broadcasted_iota(I32, (c_late, 1), 0), starts)
     first_p = last_p = 0
@@ -236,7 +241,7 @@
 
 
 def params():
-    return pltpu.CompilerParams(vmem_limit_bytes=48 * 1024 * 1024)
+    return pltpu.CompilerParams(vmem_limit_bytes=24 * 1024 * 1024)
 
 
 def one_pass(pos, starts, first, second, target, amplitudes, integrals, w_rows, before):
@@ -268,42 +273,57 @@
     def swap(x):
         return lax.ppermute(x, "col", [(i, i ^ 1) for i in range(16)])
 
-    def ring(x):
-        pairs = [(2 * z + core, 2 * ((z + 1 - 2 * core) % 8) + core) for z in range(8) for core in range(2)]
-        return lax.ppermute(x, "col", pairs)
-
-    got = [jnp.stack([t0, swap(t0)])]
-    for _ in range(1, 4):
-        got.append(ring(got[-1]))
-    core = lax.axis_index("col") % 2
-    mine = ring(lax.dynamic_slice_in_dim(got[3], core, 1, axis=1))
-    got += [swap(got[n]) for n in range(1, 4)]
+    def ring(x, step):
+        return lax.ppermute(x, "col", [(i, (i + 2 * step) % 16) for i in range(16)])
+
+    got = {(0, False): t0}
+    right = left = t0
+    for n in range(1, 4):
+        right, left = ring(right, 1), ring(left, -1)
+        got[-n, False], got[n, False] = right, left
+    late = [ring(right[:1], 1), ring(left[1:], -1)]
+    for (far, _), piece in list(got.items()):
+        got[far, True] = swap(piece)
     ws = [w0] + [along(w0, "row", n) for n in range(1, 4)]
-    total, w_late = pl.pallas_call(
-        early_kernel,
-        out_shape=(shape((v + BLOCK, LANES), F32), shape((k_local, v // 8, BLOCK), F32)),
-        in_specs=[SMEM] * 4 + [ANY] * 11,
-        out_specs=(VMEM,) * 2,
-        scratch_shapes=[
-            pltpu.VMEM((k_local, v, LANES), F32),
-            pltpu.VMEM((k_local, v, BLOCK), F32),
-            pltpu.SemaphoreType.DMA((18,)),
-        ],
+    arrived = [place for place in got if abs(place[0]) <= (1 if place[1] else 2)]
+    others = [place for place in got if place not in arrived]
+    t_all = pl.pallas_call(
+        functools.partial(place_kernel, arrived),
+        out_shape=shape((k_local, v, LANES), F32),
+        in_specs=[SMEM] + [ANY] * len(arrived),
+        out_specs=VMEM,
+        scratch_shapes=[pltpu.SemaphoreType.DMA((len(arrived),))],
+        compiler_params=params(),
+        cost_estimate=pl.CostEstimate(flops=0, bytes_accessed=3 * 10**6, transcendentals=0),
+        name="place",
+    )(pos, *[got[place] for place in arrived])
+    _, total, w_late = pl.pallas_call(
+        functools.partial(early_kernel, others),
+        out_shape=(
+            shape(t_all.shape, F32),
+            shape((v + BLOCK, LANES), F32),
+            shape((k_local, v // 8, BLOCK), F32),
+        ),
+        in_specs=[SMEM] * 4 + [VMEM] + [ANY] * (len(others) + 4),
+        out_specs=(VMEM,) * 3,
+        scratch_shapes=[pltpu.VMEM((k_local, v, BLOCK), F32), pltpu.SemaphoreType.DMA((len(others) + 4,))],
+        input_output_aliases={4: 0},
         compiler_params=params(),
         cost_estimate=pl.CostEstimate(flops=4 * 10**9, bytes_accessed=12 * 10**6, transcendentals=0),
         name="early",
-    )(pos, starts, second, target, *got, *ws)
+    )(pos, starts, second, target, t_all, *[got[place] for place in others], *ws)
+    late += [swap(piece) for piece in late]
     part = shape((b_local // 2, LANES), F32)
     total, up, down, one_1, three_0 = pl.pallas_call(
         late_kernel,
         out_shape=(shape(total.shape, F32),) + (part,) * 4,
-        in_specs=[SMEM] * 4 + [VMEM] * 4,
+        in_specs=[SMEM] * 4 + [VMEM] * 6,
         out_specs=(VMEM,) * 5,
         scratch_shapes=[pltpu.VMEM((k_local, v // 8, LANES), F32)],
         input_output_aliases={4: 0},
         compiler_params=params(),
         name="late",
-    )(pos, starts, second, target, total, w_late, mine, swap(mine))
+    )(pos, starts, second, target, total, w_late, *late)
     up, down = along(up, "depth", 1), along(down, "depth", -1)
     one_1, three_0 = along(one_1, "depth", 1), along(three_0, "depth", -1)
     one_0, three_1 = pl.pallas_call(

time: 86.7 us -> 67.9 us (0.78)
  the two profiles are of different devices: /device:TPU:1 before, /device:TPU:32 now
where the time goes in v4:
time: 67.9 us; the launch traced here: 67.7 us
  starting transfers between devices  29.1 us (43%)
  Pallas kernels  19.7 us (29%)
  waiting for transfers between devices  14.2 us (21%)
  other arithmetic  3.1 us (5%)
  between operations  1.57 us (2%)
    ppermute x9, starting transfers between devices, along(): return lax.ppermute(x, axis, [(i, (i + step) % 4) for i in range(4)])  15.4 us
    ppermute x8, starting transfers between devices, ring(): return lax.ppermute(x, 'col', [(i, (i + 2 * step) % 16) for i in range(16)])  12.9 us
    ppermute x9, waiting for transfers between devices, along(): return lax.ppermute(x, axis, [(i, (i + step) % 4) for i in range(4)])  7.27 us
    ppermute x8, waiting for transfers between devices, ring(): return lax.ppermute(x, 'col', [(i, (i + 2 * step) % 16) for i in range(16)])  6.86 us
    pallas_call x1, Pallas kernels, one_pass(): pl.pallas_call(functools.partial(early_kernel, others), out_shape=(shape(...  5.7 us
    pallas_call x1, Pallas kernels, one_pass(): pl.pallas_call(expand_kernel, out_shape=shape((1, b_local, x_local), F32)...  4 us
    pallas_call x1, Pallas kernels, one_pass(): pl.pallas_call(late_kernel, out_shape=(shape(total.shape, F32),) + (part,...  2.66 us
    pallas_call x1, Pallas kernels, one_pass(): pl.pallas_call(pack_t_kernel, out_shape=(shape((k_local, c_local, LANES),...  2.25 us
  transfers between devices with their start and end apart: 26, of which 11 were waited for; matrix products, arithmetic and copies ran while one was open for 3% of the time, Pallas kernels for 16%

profile of v4, /device:TPU:32, one launch (start us, length us, event | category | flops | bytes accessed | tf_op | source)
XLA Modules:
  0.0 67.7 jit_solution(12647403325142871535)
XLA Ops:
  0.0 0.8 %convert_reduce_fusion.starts = s32[16]{0:T(128)S(1)} fusion(s32[768]{0:T(1024)} %param.10), kind=kLoop, calls=%fused_computation.1 | loop fusion | flops 36848 | bytes 3136 | tf_op jit(solution)/shard_map/reduce_sum | solution.py:353
  0.8 0.1 stack.48.pos
  0.9 2.3 %pack_t.5 = (f32[2,48,512]{2,1,0:T(8,128)S(1)}, bf16[512,1536]{1,0:T(8,128)(2,1)S(1)}) custom-call(s32[8]{0:T(128)S(1)} %stack.48.pos, s32[16]{0:T(128)S(1)} %convert_reduce_fusion.starts, s32[8]{0:T(128)} %first.3, s32[8]{0:T(128)} %second.7, f32[2,48,1536]{2,1,0:T(8,128)} %t_ref.1), custom_call_target="tpu_custom_call" | custom-call | tf_op jit(solution)/shard_map/pack_t/pallas_call | solution.py:252
  3.2 2.0 %collective-permute-start.26 = (f32[2,48,512]{2,1,0:T(8,128)S(1)}, f32[2,48,512]{2,1,0:T(8,128)S(1)}, u32[]{:S(2)}, u32[]{:S(2)}) collective-permute-start(f32[2,48,512]{2,1,0:T(8,128)S(1)} %get-tuple-element.201.refs_0_), channel_id=1, source_target_pairs={{0,8},{4,12},{8,16},{12,20},{16,24},{20,28},{24,32},{28,36},{32,40... | collective-permute-start | bytes 589832 | tf_op jit(solution)/shard_map/ppermute | solution.py:277
  5.2 0.1 collective-permute-start.27
  5.3 1.9 %pack_w.2.refs_6_ = f32[2,192,128]{2,1,0:T(8,128)S(1)} custom-call(s32[8]{0:T(128)S(1)} %stack.48.pos, s32[16]{0:T(128)S(1)} %convert_reduce_fusion.starts, s32[8]{0:T(128)} %second.7, s32[16]{0:T(128)} %target.7, f32[2304,128]{1,0:T(8,128)} %bitcast.19), custom_call_target="tpu_custom_call" | custom-call | flops 1000000000 | bytes 4000000 | tf_op jit(solution)/shard_map/pack_w/pallas_call | solution.py:260
  7.2 1.6 %collective-permute-start.39 = (f32[2,192,128]{2,1,0:T(8,128)S(1)}, f32[2,192,128]{2,1,0:T(8,128)S(1)}, u32[]{:S(2)}, u32[]{:S(2)}) collective-permute-start(f32[2,192,128]{2,1,0:T(8,128)S(1)} %pack_w.2.refs_6_), channel_id=1, source_target_pairs={{0,64},{64,128},{128,192},{192,0},{1,65},{65,129},{129,193},{193,1... | collective-permute-start | bytes 589832 | tf_op jit(solution)/shard_map/ppermute | solution.py:271
  8.8 1.1 %collective-permute-done.26.refs_1_ = f32[2,48,512]{2,1,0:T(8,128)S(1)} collective-permute-done((f32[2,48,512]{2,1,0:T(8,128)S(1)}, f32[2,48,512]{2,1,0:T(8,128)S(1)}, u32[]{:S(2)}, u32[]{:S(2)}) %collective-permute-start.26) | collective-permute-done | bytes 196640 | tf_op jit(solution)/shard_map/ppermute | solution.py:277
  9.9 1.9 %collective-permute-start.28 = (f32[2,48,512]{2,1,0:T(8,128)S(1)}, f32[2,48,512]{2,1,0:T(8,128)S(1)}, u32[]{:S(2)}, u32[]{:S(2)}) collective-permute-start(f32[2,48,512]{2,1,0:T(8,128)S(1)} %collective-permute-done.26.refs_1_), channel_id=1, source_target_pairs={{0,8},{4,12},{8,16},{12,20},{16,24},{20,28},{24,32},{28,36},{32,40... | collective-permute-start | bytes 589832 | tf_op jit(solution)/shard_map/ppermute | solution.py:277
  11.8 0.0 collective-permute-done.27.refs_2_
  11.8 2.3 %collective-permute-start.29 = (f32[2,48,512]{2,1,0:T(8,128)S(1)}, f32[2,48,512]{2,1,0:T(8,128)S(1)}, u32[]{:S(2)}, u32[]{:S(2)}) collective-permute-start(f32[2,48,512]{2,1,0:T(8,128)S(1)} %collective-permute-done.27.refs_2_), channel_id=1, source_target_pairs={{0,56},{4,60},{8,0},{12,4},{16,8},{20,12},{24,16},{28,20},{32,24},... | collective-permute-start | bytes 589832 | tf_op jit(solution)/shard_map/ppermute | solution.py:277
  14.1 3.0 %collective-permute-start.40 = (f32[2,192,128]{2,1,0:T(8,128)S(1)}, f32[2,192,128]{2,1,0:T(8,128)S(1)}, u32[]{:S(2)}, u32[]{:S(2)}) collective-permute-start(f32[2,192,128]{2,1,0:T(8,128)S(1)} %pack_w.2.refs_6_), channel_id=1, source_target_pairs={{0,128},{64,192},{128,0},{192,64},{1,129},{65,193},{129,1},{193,65... | collective-permute-start | bytes 589832 | tf_op jit(solution)/shard_map/ppermute | solution.py:271
  17.1 0.0 collective-permute-done.30.refs_5_
  17.1 1.1 %collective-permute-start.41 = (f32[2,192,128]{2,1,0:T(8,128)S(1)}, f32[2,192,128]{2,1,0:T(8,128)S(1)}, u32[]{:S(2)}, u32[]{:S(2)}) collective-permute-start(f32[2,192,128]{2,1,0:T(8,128)S(1)} %pack_w.2.refs_6_), channel_id=1, source_target_pairs={{0,192},{64,0},{128,64},{192,128},{1,193},{65,1},{129,65},{193,129... | collective-permute-start | bytes 589832 | tf_op jit(solution)/shard_map/ppermute | solution.py:271
  18.3 0.1 collective-permute-done.28.refs_3_
  18.4 0.7 collective-permute-start.33
  19.1 0.0 collective-permute-done.29.refs_4_
  19.1 2.6 %collective-permute-start.34 = (f32[2,48,512]{2,1,0:T(8,128)S(1)}, f32[2,48,512]{2,1,0:T(8,128)S(1)}, u32[]{:S(2)}, u32[]{:S(2)}) collective-permute-start(f32[2,48,512]{2,1,0:T(8,128)S(1)} %collective-permute-done.29.refs_4_), channel_id=1, source_target_pairs={{0,56},{4,60},{8,0},{12,4},{16,8},{20,12},{24,16},{28,20},{32,24},... | collective-permute-start | bytes 589832 | tf_op jit(solution)/shard_map/ppermute | solution.py:277
  21.7 0.2 collective-permute-start.32
  21.9 3.8 %collective-permute-done.41.refs_9_ = f32[2,192,128]{2,1,0:T(8,128)S(1)} collective-permute-done((f32[2,192,128]{2,1,0:T(8,128)S(1)}, f32[2,192,128]{2,1,0:T(8,128)S(1)}, u32[]{:S(2)}, u32[]{:S(2)}) %collective-permute-start.41) | collective-permute-done | bytes 196640 | tf_op jit(solution)/shard_map/ppermute | solution.py:271
  25.7 0.5 collective-permute-start.36
  26.2 0.9 %collective-permute-done.33.refs_0_ = f32[2,48,512]{2,1,0:T(8,128)S(1)} collective-permute-done((f32[2,48,512]{2,1,0:T(8,128)S(1)}, f32[2,48,512]{2,1,0:T(8,128)S(1)}, u32[]{:S(2)}, u32[]{:S(2)}) %collective-permute-start.33) | collective-permute-done | bytes 196640 | tf_op jit(solution)/shard_map/ppermute | solution.py:277
  27.1 0.4 collective-permute-done.34.refs_1_
  27.5 0.1 collective-permute-start.38
  27.7 3.2 %collective-permute-start.42 = (f32[1,48,512]{2,1,0:T(8,128)S(1)}, f32[1,48,512]{2,1,0:T(8,128)S(1)}, u32[]{:S(2)}, u32[]{:S(2)}) collective-permute-start(f32[1,48,512]{2,1,0:T(8,128)S(1)} %slice.30), channel_id=1, source_target_pairs={{0,8},{4,12},{8,16},{12,20},{16,24},{20,28},{24,32},{28,36},{32,40... | collective-permute-start | bytes 294920 | tf_op jit(solution)/shard_map/ppermute | solution.py:277
  30.9 0.0 copy-start.1
  30.9 0.0 copy-start.2
  30.9 1.8 %place.2.given = f32[2,768,512]{2,1,0:T(8,128)S(1)} custom-call(s32[8]{0:T(128)S(1)} %stack.48.pos, f32[2,48,512]{2,1,0:T(8,128)S(1)} %get-tuple-element.201.refs_0_, f32[2,48,512]{2,1,0:T(8,128)S(1)} %collective-permute-done.26.refs_1_, f32[2,48,512]{2,1,0:T(8,128)S(1)} %collective-permute-done.27.refs_2_, ...), custom_call_target="tpu_custom_call" | custom-call | bytes 3000000 | tf_op jit(solution)/shard_map/place/pallas_call | solution.py:290
  32.7 0.9 %collective-permute-done.42.t0 = f32[1,48,512]{2,1,0:T(8,128)S(1)} collective-permute-done((f32[1,48,512]{2,1,0:T(8,128)S(1)}, f32[1,48,512]{2,1,0:T(8,128)S(1)}, u32[]{:S(2)}, u32[]{:S(2)}) %collective-permute-start.42) | collective-permute-done | bytes 98336 | tf_op jit(solution)/shard_map/ppermute | solution.py:277
  33.7 3.4 %collective-permute-done.43.t1 = f32[1,48,512]{2,1,0:T(8,128)S(1)} collective-permute-done((f32[1,48,512]{2,1,0:T(8,128)S(1)}, f32[1,48,512]{2,1,0:T(8,128)S(1)}, u32[]{:S(2)}, u32[]{:S(2)}) %collective-permute-start.43) | collective-permute-done | bytes 98336 | tf_op jit(solution)/shard_map/ppermute | solution.py:277
  37.1 5.7 %early.5 = (f32[2,768,512]{2,1,0:T(8,128)S(1)}, f32[896,512]{1,0:T(8,128)S(1)}, f32[2,96,128]{2,1,0:T(8,128)S(1)}) custom-call(s32[8]{0:T(128)S(1)} %stack.48.pos, s32[16]{0:T(128)S(1)} %convert_reduce_fusion.starts, s32[8]{0:T(128)S(1)} %copy-done.2, s32[16]{0:T(128)S(1)} %copy-done.1, ...), custom_call_target="tpu_custom_call", output_to_operand_aliasing={{0}: (4, {})} | custom-call | flops 4000000000 | bytes 12000000 | tf_op jit(solution)/shard_map/early/pallas_call | solution.py:300
  42.8 2.7 %late.5 = (f32[896,512]{1,0:T(8,128)S(1)}, f32[96,512]{1,0:T(8,128)S(1)}, f32[96,512]{1,0:T(8,128)S(1)}, f32[96,512]{1,0:T(8,128)}, f32[96,512]{1,0:T(8,128)}) custom-call(s32[8]{0:T(128)S(1)} %stack.48.pos, s32[16]{0:T(128)S(1)} %convert_reduce_fusion.starts, s32[8]{0:T(128)S(1)} %copy-done.2, s32[16]{0:T(128)S(1)} %copy-done.1, ...), custom_call_target="tpu_custom_call", output_to_operand_aliasing={{0}: (4, {})} | custom-call | tf_op jit(solution)/shard_map/late/pallas_call | solution.py:317
  45.5 1.6 %collective-permute-start.46 = (f32[96,512]{1,0:T(8,128)S(1)}, f32[96,512]{1,0:T(8,128)S(1)}, u32[]{:S(2)}, u32[]{:S(2)}) collective-permute-start(f32[96,512]{1,0:T(8,128)S(1)} %get-tuple-element.205), channel_id=1, source_target_pairs={{0,1},{1,2},{2,3},{3,0},{4,5},{5,6},{6,7},{7,4},{8,9},{9,10},{10,1... | collective-permute-start | bytes 589832 | tf_op jit(solution)/shard_map/ppermute | solution.py:271
  47.0 1.7 %collective-permute-start.47 = (f32[96,512]{1,0:T(8,128)S(1)}, f32[96,512]{1,0:T(8,128)S(1)}, u32[]{:S(2)}, u32[]{:S(2)}) collective-permute-start(f32[96,512]{1,0:T(8,128)S(1)} %get-tuple-element.206), channel_id=1, source_target_pairs={{0,3},{1,0},{2,1},{3,2},{4,7},{5,4},{6,5},{7,6},{8,11},{9,8},{10,9... | collective-permute-start | bytes 589832 | tf_op jit(solution)/shard_map/ppermute | solution.py:271
  48.7 0.8 %subtract_reduce_fusion = (s32[]{:T(128)}, s32[8]{0:T(128)S(1)}, s32[8]{0:T(128)S(1)}) fusion(s32[16]{0:T(128)S(1)} %convert_reduce_fusion.starts), kind=kLoop, calls=%fused_computation.11 | loop fusion | flops 143 | bytes 132 | tf_op jit(solution)/shard_map/reduce_max | solution.py:373
  49.5 0.4 collective-permute-start.49
  49.8 2.9 %collective-permute-start.50 = (f32[96,512]{1,0:T(8,128)}, f32[96,512]{1,0:T(8,128)}, u32[]{:S(2)}, u32[]{:S(2)}) collective-permute-start(f32[96,512]{1,0:T(8,128)} %get-tuple-element.209), channel_id=1, source_target_pairs={{0,3},{1,0},{2,1},{3,2},{4,7},{5,4},{6,5},{7,6},{8,11},{9,8},{10,9... | collective-permute-start | bytes 589832 | tf_op jit(solution)/shard_map/ppermute | solution.py:271
  52.7 1.7 %collective-permute-done.46.relay_up = f32[96,512]{1,0:T(8,128)S(1)} collective-permute-done((f32[96,512]{1,0:T(8,128)S(1)}, f32[96,512]{1,0:T(8,128)S(1)}, u32[]{:S(2)}, u32[]{:S(2)}) %collective-permute-start.46) | collective-permute-done | bytes 196640 | tf_op jit(solution)/shard_map/ppermute | solution.py:271
  54.4 0.4 collective-permute-done.47.relay_down
  54.8 1.4 %join.5 = (f32[96,512]{1,0:T(8,128)}, f32[96,512]{1,0:T(8,128)}) custom-call(s32[8]{0:T(128)S(1)} %stack.48.pos, f32[896,512]{1,0:T(8,128)S(1)} %get-tuple-element.204.total.refs_0_, f32[96,512]{1,0:T(8,128)S(1)} %collective-permute-done.46.relay_up, f32[96,512]{1,0:T(8,128)S(1)} %collective-permute-done.47.relay_down), custom_call_target="tpu_custom_call" | custom-call | tf_op jit(solution)/shard_map/join/pallas_call | solution.py:329
  56.2 1.6 %collective-permute-start.48 = (f32[96,512]{1,0:T(8,128)}, f32[96,512]{1,0:T(8,128)}, u32[]{:S(2)}, u32[]{:S(2)}) collective-permute-start(f32[96,512]{1,0:T(8,128)} %get-tuple-element.207), channel_id=1, source_target_pairs={{0,1},{1,2},{2,3},{3,0},{4,5},{5,6},{6,7},{7,4},{8,9},{9,10},{10,1... | collective-permute-start | bytes 589832 | tf_op jit(solution)/shard_map/ppermute | solution.py:271
  57.7 1.7 %collective-permute-start.51 = (f32[96,512]{1,0:T(8,128)}, f32[96,512]{1,0:T(8,128)}, u32[]{:S(2)}, u32[]{:S(2)}) collective-permute-start(f32[96,512]{1,0:T(8,128)} %get-tuple-element.210), channel_id=1, source_target_pairs={{0,3},{1,0},{2,1},{3,2},{4,7},{5,4},{6,5},{7,6},{8,11},{9,8},{10,9... | collective-permute-start | bytes 589832 | tf_op jit(solution)/shard_map/ppermute | solution.py:271
  59.4 0.1 subtract_maximum_fusion
  59.5 0.7 %multiply_reduce_fusion = s32[4,8]{1,0:T(4,128)S(1)} fusion(s32[8,8,8]{2,1,0:T(8,128)S(1)} %fusion, s32[4,8]{1,0:T(4,128)S(1)} %subtract_maximum_fusion), kind=kLoop, calls=%fused_computation | loop fusion | flops 4064 | bytes 2304 | tf_op jit(solution)/shard_map/reduce_sum | solution.py:371
  60.2 0.7 %reduce_max.18 = s32[]{:T(128)} reduce(s32[4,8]{1,0:T(4,128)S(1)} %multiply_reduce_fusion, s32[]{:T(128)} %constant.89.clone.1), dimensions={0,1}, to_apply=%region_2.0 | reduce | flops 31 | bytes 136 | tf_op jit(solution)/shard_map/reduce_max | solution.py:371
  62.4 1.1 %collective-permute-done.48.refs_1_ = f32[96,512]{1,0:T(8,128)} collective-permute-done((f32[96,512]{1,0:T(8,128)}, f32[96,512]{1,0:T(8,128)}, u32[]{:S(2)}, u32[]{:S(2)}) %collective-permute-start.48) | collective-permute-done | bytes 196640 | tf_op jit(solution)/shard_map/ppermute | solution.py:271
  63.4 0.3 collective-permute-done.51.refs_4_
  63.7 4.0 %expand.5 = f32[1,192,1536]{2,1,0:T(8,128)} custom-call(s32[8]{0:T(128)S(1)} %stack.48.pos, s32[16]{0:T(128)S(1)} %convert_reduce_fusion.starts, s32[8]{0:T(128)S(1)} %copy-done, s32[16]{0:T(128)S(1)} %copy-done.1, bf16[512,1536]{1,0:T(8,128)(2,1)S(1)} %get-tuple-element.200.g_ref, f32[896,512]{1,0:T(8,128)S(1)} %get-tuple-element.204.total.refs_0_, ...), custom_call_target="tpu_custom_call" | custom-call | tf_op jit(solution)/shard_map/expand/pallas_call | solution.py:340
  (30 shorter events, 0.1 us)
Async XLA Ops:
  3.2 6.7 %collective-permute-start.26 = (f32[2,48,512]{2,1,0:T(8,128)S(1)}, f32[2,48,512]{2,1,0:T(8,128)S(1)}, u32[]{:S(2)}, u32[]{:S(2)}) collective-permute-start(f32[2,48,512]{2,1,0:T(8,128)S(1)} %get-tuple-element.201.refs_0_), channel_id=1, source_target_pairs={{0,8},{4,12},{8,16},{12,20},{16,24},{20,28},{24,32},{28,36},{32,40... | collective-permute-start | bytes 589832 | tf_op jit(solution)/shard_map/ppermute | solution.py:277
  5.2 6.6 %collective-permute-start.27 = (f32[2,48,512]{2,1,0:T(8,128)S(1)}, f32[2,48,512]{2,1,0:T(8,128)S(1)}, u32[]{:S(2)}, u32[]{:S(2)}) collective-permute-start(f32[2,48,512]{2,1,0:T(8,128)S(1)} %get-tuple-element.201.refs_0_), channel_id=1, source_target_pairs={{0,56},{4,60},{8,0},{12,4},{16,8},{20,12},{24,16},{28,20},{32,24},... | collective-permute-start | bytes 589832 | tf_op jit(solution)/shard_map/ppermute | solution.py:277
  5.3 11.9 %collective-permute-start.30 = (f32[2,48,512]{2,1,0:T(8,128)S(1)}, f32[2,48,512]{2,1,0:T(8,128)S(1)}, u32[]{:S(2)}, u32[]{:S(2)}) collective-permute-start(f32[2,48,512]{2,1,0:T(8,128)S(1)} %get-tuple-element.201.refs_0_), channel_id=1, source_target_pairs={{0,4},{4,0},{8,12},{12,8},{16,20},{20,16},{24,28},{28,24},{32,36},... | collective-permute-start | bytes 589832 | tf_op jit(solution)/shard_map/ppermute | solution.py:274
  5.3 16.4 %copy-start = (s32[8]{0:T(128)S(1)}, s32[8]{0:T(128)}, u32[]{:S(2)}) copy-start(s32[8]{0:T(128)} %first.3) | copy-start | bytes 100
  7.2 11.1 %collective-permute-start.39 = (f32[2,192,128]{2,1,0:T(8,128)S(1)}, f32[2,192,128]{2,1,0:T(8,128)S(1)}, u32[]{:S(2)}, u32[]{:S(2)}) collective-permute-start(f32[2,192,128]{2,1,0:T(8,128)S(1)} %pack_w.2.refs_6_), channel_id=1, source_target_pairs={{0,64},{64,128},{128,192},{192,0},{1,65},{65,129},{129,193},{193,1... | collective-permute-start | bytes 589832 | tf_op jit(solution)/shard_map/ppermute | solution.py:271
  9.9 8.5 %collective-permute-start.28 = (f32[2,48,512]{2,1,0:T(8,128)S(1)}, f32[2,48,512]{2,1,0:T(8,128)S(1)}, u32[]{:S(2)}, u32[]{:S(2)}) collective-permute-start(f32[2,48,512]{2,1,0:T(8,128)S(1)} %collective-permute-done.26.refs_1_), channel_id=1, source_target_pairs={{0,8},{4,12},{8,16},{12,20},{16,24},{20,28},{24,32},{28,36},{32,40... | collective-permute-start | bytes 589832 | tf_op jit(solution)/shard_map/ppermute | solution.py:277
  11.8 7.3 %collective-permute-start.29 = (f32[2,48,512]{2,1,0:T(8,128)S(1)}, f32[2,48,512]{2,1,0:T(8,128)S(1)}, u32[]{:S(2)}, u32[]{:S(2)}) collective-permute-start(f32[2,48,512]{2,1,0:T(8,128)S(1)} %collective-permute-done.27.refs_2_), channel_id=1, source_target_pairs={{0,56},{4,60},{8,0},{12,4},{16,8},{20,12},{24,16},{28,20},{32,24},... | collective-permute-start | bytes 589832 | tf_op jit(solution)/shard_map/ppermute | solution.py:277
  14.1 7.6 %collective-permute-start.40 = (f32[2,192,128]{2,1,0:T(8,128)S(1)}, f32[2,192,128]{2,1,0:T(8,128)S(1)}, u32[]{:S(2)}, u32[]{:S(2)}) collective-permute-start(f32[2,192,128]{2,1,0:T(8,128)S(1)} %pack_w.2.refs_6_), channel_id=1, source_target_pairs={{0,128},{64,192},{128,0},{192,64},{1,129},{65,193},{129,1},{193,65... | collective-permute-start | bytes 589832 | tf_op jit(solution)/shard_map/ppermute | solution.py:271
  17.1 8.6 %collective-permute-start.41 = (f32[2,192,128]{2,1,0:T(8,128)S(1)}, f32[2,192,128]{2,1,0:T(8,128)S(1)}, u32[]{:S(2)}, u32[]{:S(2)}) collective-permute-start(f32[2,192,128]{2,1,0:T(8,128)S(1)} %pack_w.2.refs_6_), channel_id=1, source_target_pairs={{0,192},{64,0},{128,64},{192,128},{1,193},{65,1},{129,65},{193,129... | collective-permute-start | bytes 589832 | tf_op jit(solution)/shard_map/ppermute | solution.py:271
  18.3 7.4 %collective-permute-start.31 = (f32[2,48,512]{2,1,0:T(8,128)S(1)}, f32[2,48,512]{2,1,0:T(8,128)S(1)}, u32[]{:S(2)}, u32[]{:S(2)}) collective-permute-start(f32[2,48,512]{2,1,0:T(8,128)S(1)} %collective-permute-done.26.refs_1_), channel_id=1, source_target_pairs={{0,4},{4,0},{8,12},{12,8},{16,20},{20,16},{24,28},{28,24},{32,36},... | collective-permute-start | bytes 589832 | tf_op jit(solution)/shard_map/ppermute | solution.py:274
  18.4 8.7 %collective-permute-start.33 = (f32[2,48,512]{2,1,0:T(8,128)S(1)}, f32[2,48,512]{2,1,0:T(8,128)S(1)}, u32[]{:S(2)}, u32[]{:S(2)}) collective-permute-start(f32[2,48,512]{2,1,0:T(8,128)S(1)} %collective-permute-done.28.refs_3_), channel_id=1, source_target_pairs={{0,8},{4,12},{8,16},{12,20},{16,24},{20,28},{24,32},{28,36},{32,40... | collective-permute-start | bytes 589832 | tf_op jit(solution)/shard_map/ppermute | solution.py:277
  19.1 8.5 %collective-permute-start.34 = (f32[2,48,512]{2,1,0:T(8,128)S(1)}, f32[2,48,512]{2,1,0:T(8,128)S(1)}, u32[]{:S(2)}, u32[]{:S(2)}) collective-permute-start(f32[2,48,512]{2,1,0:T(8,128)S(1)} %collective-permute-done.29.refs_4_), channel_id=1, source_target_pairs={{0,56},{4,60},{8,0},{12,4},{16,8},{20,12},{24,16},{28,20},{32,24},... | collective-permute-start | bytes 589832 | tf_op jit(solution)/shard_map/ppermute | solution.py:277
  21.7 5.9 %collective-permute-start.32 = (f32[2,48,512]{2,1,0:T(8,128)S(1)}, f32[2,48,512]{2,1,0:T(8,128)S(1)}, u32[]{:S(2)}, u32[]{:S(2)}) collective-permute-start(f32[2,48,512]{2,1,0:T(8,128)S(1)} %collective-permute-done.27.refs_2_), channel_id=1, source_target_pairs={{0,4},{4,0},{8,12},{12,8},{16,20},{20,16},{24,28},{28,24},{32,36},... | collective-permute-start | bytes 589832 | tf_op jit(solution)/shard_map/ppermute | solution.py:274
  25.7 5.2 %collective-permute-start.35 = (f32[2,48,512]{2,1,0:T(8,128)S(1)}, f32[2,48,512]{2,1,0:T(8,128)S(1)}, u32[]{:S(2)}, u32[]{:S(2)}) collective-permute-start(f32[2,48,512]{2,1,0:T(8,128)S(1)} %collective-permute-done.28.refs_3_), channel_id=1, source_target_pairs={{0,4},{4,0},{8,12},{12,8},{16,20},{20,16},{24,28},{28,24},{32,36},... | collective-permute-start | bytes 589832 | tf_op jit(solution)/shard_map/ppermute | solution.py:274
  25.7 11.3 %collective-permute-start.36 = (f32[2,48,512]{2,1,0:T(8,128)S(1)}, f32[2,48,512]{2,1,0:T(8,128)S(1)}, u32[]{:S(2)}, u32[]{:S(2)}) collective-permute-start(f32[2,48,512]{2,1,0:T(8,128)S(1)} %collective-permute-done.29.refs_4_), channel_id=1, source_target_pairs={{0,4},{4,0},{8,12},{12,8},{16,20},{20,16},{24,28},{28,24},{32,36},... | collective-permute-start | bytes 589832 | tf_op jit(solution)/shard_map/ppermute | solution.py:274
  27.1 9.9 %collective-permute-start.37 = (f32[2,48,512]{2,1,0:T(8,128)S(1)}, f32[2,48,512]{2,1,0:T(8,128)S(1)}, u32[]{:S(2)}, u32[]{:S(2)}) collective-permute-start(f32[2,48,512]{2,1,0:T(8,128)S(1)} %collective-permute-done.33.refs_0_), channel_id=1, source_target_pairs={{0,4},{4,0},{8,12},{12,8},{16,20},{20,16},{24,28},{28,24},{32,36},... | collective-permute-start | bytes 589832 | tf_op jit(solution)/shard_map/ppermute | solution.py:274
  27.5 9.5 %collective-permute-start.38 = (f32[2,48,512]{2,1,0:T(8,128)S(1)}, f32[2,48,512]{2,1,0:T(8,128)S(1)}, u32[]{:S(2)}, u32[]{:S(2)}) collective-permute-start(f32[2,48,512]{2,1,0:T(8,128)S(1)} %collective-permute-done.34.refs_1_), channel_id=1, source_target_pairs={{0,4},{4,0},{8,12},{12,8},{16,20},{20,16},{24,28},{28,24},{32,36},... | collective-permute-start | bytes 589832 | tf_op jit(solution)/shard_map/ppermute | solution.py:274
  27.7 6.0 %collective-permute-start.42 = (f32[1,48,512]{2,1,0:T(8,128)S(1)}, f32[1,48,512]{2,1,0:T(8,128)S(1)}, u32[]{:S(2)}, u32[]{:S(2)}) collective-permute-start(f32[1,48,512]{2,1,0:T(8,128)S(1)} %slice.30), channel_id=1, source_target_pairs={{0,8},{4,12},{8,16},{12,20},{16,24},{20,28},{24,32},{28,36},{32,40... | collective-permute-start | bytes 294920 | tf_op jit(solution)/shard_map/ppermute | solution.py:277
  30.9 6.1 %collective-permute-start.43 = (f32[1,48,512]{2,1,0:T(8,128)S(1)}, f32[1,48,512]{2,1,0:T(8,128)S(1)}, u32[]{:S(2)}, u32[]{:S(2)}) collective-permute-start(f32[1,48,512]{2,1,0:T(8,128)S(1)} %slice.31), channel_id=1, source_target_pairs={{0,56},{4,60},{8,0},{12,4},{16,8},{20,12},{24,16},{28,20},{32,24},... | collective-permute-start | bytes 294920 | tf_op jit(solution)/shard_map/ppermute | solution.py:277
  30.9 6.1 %copy-start.1 = (s32[16]{0:T(128)S(1)}, s32[16]{0:T(128)}, u32[]{:S(2)}) copy-start(s32[16]{0:T(128)} %target.7) | copy-start | bytes 196
  30.9 6.1 %copy-start.2 = (s32[8]{0:T(128)S(1)}, s32[8]{0:T(128)}, u32[]{:S(2)}) copy-start(s32[8]{0:T(128)} %second.7) | copy-start | bytes 100
  33.7 9.1 %collective-permute-start.44 = (f32[1,48,512]{2,1,0:T(8,128)S(1)}, f32[1,48,512]{2,1,0:T(8,128)S(1)}, u32[]{:S(2)}, u32[]{:S(2)}) collective-permute-start(f32[1,48,512]{2,1,0:T(8,128)S(1)} %collective-permute-done.42.t0), channel_id=1, source_target_pairs={{0,4},{4,0},{8,12},{12,8},{16,20},{20,16},{24,28},{28,24},{32,36},... | collective-permute-start | bytes 294920 | tf_op jit(solution)/shard_map/ppermute | solution.py:274
  37.0 5.8 %collective-permute-start.45 = (f32[1,48,512]{2,1,0:T(8,128)S(1)}, f32[1,48,512]{2,1,0:T(8,128)S(1)}, u32[]{:S(2)}, u32[]{:S(2)}) collective-permute-start(f32[1,48,512]{2,1,0:T(8,128)S(1)} %collective-permute-done.43.t1), channel_id=1, source_target_pairs={{0,4},{4,0},{8,12},{12,8},{16,20},{20,16},{24,28},{28,24},{32,36},... | collective-permute-start | bytes 294920 | tf_op jit(solution)/shard_map/ppermute | solution.py:274
  45.5 9.0 %collective-permute-start.46 = (f32[96,512]{1,0:T(8,128)S(1)}, f32[96,512]{1,0:T(8,128)S(1)}, u32[]{:S(2)}, u32[]{:S(2)}) collective-permute-start(f32[96,512]{1,0:T(8,128)S(1)} %get-tuple-element.205), channel_id=1, source_target_pairs={{0,1},{1,2},{2,3},{3,0},{4,5},{5,6},{6,7},{7,4},{8,9},{9,10},{10,1... | collective-permute-start | bytes 589832 | tf_op jit(solution)/shard_map/ppermute | solution.py:271
  47.0 7.8 %collective-permute-start.47 = (f32[96,512]{1,0:T(8,128)S(1)}, f32[96,512]{1,0:T(8,128)S(1)}, u32[]{:S(2)}, u32[]{:S(2)}) collective-permute-start(f32[96,512]{1,0:T(8,128)S(1)} %get-tuple-element.206), channel_id=1, source_target_pairs={{0,3},{1,0},{2,1},{3,2},{4,7},{5,4},{6,5},{7,6},{8,11},{9,8},{10,9... | collective-permute-start | bytes 589832 | tf_op jit(solution)/shard_map/ppermute | solution.py:271
  49.5 12.9 %collective-permute-start.49 = (f32[96,512]{1,0:T(8,128)}, f32[96,512]{1,0:T(8,128)}, u32[]{:S(2)}, u32[]{:S(2)}) collective-permute-start(f32[96,512]{1,0:T(8,128)} %get-tuple-element.208), channel_id=1, source_target_pairs={{0,1},{1,2},{2,3},{3,0},{4,5},{5,6},{6,7},{7,4},{8,9},{9,10},{10,1... | collective-permute-start | bytes 589832 | tf_op jit(solution)/shard_map/ppermute | solution.py:271
  49.8 12.5 %collective-permute-start.50 = (f32[96,512]{1,0:T(8,128)}, f32[96,512]{1,0:T(8,128)}, u32[]{:S(2)}, u32[]{:S(2)}) collective-permute-start(f32[96,512]{1,0:T(8,128)} %get-tuple-element.209), channel_id=1, source_target_pairs={{0,3},{1,0},{2,1},{3,2},{4,7},{5,4},{6,5},{7,6},{8,11},{9,8},{10,9... | collective-permute-start | bytes 589832 | tf_op jit(solution)/shard_map/ppermute | solution.py:271
  56.2 7.3 %collective-permute-start.48 = (f32[96,512]{1,0:T(8,128)}, f32[96,512]{1,0:T(8,128)}, u32[]{:S(2)}, u32[]{:S(2)}) collective-permute-start(f32[96,512]{1,0:T(8,128)} %get-tuple-element.207), channel_id=1, source_target_pairs={{0,1},{1,2},{2,3},{3,0},{4,5},{5,6},{6,7},{7,4},{8,9},{9,10},{10,1... | collective-permute-start | bytes 589832 | tf_op jit(solution)/shard_map/ppermute | solution.py:271
  57.7 6.0 %collective-permute-start.51 = (f32[96,512]{1,0:T(8,128)}, f32[96,512]{1,0:T(8,128)}, u32[]{:S(2)}, u32[]{:S(2)}) collective-permute-start(f32[96,512]{1,0:T(8,128)} %get-tuple-element.210), channel_id=1, source_target_pairs={{0,3},{1,0},{2,1},{3,2},{4,7},{5,4},{6,5},{7,6},{8,11},{9,8},{10,9... | collective-permute-start | bytes 589832 | tf_op jit(solution)/shard_map/ppermute | solution.py:271

commit v5 on v4

--- a/solution.py
+++ b/solution.py
@@ -108,51 +108,50 @@
     return both[: w.shape[1]] + both[w.shape[1] :] + tn(w_high, t_low)
 
 
-def fetch_windows(pos, windows, into, sems):
-    copies = []
-    for n, ((far, other), piece) in enumerate(windows):
-        core = 1 - pos[1] % 2 if other else pos[1] % 2
-        at = (lax.rem(pos[1] // 2 + far + 8, 8) * 2 + core) * piece.shape[1]
-        there = into.at[:, pl.ds(pl.multiple_of(at, 8), piece.shape[1]), :]
-        copies.append(pltpu.make_async_copy(piece, there, sems.at[n]))
-        copies[-1].start()
-    return copies
+def put_window(pos, place, piece, into, k=None):
+    size = piece.shape[1]
+    core = 1 - pos[1] % 2 if place[1] else pos[1] % 2
+    at = (lax.rem(pos[1] // 2 + place[0] + 8, 8) * 2 + core) * size
+    rows = pl.ds(pl.multiple_of(at, 8), size)
+    for n in range(piece.shape[0]):
+        into[n if k is None else k, rows, :] = piece[n]
 
 
 def place_kernel(where, pos, *refs):
-    pieces, (t_all, sems) = refs[: len(where)], refs[len(where) :]
-    for copy in fetch_windows(pos, list(zip(where, pieces)), t_all, sems):
-        copy.wait()
-
-
-def early_kernel(where, pos, starts, second, target, given, *refs):
-    pieces, ws, (t_all, total, w_out, w_all, sems) = refs[: len(where)], refs[len(where) : len(where) + 4], refs[len(where) + 4 :]
+    pieces, (own, pair, far), (t_all, w_all) = refs[: len(where)], refs[len(where) : -2], refs[-2:]
+    for place, piece in zip(where, pieces):
+        put_window(pos, place, piece, t_all)
+    size = own.shape[1]
+    r = pos[0]
+    for row, piece in ((r, own), (r ^ 1, pair), (3 - r, far.at[0]), ((3 - r) ^ 1, far.at[1])):
+        for k in range(own.shape[0]):
+            w_all[k, pl.ds(pl.multiple_of(row * size, 8), size), :] = piece[k]
+
+
+def rows_for(pos, total, step, part):
+    b_local = (total.shape[0] - BLOCK) // 4
+    at = lax.rem(pos[2] + step, 4) * b_local + part * (b_local // 2)
+    return total[pl.ds(pl.multiple_of(at, 8), b_local // 2), :]
+
+
+def product_kernel(where, pos, starts, second, target, given, w_all, *refs):
+    pieces, (t_all, total, up, down, one, three) = refs[: len(where)], refs[len(where) :]
     k_local, c_all, _ = t_all.shape
-    chip = pos[1] // 2
-    missing = c_all // 8
-    copies = fetch_windows(pos, list(zip(where, pieces)), t_all, sems)
-    for n, w in enumerate(ws):
-        at = pl.multiple_of(lax.rem(pos[0] - n + 4, 4) * w.shape[1], 8)
-        copies.append(pltpu.make_async_copy(w, w_all.at[:, pl.ds(at, w.shape[1]), :], sems.at[len(where) + n]))
-        copies[-1].start()
-    at = pl.multiple_of(lax.rem(chip + 4, 8) * missing, 8)
-    for k in range(k_local):
-        t_all[k, pl.ds(at, missing), :] = jnp.zeros((missing, LANES), F32)
+    for (k, place), piece in zip(where, pieces):
+        put_window(pos, place, piece, t_all, k)
     total[...] = jnp.zeros_like(total)
-    for copy in copies:
-        copy.wait()
-    w_out[...] = w_all[:, pl.ds(at, missing), :]
     row = lax.broadcasted_iota(I32, (128, 1), 0)
 
     def one_irrep(irrep, _):
         s = target[pos[1]] ^ irrep
+        to = starts[irrep] // 8 * 8 + pos[4] * BLOCK
         spans = []
         for k in range(k_local):
             p = s ^ second[pos[2] * k_local + k]
             spans.append((starts[p], starts[p + 1], starts[p] // 8 * 8))
-        trips = [(end - aligned + 127) // 128 for _, end, aligned in spans]
-
-        def step(n, acc):
+        trips = jnp.maximum(*[(end - aligned + 127) // 128 for _, end, aligned in spans])
+
+        def step(n, _):
             w_rows, t_rows = [], []
             for k, (begin, end, aligned) in enumerate(spans):
                 nominal = aligned + n * 128
@@ -161,52 +160,13 @@
                 keep = (c >= jnp.maximum(begin, nominal)) & (c < end)
                 w_rows.append(jnp.where(keep, w_all[k, pl.ds(at, 128), :], 0.0))
                 t_rows.append(t_all[k, pl.ds(at, 128), :])
-            return acc + three_terms(jnp.concatenate(w_rows, 0), jnp.concatenate(t_rows, 0))
-
-        sums = lax.fori_loop(0, jnp.maximum(*trips), step, jnp.zeros((BLOCK, LANES), F32))
-        to = starts[irrep] // 8 * 8 + pos[4] * BLOCK
-
-        @pl.when(to < starts[irrep + 1])
-        def _():
-            total[pl.ds(pl.multiple_of(to, 8), BLOCK), :] += sums
-
-        return 0
+            term = three_terms(jnp.concatenate(w_rows, 0), jnp.concatenate(t_rows, 0))
+            total[pl.ds(pl.multiple_of(to, 8), BLOCK), :] += term
+            return 0
+
+        return lax.fori_loop(0, jnp.where(to < starts[irrep + 1], trips, 0), step, 0)
 
     lax.fori_loop(0, 8, one_irrep, 0)
-
-
-def rows_for(pos, total, step, part):
-    b_local = (total.shape[0] - BLOCK) // 4
-    at = lax.rem(pos[2] + step, 4) * b_local + part * (b_local // 2)
-    return total[pl.ds(pl.multiple_of(at, 8), b_local // 2), :]
-
-
-def late_kernel(pos, starts, second, target, given, w, t0, t1, u0, u1, total, up, down, one, three, t_all):
-    half = t0.shape[1]
-    c_late = 2 * half
-    chip, core = pos[1] // 2, pos[1] % 2
-    for k, of_core, piece in ((0, core, t0), (1, core, t1), (0, 1 - core, u0), (1, 1 - core, u1)):
-        t_all[k, pl.ds(pl.multiple_of(of_core * half, 8), half), :] = piece[0]
-    base = lax.rem(chip + 4, 8) * c_late
-    label = label_of(base + lax.broadcasted_iota(I32, (c_late, 1), 0), starts)
-    first_p = last_p = 0
-    for irrep in range(1, 8):
-        first_p = first_p + (base >= starts[irrep]).astype(I32)
-        last_p = last_p + (base + c_late - 1 >= starts[irrep]).astype(I32)
-
-    def one_p(p, _):
-        for k in range(2):
-            irrep = p ^ second[pos[2] * 2 + k] ^ target[pos[1]]
-            term = three_terms(jnp.where(label == p, w[k], 0.0), t_all[k])
-            to = starts[irrep] // 8 * 8 + pos[4] * BLOCK
-
-            @pl.when(to < starts[irrep + 1])
-            def _(term=term, to=to):
-                total[pl.ds(pl.multiple_of(to, 8), BLOCK), :] += term
-
-        return 0
-
-    lax.fori_loop(first_p, last_p + 1, one_p, 0)
     for out, step, part in ((up, 2, 0), (down, 2, 1), (one, 1, 1), (three, 3, 0)):
         out[...] = rows_for(pos, total, step, part)
 
@@ -240,8 +200,8 @@
     lax.fori_loop(0, x_local // width, tile, 0)
 
 
-def params():
-    return pltpu.CompilerParams(vmem_limit_bytes=24 * 1024 * 1024)
+def params(mib=16):
+    return pltpu.CompilerParams(vmem_limit_bytes=mib * 1024 * 1024)
 
 
 def one_pass(pos, starts, first, second, target, amplitudes, integrals, w_rows, before):
@@ -284,46 +244,29 @@
     late = [ring(right[:1], 1), ring(left[1:], -1)]
     for (far, _), piece in list(got.items()):
         got[far, True] = swap(piece)
-    ws = [w0] + [along(w0, "row", n) for n in range(1, 4)]
-    arrived = [place for place in got if abs(place[0]) <= (1 if place[1] else 2)]
-    others = [place for place in got if place not in arrived]
-    t_all = pl.pallas_call(
-        functools.partial(place_kernel, arrived),
-        out_shape=shape((k_local, v, LANES), F32),
-        in_specs=[SMEM] + [ANY] * len(arrived),
-        out_specs=VMEM,
-        scratch_shapes=[pltpu.SemaphoreType.DMA((len(arrived),))],
-        compiler_params=params(),
-        cost_estimate=pl.CostEstimate(flops=0, bytes_accessed=3 * 10**6, transcendentals=0),
+    pair = lax.ppermute(w0, "row", [(i, i ^ 1) for i in range(4)])
+    far = lax.ppermute(jnp.stack([w0, pair]), "row", [(i, 3 - i) for i in range(4)])
+    t_all, w_all = pl.pallas_call(
+        functools.partial(place_kernel, list(got)),
+        out_shape=(shape((k_local, v, LANES), F32), shape((k_local, v, BLOCK), F32)),
+        in_specs=[SMEM] + [VMEM] * (len(got) + 3),
+        out_specs=(VMEM,) * 2,
+        compiler_params=params(),
+        cost_estimate=pl.CostEstimate(flops=0, bytes_accessed=7 * 10**6, transcendentals=0),
         name="place",
-    )(pos, *[got[place] for place in arrived])
-    _, total, w_late = pl.pallas_call(
-        functools.partial(early_kernel, others),
-        out_shape=(
-            shape(t_all.shape, F32),
-            shape((v + BLOCK, LANES), F32),
-            shape((k_local, v // 8, BLOCK), F32),
-        ),
-        in_specs=[SMEM] * 4 + [VMEM] + [ANY] * (len(others) + 4),
-        out_specs=(VMEM,) * 3,
-        scratch_shapes=[pltpu.VMEM((k_local, v, BLOCK), F32), pltpu.SemaphoreType.DMA((len(others) + 4,))],
+    )(pos, *got.values(), w0, pair, far)
+    late += [swap(piece) for piece in late]
+    where = [(0, (4, False)), (1, (4, False)), (0, (4, True)), (1, (4, True))]
+    part = shape((b_local // 2, LANES), F32)
+    _, total, up, down, one_1, three_0 = pl.pallas_call(
+        functools.partial(product_kernel, where),
+        out_shape=(shape(t_all.shape, F32), shape((v + BLOCK, LANES), F32)) + (part,) * 4,
+        in_specs=[SMEM] * 4 + [VMEM] * 6,
+        out_specs=(VMEM,) * 6,
         input_output_aliases={4: 0},
         compiler_params=params(),
-        cost_estimate=pl.CostEstimate(flops=4 * 10**9, bytes_accessed=12 * 10**6, transcendentals=0),
-        name="early",
-    )(pos, starts, second, target, t_all, *[got[place] for place in others], *ws)
-    late += [swap(piece) for piece in late]
-    part = shape((b_local // 2, LANES), F32)
-    total, up, down, one_1, three_0 = pl.pallas_call(
-        late_kernel,
-        out_shape=(shape(total.shape, F32),) + (part,) * 4,
-        in_specs=[SMEM] * 4 + [VMEM] * 6,
-        out_specs=(VMEM,) * 5,
-        scratch_shapes=[pltpu.VMEM((k_local, v // 8, LANES), F32)],
-        input_output_aliases={4: 0},
-        compiler_params=params(),
-        name="late",
-    )(pos, starts, second, target, total, w_late, *late)
+        name="product",
+    )(pos, starts, second, target, t_all, w_all, *late)
     up, down = along(up, "depth", 1), along(down, "depth", -1)
     one_1, three_0 = along(one_1, "depth", 1), along(three_0, "depth", -1)
     one_0, three_1 = pl.pallas_call(
@@ -331,7 +274,7 @@
         out_shape=(part,) * 2,
         in_specs=[SMEM] + [VMEM] * 3,
         out_specs=(VMEM,) * 2,
-        compiler_params=params(),
+        compiler_params=params(4),
         name="join",
     )(pos, total, up, down)
     one_0, three_1 = along(one_0, "depth", 1), along(three_1, "depth", -1)

time: 67.9 us -> 66.4 us (0.978)
  the two profiles are of different devices: /device:TPU:32 before, /device:TPU:24 now
where the time goes in v5:
time: 66.4 us; the launch traced here: 66.2 us
  starting transfers between devices  27.2 us (41%)
  waiting for transfers between devices  19.5 us (29%)
  Pallas kernels  14.7 us (22%)
  other arithmetic  3.13 us (5%)
  between operations  1.49 us (2%)
    ppermute x8, starting transfers between devices, ring(): return lax.ppermute(x, 'col', [(i, (i + 2 * step) % 16) for i in range(16)])  15.1 us
    ppermute x8, waiting for transfers between devices, ring(): return lax.ppermute(x, 'col', [(i, (i + 2 * step) % 16) for i in range(16)])  9.9 us
    ppermute x6, waiting for transfers between devices, along(): return lax.ppermute(x, axis, [(i, (i + step) % 4) for i in range(4)])  7.04 us
    ppermute x6, starting transfers between devices, along(): return lax.ppermute(x, axis, [(i, (i + step) % 4) for i in range(4)])  6.08 us
    pallas_call x1, Pallas kernels, one_pass(): pl.pallas_call(functools.partial(product_kernel, where), out_shape=(shape...  4.41 us
    pallas_call x1, Pallas kernels, one_pass(): pl.pallas_call(expand_kernel, out_shape=shape((1, b_local, x_local), F32)...  3.98 us
    ppermute x1, starting transfers between devices, one_pass(): lax.ppermute(jnp.stack([w0, pair]), 'row', [(i, 3 - i) for i in range(4)])  2.85 us
    pallas_call x1, Pallas kernels, one_pass(): pl.pallas_call(pack_t_kernel, out_shape=(shape((k_local, c_local, LANES),...  2.24 us
  transfers between devices with their start and end apart: 25, of which 11 were waited for; matrix products, arithmetic and copies ran while one was open for 4% of the time, Pallas kernels for 6%

profile of v5, /device:TPU:24, one launch (start us, length us, event | category | flops | bytes accessed | tf_op | source)
XLA Modules:
  0.0 66.2 jit_solution(3791124372062769604)
XLA Ops:
  0.0 0.8 %convert_reduce_fusion.starts = s32[16]{0:T(128)S(1)} fusion(s32[768]{0:T(1024)} %param.10), kind=kLoop, calls=%fused_computation.3 | loop fusion | flops 36848 | bytes 3136 | tf_op jit(solution)/shard_map/reduce_sum | solution.py:296
  0.8 0.1 stack.75.pos
  0.9 2.2 %pack_t.5 = (f32[2,48,512]{2,1,0:T(8,128)S(1)}, bf16[512,1536]{1,0:T(8,128)(2,1)S(1)}) custom-call(s32[8]{0:T(128)S(1)} %stack.75.pos, s32[16]{0:T(128)S(1)} %convert_reduce_fusion.starts, s32[8]{0:T(128)} %first.3, s32[8]{0:T(128)} %second.5, f32[2,48,1536]{2,1,0:T(8,128)} %t_ref.1), custom_call_target="tpu_custom_call" | custom-call | tf_op jit(solution)/shard_map/pack_t/pallas_call | solution.py:212
  3.2 5.9 %collective-permute-start.26 = (f32[2,48,512]{2,1,0:T(8,128)S(1)}, f32[2,48,512]{2,1,0:T(8,128)S(1)}, u32[]{:S(2)}, u32[]{:S(2)}) collective-permute-start(f32[2,48,512]{2,1,0:T(8,128)S(1)} %get-tuple-element.201.refs_0_), channel_id=1, source_target_pairs={{0,56},{4,60},{8,0},{12,4},{16,8},{20,12},{24,16},{28,20},{32,24},... | collective-permute-start | bytes 589832 | tf_op jit(solution)/shard_map/ppermute | solution.py:237
  9.1 0.0 collective-permute-start.25
  9.1 4.1 %collective-permute-done.26.refs_2_ = f32[2,48,512]{2,1,0:T(8,128)S(1)} collective-permute-done((f32[2,48,512]{2,1,0:T(8,128)S(1)}, f32[2,48,512]{2,1,0:T(8,128)S(1)}, u32[]{:S(2)}, u32[]{:S(2)}) %collective-permute-start.26) | collective-permute-done | bytes 196640 | tf_op jit(solution)/shard_map/ppermute | solution.py:237
  13.2 3.7 %collective-permute-start.28 = (f32[2,48,512]{2,1,0:T(8,128)S(1)}, f32[2,48,512]{2,1,0:T(8,128)S(1)}, u32[]{:S(2)}, u32[]{:S(2)}) collective-permute-start(f32[2,48,512]{2,1,0:T(8,128)S(1)} %collective-permute-done.26.refs_2_), channel_id=1, source_target_pairs={{0,56},{4,60},{8,0},{12,4},{16,8},{20,12},{24,16},{28,20},{32,24},... | collective-permute-start | bytes 589832 | tf_op jit(solution)/shard_map/ppermute | solution.py:237
  16.9 0.0 collective-permute-done.25.refs_1_
  16.9 0.0 collective-permute-start.27
  17.0 1.9 %pack_w.2.refs_14_ = f32[2,192,128]{2,1,0:T(8,128)S(1)} custom-call(s32[8]{0:T(128)S(1)} %stack.75.pos, s32[16]{0:T(128)S(1)} %convert_reduce_fusion.starts, s32[8]{0:T(128)} %second.5, s32[16]{0:T(128)} %target.5, f32[2304,128]{1,0:T(8,128)} %bitcast.31), custom_call_target="tpu_custom_call" | custom-call | flops 1000000000 | bytes 4000000 | tf_op jit(solution)/shard_map/pack_w/pallas_call | solution.py:220
  18.9 1.6 %collective-permute-start.38 = (f32[2,192,128]{2,1,0:T(8,128)S(1)}, f32[2,192,128]{2,1,0:T(8,128)S(1)}, u32[]{:S(2)}, u32[]{:S(2)}) collective-permute-start(f32[2,192,128]{2,1,0:T(8,128)S(1)} %pack_w.2.refs_14_), channel_id=1, source_target_pairs={{0,64},{64,0},{128,192},{192,128},{1,65},{65,1},{129,193},{193,129... | collective-permute-start | bytes 589832 | tf_op jit(solution)/shard_map/ppermute | solution.py:247
  20.5 0.0 collective-permute-done.28.refs_4_
  20.5 3.4 %collective-permute-start.30 = (f32[2,48,512]{2,1,0:T(8,128)S(1)}, f32[2,48,512]{2,1,0:T(8,128)S(1)}, u32[]{:S(2)}, u32[]{:S(2)}) collective-permute-start(f32[2,48,512]{2,1,0:T(8,128)S(1)} %collective-permute-done.28.refs_4_), channel_id=1, source_target_pairs={{0,56},{4,60},{8,0},{12,4},{16,8},{20,12},{24,16},{28,20},{32,24},... | collective-permute-start | bytes 589832 | tf_op jit(solution)/shard_map/ppermute | solution.py:237
  23.9 0.0 collective-permute-done.27.refs_3_
  23.9 0.7 %collective-permute-done.38.refs_15_ = f32[2,192,128]{2,1,0:T(8,128)S(1)} collective-permute-done((f32[2,192,128]{2,1,0:T(8,128)S(1)}, f32[2,192,128]{2,1,0:T(8,128)S(1)}, u32[]{:S(2)}, u32[]{:S(2)}) %collective-permute-start.38) | collective-permute-done | bytes 196640 | tf_op jit(solution)/shard_map/ppermute | solution.py:247
  24.7 2.8 %collective-permute-start.39 = (f32[2,2,192,128]{3,2,1,0:T(8,128)S(1)}, f32[2,2,192,128]{3,2,1,0:T(8,128)S(1)}, u32[]{:S(2)}, u32[]{:S(2)}) collective-permute-start(f32[2,2,192,128]{3,2,1,0:T(8,128)S(1)} %pad_maximum_fusion.1), channel_id=1, source_target_pairs={{0,192},{64,128},{128,64},{192,0},{1,193},{65,129},{129,65},{193,1... | collective-permute-start | bytes 1179656 | tf_op jit(solution)/shard_map/ppermute | solution.py:248
  27.5 0.0 collective-permute-start.31
  27.5 0.5 collective-permute-start.33
  28.1 0.0 collective-permute-start.32
  28.1 2.8 %collective-permute-done.29.refs_5_ = f32[2,48,512]{2,1,0:T(8,128)S(1)} collective-permute-done((f32[2,48,512]{2,1,0:T(8,128)S(1)}, f32[2,48,512]{2,1,0:T(8,128)S(1)}, u32[]{:S(2)}, u32[]{:S(2)}) %collective-permute-start.29) | collective-permute-done | bytes 196640 | tf_op jit(solution)/shard_map/ppermute | solution.py:237
  30.9 0.6 collective-permute-start.34
  31.5 1.0 %collective-permute-start.41 = (f32[1,48,512]{2,1,0:T(8,128)S(1)}, f32[1,48,512]{2,1,0:T(8,128)S(1)}, u32[]{:S(2)}, u32[]{:S(2)}) collective-permute-start(f32[1,48,512]{2,1,0:T(8,128)S(1)} %slice.31), channel_id=1, source_target_pairs={{0,56},{4,60},{8,0},{12,4},{16,8},{20,12},{24,16},{28,20},{32,24},... | collective-permute-start | bytes 294920 | tf_op jit(solution)/shard_map/ppermute | solution.py:237
  32.5 1.0 %collective-permute-start.40 = (f32[1,48,512]{2,1,0:T(8,128)S(1)}, f32[1,48,512]{2,1,0:T(8,128)S(1)}, u32[]{:S(2)}, u32[]{:S(2)}) collective-permute-start(f32[1,48,512]{2,1,0:T(8,128)S(1)} %slice.30), channel_id=1, source_target_pairs={{0,8},{4,12},{8,16},{12,20},{16,24},{20,28},{24,32},{28,36},{32,40... | collective-permute-start | bytes 294920 | tf_op jit(solution)/shard_map/ppermute | solution.py:237
  33.5 1.4 %collective-permute-done.39.refs_16_ = f32[2,2,192,128]{3,2,1,0:T(8,128)S(1)} collective-permute-done((f32[2,2,192,128]{3,2,1,0:T(8,128)S(1)}, f32[2,2,192,128]{3,2,1,0:T(8,128)S(1)}, u32[]{:S(2)}, u32[]{:S(2)}) %collective-permute-start.39) | collective-permute-done | bytes 393248 | tf_op jit(solution)/shard_map/ppermute | solution.py:248
  34.8 0.0 collective-permute-start.37
  34.9 0.5 collective-permute-start.36
  35.4 0.9 %collective-permute-done.41.refs_1_ = f32[1,48,512]{2,1,0:T(8,128)S(1)} collective-permute-done((f32[1,48,512]{2,1,0:T(8,128)S(1)}, f32[1,48,512]{2,1,0:T(8,128)S(1)}, u32[]{:S(2)}, u32[]{:S(2)}) %collective-permute-start.41) | collective-permute-done | bytes 98336 | tf_op jit(solution)/shard_map/ppermute | solution.py:237
  36.3 2.1 %collective-permute-done.40.refs_0_ = f32[1,48,512]{2,1,0:T(8,128)S(1)} collective-permute-done((f32[1,48,512]{2,1,0:T(8,128)S(1)}, f32[1,48,512]{2,1,0:T(8,128)S(1)}, u32[]{:S(2)}, u32[]{:S(2)}) %collective-permute-start.40) | collective-permute-done | bytes 98336 | tf_op jit(solution)/shard_map/ppermute | solution.py:237
  38.4 0.0 copy-start.2
  38.4 0.8 %place.5 = (f32[2,768,512]{2,1,0:T(8,128)S(1)}, f32[2,768,128]{2,1,0:T(8,128)S(1)}) custom-call(s32[8]{0:T(128)S(1)} %stack.75.pos, f32[2,48,512]{2,1,0:T(8,128)S(1)} %get-tuple-element.201.refs_0_, f32[2,48,512]{2,1,0:T(8,128)S(1)} %collective-permute-done.25.refs_1_, f32[2,48,512]{2,1,0:T(8,128)S(1)} %collective-permute-done.26.refs_2_, ...), custom_call_target="tpu_custom_call" | custom-call | bytes 7000000 | tf_op jit(solution)/shard_map/place/pallas_call | solution.py:249
  39.2 0.4 collective-permute-done.42.refs_2_
  39.7 4.4 %product.5 = (f32[2,768,512]{2,1,0:T(8,128)S(1)}, f32[896,512]{1,0:T(8,128)S(1)}, f32[96,512]{1,0:T(8,128)S(1)}, f32[96,512]{1,0:T(8,128)S(1)}, f32[96,512]{1,0:T(8,128)}, /*index=5*/f32[96,512]{1,0:T(8,128)}) custom-call(s32[8]{0:T(128)S(1)} %stack.75.pos, s32[16]{0:T(128)S(1)} %convert_reduce_fusion.starts, ...), custom_call_target="tpu_custom_call", output_to_operand_aliasing={{0}: (4, {})} | custom-call | tf_op jit(solution)/shard_map/product/pallas_call | solution.py:261
  44.1 0.2 collective-permute-start.44
  44.3 1.8 %collective-permute-start.45 = (f32[96,512]{1,0:T(8,128)S(1)}, f32[96,512]{1,0:T(8,128)S(1)}, u32[]{:S(2)}, u32[]{:S(2)}) collective-permute-start(f32[96,512]{1,0:T(8,128)S(1)} %get-tuple-element.206), channel_id=1, source_target_pairs={{0,3},{1,0},{2,1},{3,2},{4,7},{5,4},{6,5},{7,6},{8,11},{9,8},{10,9... | collective-permute-start | bytes 589832 | tf_op jit(solution)/shard_map/ppermute | solution.py:231
  46.1 0.8 %subtract_reduce_fusion = (s32[]{:T(128)}, s32[8]{0:T(128)S(1)}, s32[8]{0:T(128)S(1)}) fusion(s32[16]{0:T(128)S(1)} %convert_reduce_fusion.starts), kind=kLoop, calls=%fused_computation.13 | loop fusion | flops 143 | bytes 132 | tf_op jit(solution)/shard_map/reduce_max | solution.py:316
  46.9 1.4 %collective-permute-start.47 = (f32[96,512]{1,0:T(8,128)}, f32[96,512]{1,0:T(8,128)}, u32[]{:S(2)}, u32[]{:S(2)}) collective-permute-start(f32[96,512]{1,0:T(8,128)} %get-tuple-element.208), channel_id=1, source_target_pairs={{0,1},{1,2},{2,3},{3,0},{4,5},{5,6},{6,7},{7,4},{8,9},{9,10},{10,1... | collective-permute-start | bytes 589832 | tf_op jit(solution)/shard_map/ppermute | solution.py:231
  48.3 0.6 collective-permute-start.48
  48.9 3.0 %collective-permute-done.44.relay_up = f32[96,512]{1,0:T(8,128)S(1)} collective-permute-done((f32[96,512]{1,0:T(8,128)S(1)}, f32[96,512]{1,0:T(8,128)S(1)}, u32[]{:S(2)}, u32[]{:S(2)}) %collective-permute-start.44) | collective-permute-done | bytes 196640 | tf_op jit(solution)/shard_map/ppermute | solution.py:231
  51.9 0.9 %collective-permute-done.45.relay_down = f32[96,512]{1,0:T(8,128)S(1)} collective-permute-done((f32[96,512]{1,0:T(8,128)S(1)}, f32[96,512]{1,0:T(8,128)S(1)}, u32[]{:S(2)}, u32[]{:S(2)}) %collective-permute-start.45) | collective-permute-done | bytes 196640 | tf_op jit(solution)/shard_map/ppermute | solution.py:231
  52.8 1.3 %join.5 = (f32[96,512]{1,0:T(8,128)}, f32[96,512]{1,0:T(8,128)}) custom-call(s32[8]{0:T(128)S(1)} %stack.75.pos, f32[896,512]{1,0:T(8,128)S(1)} %get-tuple-element.204.total.refs_0_, f32[96,512]{1,0:T(8,128)S(1)} %collective-permute-done.44.relay_up, f32[96,512]{1,0:T(8,128)S(1)} %collective-permute-done.45.relay_down), custom_call_target="tpu_custom_call" | custom-call | tf_op jit(solution)/shard_map/join/pallas_call | solution.py:272
  54.2 0.9 %collective-permute-start.46 = (f32[96,512]{1,0:T(8,128)}, f32[96,512]{1,0:T(8,128)}, u32[]{:S(2)}, u32[]{:S(2)}) collective-permute-start(f32[96,512]{1,0:T(8,128)} %get-tuple-element.207), channel_id=1, source_target_pairs={{0,1},{1,2},{2,3},{3,0},{4,5},{5,6},{6,7},{7,4},{8,9},{9,10},{10,1... | collective-permute-start | bytes 589832 | tf_op jit(solution)/shard_map/ppermute | solution.py:231
  55.0 1.2 %collective-permute-start.49 = (f32[96,512]{1,0:T(8,128)}, f32[96,512]{1,0:T(8,128)}, u32[]{:S(2)}, u32[]{:S(2)}) collective-permute-start(f32[96,512]{1,0:T(8,128)} %get-tuple-element.210), channel_id=1, source_target_pairs={{0,3},{1,0},{2,1},{3,2},{4,7},{5,4},{6,5},{7,6},{8,11},{9,8},{10,9... | collective-permute-start | bytes 589832 | tf_op jit(solution)/shard_map/ppermute | solution.py:231
  56.2 0.1 subtract_maximum_fusion
  56.9 0.7 %multiply_reduce_fusion = s32[4,8]{1,0:T(4,128)S(1)} fusion(s32[8,8,8]{2,1,0:T(8,128)S(1)} %fusion, s32[4,8]{1,0:T(4,128)S(1)} %subtract_maximum_fusion), kind=kLoop, calls=%fused_computation.2 | loop fusion | flops 4064 | bytes 2304 | tf_op jit(solution)/shard_map/reduce_sum | solution.py:314
  57.6 0.7 %reduce_max.18 = s32[]{:T(128)} reduce(s32[4,8]{1,0:T(4,128)S(1)} %multiply_reduce_fusion, s32[]{:T(128)} %constant.89.clone.1), dimensions={0,1}, to_apply=%region_2.0 | reduce | flops 31 | bytes 136 | tf_op jit(solution)/shard_map/reduce_max | solution.py:314
  59.1 1.1 %collective-permute-done.46.refs_1_ = f32[96,512]{1,0:T(8,128)} collective-permute-done((f32[96,512]{1,0:T(8,128)}, f32[96,512]{1,0:T(8,128)}, u32[]{:S(2)}, u32[]{:S(2)}) %collective-permute-start.46) | collective-permute-done | bytes 196640 | tf_op jit(solution)/shard_map/ppermute | solution.py:231
  60.1 2.1 %collective-permute-done.49.refs_4_ = f32[96,512]{1,0:T(8,128)} collective-permute-done((f32[96,512]{1,0:T(8,128)}, f32[96,512]{1,0:T(8,128)}, u32[]{:S(2)}, u32[]{:S(2)}) %collective-permute-start.49) | collective-permute-done | bytes 196640 | tf_op jit(solution)/shard_map/ppermute | solution.py:231
  62.2 4.0 %expand.5 = f32[1,192,1536]{2,1,0:T(8,128)} custom-call(s32[8]{0:T(128)S(1)} %stack.75.pos, s32[16]{0:T(128)S(1)} %convert_reduce_fusion.starts, s32[8]{0:T(128)S(1)} %copy-done, s32[16]{0:T(128)S(1)} %copy-done.1, bf16[512,1536]{1,0:T(8,128)(2,1)S(1)} %get-tuple-element.200.g_ref, f32[896,512]{1,0:T(8,128)S(1)} %get-tuple-element.204.total.refs_0_, ...), custom_call_target="tpu_custom_call" | custom-call | tf_op jit(solution)/shard_map/expand/pallas_call | solution.py:283
  (28 shorter events, 0.1 us)
Async XLA Ops:
  3.2 10.1 %collective-permute-start.26 = (f32[2,48,512]{2,1,0:T(8,128)S(1)}, f32[2,48,512]{2,1,0:T(8,128)S(1)}, u32[]{:S(2)}, u32[]{:S(2)}) collective-permute-start(f32[2,48,512]{2,1,0:T(8,128)S(1)} %get-tuple-element.201.refs_0_), channel_id=1, source_target_pairs={{0,56},{4,60},{8,0},{12,4},{16,8},{20,12},{24,16},{28,20},{32,24},... | collective-permute-start | bytes 589832 | tf_op jit(solution)/shard_map/ppermute | solution.py:237
  9.1 7.8 %collective-permute-start.25 = (f32[2,48,512]{2,1,0:T(8,128)S(1)}, f32[2,48,512]{2,1,0:T(8,128)S(1)}, u32[]{:S(2)}, u32[]{:S(2)}) collective-permute-start(f32[2,48,512]{2,1,0:T(8,128)S(1)} %get-tuple-element.201.refs_0_), channel_id=1, source_target_pairs={{0,8},{4,12},{8,16},{12,20},{16,24},{20,28},{24,32},{28,36},{32,40... | collective-permute-start | bytes 589832 | tf_op jit(solution)/shard_map/ppermute | solution.py:237
  13.2 7.2 %collective-permute-start.28 = (f32[2,48,512]{2,1,0:T(8,128)S(1)}, f32[2,48,512]{2,1,0:T(8,128)S(1)}, u32[]{:S(2)}, u32[]{:S(2)}) collective-permute-start(f32[2,48,512]{2,1,0:T(8,128)S(1)} %collective-permute-done.26.refs_2_), channel_id=1, source_target_pairs={{0,56},{4,60},{8,0},{12,4},{16,8},{20,12},{24,16},{28,20},{32,24},... | collective-permute-start | bytes 589832 | tf_op jit(solution)/shard_map/ppermute | solution.py:237
  16.9 7.0 %collective-permute-start.27 = (f32[2,48,512]{2,1,0:T(8,128)S(1)}, f32[2,48,512]{2,1,0:T(8,128)S(1)}, u32[]{:S(2)}, u32[]{:S(2)}) collective-permute-start(f32[2,48,512]{2,1,0:T(8,128)S(1)} %collective-permute-done.25.refs_1_), channel_id=1, source_target_pairs={{0,8},{4,12},{8,16},{12,20},{16,24},{20,28},{24,32},{28,36},{32,40... | collective-permute-start | bytes 589832 | tf_op jit(solution)/shard_map/ppermute | solution.py:237
  16.9 13.9 %copy-start = (s32[8]{0:T(128)S(1)}, s32[8]{0:T(128)}, u32[]{:S(2)}) copy-start(s32[8]{0:T(128)} %first.3) | copy-start | bytes 100
  18.9 5.8 %collective-permute-start.38 = (f32[2,192,128]{2,1,0:T(8,128)S(1)}, f32[2,192,128]{2,1,0:T(8,128)S(1)}, u32[]{:S(2)}, u32[]{:S(2)}) collective-permute-start(f32[2,192,128]{2,1,0:T(8,128)S(1)} %pack_w.2.refs_14_), channel_id=1, source_target_pairs={{0,64},{64,0},{128,192},{192,128},{1,65},{65,1},{129,193},{193,129... | collective-permute-start | bytes 589832 | tf_op jit(solution)/shard_map/ppermute | solution.py:247
  20.5 7.6 %collective-permute-start.30 = (f32[2,48,512]{2,1,0:T(8,128)S(1)}, f32[2,48,512]{2,1,0:T(8,128)S(1)}, u32[]{:S(2)}, u32[]{:S(2)}) collective-permute-start(f32[2,48,512]{2,1,0:T(8,128)S(1)} %collective-permute-done.28.refs_4_), channel_id=1, source_target_pairs={{0,56},{4,60},{8,0},{12,4},{16,8},{20,12},{24,16},{28,20},{32,24},... | collective-permute-start | bytes 589832 | tf_op jit(solution)/shard_map/ppermute | solution.py:237
  23.9 6.9 %collective-permute-start.29 = (f32[2,48,512]{2,1,0:T(8,128)S(1)}, f32[2,48,512]{2,1,0:T(8,128)S(1)}, u32[]{:S(2)}, u32[]{:S(2)}) collective-permute-start(f32[2,48,512]{2,1,0:T(8,128)S(1)} %collective-permute-done.27.refs_3_), channel_id=1, source_target_pairs={{0,8},{4,12},{8,16},{12,20},{16,24},{20,28},{24,32},{28,36},{32,40... | collective-permute-start | bytes 589832 | tf_op jit(solution)/shard_map/ppermute | solution.py:237
  24.7 10.2 %collective-permute-start.39 = (f32[2,2,192,128]{3,2,1,0:T(8,128)S(1)}, f32[2,2,192,128]{3,2,1,0:T(8,128)S(1)}, u32[]{:S(2)}, u32[]{:S(2)}) collective-permute-start(f32[2,2,192,128]{3,2,1,0:T(8,128)S(1)} %pad_maximum_fusion.1), channel_id=1, source_target_pairs={{0,192},{64,128},{128,64},{192,0},{1,193},{65,129},{129,65},{193,1... | collective-permute-start | bytes 1179656 | tf_op jit(solution)/shard_map/ppermute | solution.py:248
  27.5 3.3 %collective-permute-start.31 = (f32[2,48,512]{2,1,0:T(8,128)S(1)}, f32[2,48,512]{2,1,0:T(8,128)S(1)}, u32[]{:S(2)}, u32[]{:S(2)}) collective-permute-start(f32[2,48,512]{2,1,0:T(8,128)S(1)} %get-tuple-element.201.refs_0_), channel_id=1, source_target_pairs={{0,4},{4,0},{8,12},{12,8},{16,20},{20,16},{24,28},{28,24},{32,36},... | collective-permute-start | bytes 589832 | tf_op jit(solution)/shard_map/ppermute | solution.py:234
  27.5 3.9 %collective-permute-start.33 = (f32[2,48,512]{2,1,0:T(8,128)S(1)}, f32[2,48,512]{2,1,0:T(8,128)S(1)}, u32[]{:S(2)}, u32[]{:S(2)}) collective-permute-start(f32[2,48,512]{2,1,0:T(8,128)S(1)} %collective-permute-done.26.refs_2_), channel_id=1, source_target_pairs={{0,4},{4,0},{8,12},{12,8},{16,20},{20,16},{24,28},{28,24},{32,36},... | collective-permute-start | bytes 589832 | tf_op jit(solution)/shard_map/ppermute | solution.py:234
  28.1 4.4 %collective-permute-start.32 = (f32[2,48,512]{2,1,0:T(8,128)S(1)}, f32[2,48,512]{2,1,0:T(8,128)S(1)}, u32[]{:S(2)}, u32[]{:S(2)}) collective-permute-start(f32[2,48,512]{2,1,0:T(8,128)S(1)} %collective-permute-done.25.refs_1_), channel_id=1, source_target_pairs={{0,4},{4,0},{8,12},{12,8},{16,20},{20,16},{24,28},{28,24},{32,36},... | collective-permute-start | bytes 589832 | tf_op jit(solution)/shard_map/ppermute | solution.py:234
  30.8 4.0 %collective-permute-start.35 = (f32[2,48,512]{2,1,0:T(8,128)S(1)}, f32[2,48,512]{2,1,0:T(8,128)S(1)}, u32[]{:S(2)}, u32[]{:S(2)}) collective-permute-start(f32[2,48,512]{2,1,0:T(8,128)S(1)} %collective-permute-done.28.refs_4_), channel_id=1, source_target_pairs={{0,4},{4,0},{8,12},{12,8},{16,20},{20,16},{24,28},{28,24},{32,36},... | collective-permute-start | bytes 589832 | tf_op jit(solution)/shard_map/ppermute | solution.py:234
  30.9 7.5 %collective-permute-start.34 = (f32[2,48,512]{2,1,0:T(8,128)S(1)}, f32[2,48,512]{2,1,0:T(8,128)S(1)}, u32[]{:S(2)}, u32[]{:S(2)}) collective-permute-start(f32[2,48,512]{2,1,0:T(8,128)S(1)} %collective-permute-done.27.refs_3_), channel_id=1, source_target_pairs={{0,4},{4,0},{8,12},{12,8},{16,20},{20,16},{24,28},{28,24},{32,36},... | collective-permute-start | bytes 589832 | tf_op jit(solution)/shard_map/ppermute | solution.py:234
  31.5 4.8 %collective-permute-start.41 = (f32[1,48,512]{2,1,0:T(8,128)S(1)}, f32[1,48,512]{2,1,0:T(8,128)S(1)}, u32[]{:S(2)}, u32[]{:S(2)}) collective-permute-start(f32[1,48,512]{2,1,0:T(8,128)S(1)} %slice.31), channel_id=1, source_target_pairs={{0,56},{4,60},{8,0},{12,4},{16,8},{20,12},{24,16},{28,20},{32,24},... | collective-permute-start | bytes 294920 | tf_op jit(solution)/shard_map/ppermute | solution.py:237
  32.5 5.9 %collective-permute-start.40 = (f32[1,48,512]{2,1,0:T(8,128)S(1)}, f32[1,48,512]{2,1,0:T(8,128)S(1)}, u32[]{:S(2)}, u32[]{:S(2)}) collective-permute-start(f32[1,48,512]{2,1,0:T(8,128)S(1)} %slice.30), channel_id=1, source_target_pairs={{0,8},{4,12},{8,16},{12,20},{16,24},{20,28},{24,32},{28,36},{32,40... | collective-permute-start | bytes 294920 | tf_op jit(solution)/shard_map/ppermute | solution.py:237
  34.8 3.6 %collective-permute-start.37 = (f32[2,48,512]{2,1,0:T(8,128)S(1)}, f32[2,48,512]{2,1,0:T(8,128)S(1)}, u32[]{:S(2)}, u32[]{:S(2)}) collective-permute-start(f32[2,48,512]{2,1,0:T(8,128)S(1)} %collective-permute-done.30.refs_6_), channel_id=1, source_target_pairs={{0,4},{4,0},{8,12},{12,8},{16,20},{20,16},{24,28},{28,24},{32,36},... | collective-permute-start | bytes 589832 | tf_op jit(solution)/shard_map/ppermute | solution.py:234
  34.9 3.6 %collective-permute-start.36 = (f32[2,48,512]{2,1,0:T(8,128)S(1)}, f32[2,48,512]{2,1,0:T(8,128)S(1)}, u32[]{:S(2)}, u32[]{:S(2)}) collective-permute-start(f32[2,48,512]{2,1,0:T(8,128)S(1)} %collective-permute-done.29.refs_5_), channel_id=1, source_target_pairs={{0,4},{4,0},{8,12},{12,8},{16,20},{20,16},{24,28},{28,24},{32,36},... | collective-permute-start | bytes 589832 | tf_op jit(solution)/shard_map/ppermute | solution.py:234
  36.3 3.0 %collective-permute-start.43 = (f32[1,48,512]{2,1,0:T(8,128)S(1)}, f32[1,48,512]{2,1,0:T(8,128)S(1)}, u32[]{:S(2)}, u32[]{:S(2)}) collective-permute-start(f32[1,48,512]{2,1,0:T(8,128)S(1)} %collective-permute-done.41.refs_1_), channel_id=1, source_target_pairs={{0,4},{4,0},{8,12},{12,8},{16,20},{20,16},{24,28},{28,24},{32,36},... | collective-permute-start | bytes 294920 | tf_op jit(solution)/shard_map/ppermute | solution.py:234
  38.4 1.3 %collective-permute-start.42 = (f32[1,48,512]{2,1,0:T(8,128)S(1)}, f32[1,48,512]{2,1,0:T(8,128)S(1)}, u32[]{:S(2)}, u32[]{:S(2)}) collective-permute-start(f32[1,48,512]{2,1,0:T(8,128)S(1)} %collective-permute-done.40.refs_0_), channel_id=1, source_target_pairs={{0,4},{4,0},{8,12},{12,8},{16,20},{20,16},{24,28},{28,24},{32,36},... | collective-permute-start | bytes 294920 | tf_op jit(solution)/shard_map/ppermute | solution.py:234
  38.4 1.3 %copy-start.1 = (s32[16]{0:T(128)S(1)}, s32[16]{0:T(128)}, u32[]{:S(2)}) copy-start(s32[16]{0:T(128)} %target.5) | copy-start | bytes 196
  38.4 1.3 %copy-start.2 = (s32[8]{0:T(128)S(1)}, s32[8]{0:T(128)}, u32[]{:S(2)}) copy-start(s32[8]{0:T(128)} %second.5) | copy-start | bytes 100
  44.1 7.8 %collective-permute-start.44 = (f32[96,512]{1,0:T(8,128)S(1)}, f32[96,512]{1,0:T(8,128)S(1)}, u32[]{:S(2)}, u32[]{:S(2)}) collective-permute-start(f32[96,512]{1,0:T(8,128)S(1)} %get-tuple-element.205), channel_id=1, source_target_pairs={{0,1},{1,2},{2,3},{3,0},{4,5},{5,6},{6,7},{7,4},{8,9},{9,10},{10,1... | collective-permute-start | bytes 589832 | tf_op jit(solution)/shard_map/ppermute | solution.py:231
  44.3 8.5 %collective-permute-start.45 = (f32[96,512]{1,0:T(8,128)S(1)}, f32[96,512]{1,0:T(8,128)S(1)}, u32[]{:S(2)}, u32[]{:S(2)}) collective-permute-start(f32[96,512]{1,0:T(8,128)S(1)} %get-tuple-element.206), channel_id=1, source_target_pairs={{0,3},{1,0},{2,1},{3,2},{4,7},{5,4},{6,5},{7,6},{8,11},{9,8},{10,9... | collective-permute-start | bytes 589832 | tf_op jit(solution)/shard_map/ppermute | solution.py:231
  46.9 12.2 %collective-permute-start.47 = (f32[96,512]{1,0:T(8,128)}, f32[96,512]{1,0:T(8,128)}, u32[]{:S(2)}, u32[]{:S(2)}) collective-permute-start(f32[96,512]{1,0:T(8,128)} %get-tuple-element.208), channel_id=1, source_target_pairs={{0,1},{1,2},{2,3},{3,0},{4,5},{5,6},{6,7},{7,4},{8,9},{9,10},{10,1... | collective-permute-start | bytes 589832 | tf_op jit(solution)/shard_map/ppermute | solution.py:231
  48.3 10.7 %collective-permute-start.48 = (f32[96,512]{1,0:T(8,128)}, f32[96,512]{1,0:T(8,128)}, u32[]{:S(2)}, u32[]{:S(2)}) collective-permute-start(f32[96,512]{1,0:T(8,128)} %get-tuple-element.209), channel_id=1, source_target_pairs={{0,3},{1,0},{2,1},{3,2},{4,7},{5,4},{6,5},{7,6},{8,11},{9,8},{10,9... | collective-permute-start | bytes 589832 | tf_op jit(solution)/shard_map/ppermute | solution.py:231
  54.2 6.0 %collective-permute-start.46 = (f32[96,512]{1,0:T(8,128)}, f32[96,512]{1,0:T(8,128)}, u32[]{:S(2)}, u32[]{:S(2)}) collective-permute-start(f32[96,512]{1,0:T(8,128)} %get-tuple-element.207), channel_id=1, source_target_pairs={{0,1},{1,2},{2,3},{3,0},{4,5},{5,6},{6,7},{7,4},{8,9},{9,10},{10,1... | collective-permute-start | bytes 589832 | tf_op jit(solution)/shard_map/ppermute | solution.py:231
  55.0 7.2 %collective-permute-start.49 = (f32[96,512]{1,0:T(8,128)}, f32[96,512]{1,0:T(8,128)}, u32[]{:S(2)}, u32[]{:S(2)}) collective-permute-start(f32[96,512]{1,0:T(8,128)} %get-tuple-element.210), channel_id=1, source_target_pairs={{0,3},{1,0},{2,1},{3,2},{4,7},{5,4},{6,5},{7,6},{8,11},{9,8},{10,9... | collective-permute-start | bytes 589832 | tf_op jit(solution)/shard_map/ppermute | solution.py:231

commit v6 on v5

--- a/solution.py
+++ b/solution.py
@@ -81,7 +81,25 @@
             out_ref[k, :, lanes] = packed[at : at + c_local] + packed[at + c_local : at + 2 * c_local]
 
 
-def pack_w_kernel(pos, starts, second, target, w_ref, out_ref):
+def count_passes(starts, first, a_local, n_lanes, n_passes):
+    lane = lax.broadcasted_iota(I32, (8, 128), 1)
+    s, base = lane % 8, lane // 8 * a_local
+    count = [
+        jnp.maximum(jnp.minimum(starts[n + 1], base + a_local) - jnp.maximum(starts[n], base), 0) for n in range(8)
+    ]
+    places = jnp.zeros((8, 128), I32)
+    for n in range(first.shape[0]):
+        places = places + choose(s ^ first[n], count)
+    most = jnp.max(jnp.where(lane < 32, places, 0).astype(F32)).astype(I32)
+    widest = starts[1] - starts[0] // 8 * 8
+    for n in range(1, 8):
+        widest = jnp.maximum(widest, starts[n + 1] - starts[n] // 8 * 8)
+    n_lanes[0] = (most + LANES - 1) // LANES
+    n_passes[0] = (most + LANES - 1) // LANES * ((widest + BLOCK - 1) // BLOCK)
+
+
+def pack_w_kernel(a_local, pos, starts, first, second, target, w_ref, out_ref, *limits):
+    count_passes(starts, first, a_local, *limits)
     k_local, c_local, _ = out_ref.shape
     rows = k_local * c_local
     tiles = w_ref.shape[0] // rows
@@ -118,9 +136,10 @@
 
 
 def place_kernel(where, pos, *refs):
-    pieces, (own, pair, far), (t_all, w_all) = refs[: len(where)], refs[len(where) : -2], refs[-2:]
+    pieces, (own, pair, far), (t_all, w_all, total) = refs[: len(where)], refs[len(where) : -3], refs[-3:]
     for place, piece in zip(where, pieces):
         put_window(pos, place, piece, t_all)
+    total[...] = jnp.zeros_like(total)
     size = own.shape[1]
     r = pos[0]
     for row, piece in ((r, own), (r ^ 1, pair), (3 - r, far.at[0]), ((3 - r) ^ 1, far.at[1])):
@@ -134,12 +153,11 @@
     return total[pl.ds(pl.multiple_of(at, 8), b_local // 2), :]
 
 
-def product_kernel(where, pos, starts, second, target, given, w_all, *refs):
+def product_kernel(where, pos, starts, second, target, given, zeros, w_all, *refs):
     pieces, (t_all, total, up, down, one, three) = refs[: len(where)], refs[len(where) :]
     k_local, c_all, _ = t_all.shape
     for (k, place), piece in zip(where, pieces):
         put_window(pos, place, piece, t_all, k)
-    total[...] = jnp.zeros_like(total)
     row = lax.broadcasted_iota(I32, (128, 1), 0)
 
     def one_irrep(irrep, _):
@@ -178,7 +196,7 @@
 
 def expand_kernel(pos, starts, first, target, g_ref, *refs):
     total, one_0, one_1, three_0, three_1 = refs[:5]
-    out_ref = refs[-1]
+    out_ref, buffer, sems = refs[-3:]
     b_local = out_ref.shape[1]
     x_local, oi, width = out_ref.shape[2], first.shape[0], 256
     upper = rows_for(pos, total, 0, 0) + one_0[...] + three_0[...]
@@ -194,10 +212,15 @@
         s = label_of(a, starts) ^ choose(x % oi, [first[i] for i in range(oi)])
         both = jnp.dot(sums, g_ref[:, lanes], preferred_element_type=F32)
         value = jnp.where(wanted == s, both[:b_local] + both[b_local:], 0.0)
-        out_ref[0, :, lanes] = value + refs[5][0, :, lanes] if len(refs) > 6 else value
+        buffer[:, lanes] = value + refs[5][0, :, lanes] if len(refs) > 8 else value
+        pltpu.make_async_copy(buffer.at[:, lanes], out_ref.at[0, :, lanes], sems.at[n]).start()
         return 0
 
-    lax.fori_loop(0, x_local // width, tile, 0)
+    tiles = x_local // width
+    lax.fori_loop(0, tiles, tile, 0)
+    for n in range(tiles):
+        lanes = pl.ds(n * width, width)
+        pltpu.make_async_copy(buffer.at[:, lanes], out_ref.at[0, :, lanes], sems.at[n]).wait()
 
 
 def params(mib=16):
@@ -217,15 +240,15 @@
         compiler_params=params(),
         name="pack_t",
     )(pos, starts, first, second, amplitudes)
-    w0 = pl.pallas_call(
-        pack_w_kernel,
-        out_shape=shape((k_local, w_rows, BLOCK), F32),
-        in_specs=[SMEM] * 4 + [VMEM],
-        out_specs=VMEM,
+    w0, *limits = pl.pallas_call(
+        functools.partial(pack_w_kernel, x_local // first.shape[0]),
+        out_shape=(shape((k_local, w_rows, BLOCK), F32), shape((1,), I32), shape((1,), I32)),
+        in_specs=[SMEM] * 5 + [VMEM],
+        out_specs=(VMEM, SMEM, SMEM),
         compiler_params=params(),
         cost_estimate=pl.CostEstimate(flops=10**9, bytes_accessed=4 * 10**6, transcendentals=0),
         name="pack_w",
-    )(pos, starts, second, target, integrals)
+    )(pos, starts, first, second, target, integrals)
 
     def along(x, axis, step):
         return lax.ppermute(x, axis, [(i, (i + step) % 4) for i in range(4)])
@@ -246,11 +269,11 @@
         got[far, True] = swap(piece)
     pair = lax.ppermute(w0, "row", [(i, i ^ 1) for i in range(4)])
     far = lax.ppermute(jnp.stack([w0, pair]), "row", [(i, 3 - i) for i in range(4)])
-    t_all, w_all = pl.pallas_call(
+    t_all, w_all, total = pl.pallas_call(
         functools.partial(place_kernel, list(got)),
-        out_shape=(shape((k_local, v, LANES), F32), shape((k_local, v, BLOCK), F32)),
+        out_shape=(shape((k_local, v, LANES), F32), shape((k_local, v, BLOCK), F32), shape((v + BLOCK, LANES), F32)),
         in_specs=[SMEM] + [VMEM] * (len(got) + 3),
-        out_specs=(VMEM,) * 2,
+        out_specs=(VMEM,) * 3,
         compiler_params=params(),
         cost_estimate=pl.CostEstimate(flops=0, bytes_accessed=7 * 10**6, transcendentals=0),
         name="place",
@@ -260,13 +283,13 @@
     part = shape((b_local // 2, LANES), F32)
     _, total, up, down, one_1, three_0 = pl.pallas_call(
         functools.partial(product_kernel, where),
-        out_shape=(shape(t_all.shape, F32), shape((v + BLOCK, LANES), F32)) + (part,) * 4,
-        in_specs=[SMEM] * 4 + [VMEM] * 6,
+        out_shape=(shape(t_all.shape, F32), shape(total.shape, F32)) + (part,) * 4,
+        in_specs=[SMEM] * 4 + [VMEM] * 7,
         out_specs=(VMEM,) * 6,
-        input_output_aliases={4: 0},
+        input_output_aliases={4: 0, 5: 1},
         compiler_params=params(),
         name="product",
-    )(pos, starts, second, target, t_all, w_all, *late)
+    )(pos, starts, second, target, t_all, total, w_all, *late)
     up, down = along(up, "depth", 1), along(down, "depth", -1)
     one_1, three_0 = along(one_1, "depth", 1), along(three_0, "depth", -1)
     one_0, three_1 = pl.pallas_call(
@@ -280,19 +303,19 @@
     one_0, three_1 = along(one_0, "depth", 1), along(three_1, "depth", -1)
     sums = [total, one_0, one_1, three_0, three_1]
     more = [] if before is None else [before]
-    return pl.pallas_call(
+    out = pl.pallas_call(
         expand_kernel,
         out_shape=shape((1, b_local, x_local), F32),
         in_specs=[SMEM] * 4 + [VMEM] * (6 + len(more)),
-        out_specs=VMEM,
+        out_specs=ANY,
+        scratch_shapes=[pltpu.VMEM((b_local, x_local), F32), pltpu.SemaphoreType.DMA((x_local // 256,))],
         compiler_params=params(),
         name="expand",
     )(pos, starts, first, target, hot, *sums, *more)
+    return out, limits
 
 
 def per_device(amplitudes, integrals, irrep_virtual, irrep_first, irrep_second, irrep_target):
-    v = irrep_virtual.shape[0]
-    a_local = amplitudes.shape[2] // irrep_first.shape[0]
     starts = jnp.sum((irrep_virtual[None, :] < jnp.arange(16, dtype=I32)[:, None]).astype(I32), axis=1)
     where = [lax.axis_index(n).astype(I32) for n in ("row", "col", "depth")]
 
@@ -306,15 +329,9 @@
         labels = (starts, irrep_first, irrep_second, irrep_target)
         return one_pass(position(n_lane, n_block), *labels, amplitudes, flat, w_rows, before)
 
-    out = run(jnp.int32(0), jnp.int32(0), None)
-    edges = jnp.arange(0, v, a_local, dtype=I32)
-    low, high = starts[:8], starts[1:9]
-    count = jnp.maximum(jnp.minimum(high, edges[:, None] + a_local) - jnp.maximum(low, edges[:, None]), 0)
-    same = (jnp.arange(8)[:, None, None] ^ irrep_first[None, None, :]) == jnp.arange(8)[None, :, None]
-    most = jnp.max(jnp.sum(count[:, None, :, None] * same[None].astype(I32), axis=(2, 3)))
-    n_lanes = (most + LANES - 1) // LANES
-    n_blocks = (jnp.max(high - low // 8 * 8) + BLOCK - 1) // BLOCK
-    return lax.fori_loop(1, n_lanes * n_blocks, lambda n, acc: run(n % n_lanes, n // n_lanes, acc), out)
+    out, limits = run(jnp.int32(0), jnp.int32(0), None)
+    n_lanes, n_passes = (limit.reshape(()) for limit in limits)
+    return lax.fori_loop(1, n_passes, lambda n, acc: run(n % n_lanes, n // n_lanes, acc)[0], out)
 
 
 def solution(mesh):

time: 66.4 us -> 69.9 us (1.053)
  waiting for transfers between devices: 19.5 us -> 23.4 us
  other arithmetic: 3.13 us -> 0.83 us
  loops' own time: 0.01 us -> 0.79 us
  between operations: 1.49 us -> 2.24 us
    ppermute x8, waiting for transfers between devices: 9.9 us -> 14.1 us  [ring(): return lax.ppermute(x, 'col', [(i, (i + 2 * step) % 16) for i in range(16)])]
    ppermute x6, waiting for transfers between devices: 7.04 us -> 8.75 us  [along(): return lax.ppermute(x, axis, [(i, (i + step) % 4) for i in range(4)])]
    reduce_max x2 -> x0, other arithmetic: 1.48 us -> none  [the longest x1 0.77 us: per_device(): n_blocks = (jnp.max(high - low // 8 * 8) + BLOCK - 1) // BLOCK]
    ppermute x1, waiting for transfers between devices: 1.36 us -> 0.01 us  [one_pass(): lax.ppermute(jnp.stack([w0, pair]), 'row', [(i, 3 - i) for i in range(4)])]
    another operation x1, loops' own time: 0.01 us -> 0.79 us  [per_device(): lax.fori_loop(1, n_passes, lambda n, acc: run(n % n_lanes, n // n_lanes,...]
    reduce_sum x1 -> x0, other arithmetic: 0.73 us -> none  [per_device(): jnp.sum(count[:, None, :, None] * same[None].astype(I32), axis=(2, 3))]
    ppermute x1, waiting for transfers between devices: 0.73 us -> 0.01 us  [one_pass(): pair = lax.ppermute(w0, 'row', [(i, i ^ 1) for i in range(4)])]
  transfers between devices with their start and end apart: 25 -> 25, of which waited for: 11 -> 11; matrix products, arithmetic and copies ran while one was open for 4% -> 0% of each run, Pallas kernels for 6% -> 7%
where the time goes in v6:
time: 69.9 us; the launch traced here: 69.7 us
  starting transfers between devices  27.3 us (39%)
  waiting for transfers between devices  23.4 us (33%)
  Pallas kernels  15 us (21%)
  between operations  2.24 us (3%)
  other arithmetic  0.83 us (1%)
  loops' own time  0.79 us (1%)
    ppermute x8, starting transfers between devices, ring(): return lax.ppermute(x, 'col', [(i, (i + 2 * step) % 16) for i in range(16)])  15.1 us
    ppermute x8, waiting for transfers between devices, ring(): return lax.ppermute(x, 'col', [(i, (i + 2 * step) % 16) for i in range(16)])  14.1 us
    ppermute x6, waiting for transfers between devices, along(): return lax.ppermute(x, axis, [(i, (i + step) % 4) for i in range(4)])  8.75 us
    ppermute x6, starting transfers between devices, along(): return lax.ppermute(x, axis, [(i, (i + step) % 4) for i in range(4)])  6.08 us
    pallas_call x1, Pallas kernels, one_pass(): pl.pallas_call(functools.partial(product_kernel, where), out_shape=(shape...  4.31 us
    pallas_call x1, Pallas kernels, one_pass(): pl.pallas_call(expand_kernel, out_shape=shape((1, b_local, x_local), F32)...  3.72 us
    ppermute x1, starting transfers between devices, one_pass(): lax.ppermute(jnp.stack([w0, pair]), 'row', [(i, 3 - i) for i in range(4)])  2.86 us
    pallas_call x1, Pallas kernels, one_pass(): pl.pallas_call(functools.partial(pack_w_kernel, x_local // first.shape[0]...  2.47 us
  transfers between devices with their start and end apart: 25, of which 11 were waited for; matrix products, arithmetic and copies ran while one was open for 0% of the time, Pallas kernels for 7%

profile of v6, /device:TPU:24, one launch (start us, length us, event | category | flops | bytes accessed | tf_op | source)
XLA Modules:
  0.0 69.7 jit_solution(7253368808922744629)
XLA Ops:
  0.0 0.8 %convert_reduce_fusion.starts = s32[16]{0:T(128)S(1)} fusion(s32[768]{0:T(1024)} %param.10), kind=kLoop, calls=%fused_computation.2 | loop fusion | flops 36848 | bytes 3136 | tf_op jit(solution)/shard_map/reduce_sum | solution.py:319
  0.8 0.1 stack.75.pos
  0.9 2.2 %pack_t.5 = (f32[2,48,512]{2,1,0:T(8,128)S(1)}, bf16[512,1536]{1,0:T(8,128)(2,1)S(1)}) custom-call(s32[8]{0:T(128)S(1)} %stack.75.pos, s32[16]{0:T(128)S(1)} %convert_reduce_fusion.starts, s32[8]{0:T(128)} %first.5, s32[8]{0:T(128)} %second.5, f32[2,48,1536]{2,1,0:T(8,128)} %t_ref.1), custom_call_target="tpu_custom_call" | custom-call | tf_op jit(solution)/shard_map/pack_t/pallas_call | solution.py:235
  3.2 5.9 %collective-permute-start.26 = (f32[2,48,512]{2,1,0:T(8,128)S(1)}, f32[2,48,512]{2,1,0:T(8,128)S(1)}, u32[]{:S(2)}, u32[]{:S(2)}) collective-permute-start(f32[2,48,512]{2,1,0:T(8,128)S(1)} %get-tuple-element.207.refs_0_), channel_id=1, source_target_pairs={{0,56},{4,60},{8,0},{12,4},{16,8},{20,12},{24,16},{28,20},{32,24},... | collective-permute-start | bytes 589832 | tf_op jit(solution)/shard_map/ppermute | solution.py:260
  9.1 0.0 collective-permute-start.25
  9.1 2.5 %pack_w.5 = (f32[2,192,128]{2,1,0:T(8,128)S(1)}, s32[1]{0:T(128)}, s32[1]{0:T(128)}) custom-call(s32[8]{0:T(128)S(1)} %stack.75.pos, s32[16]{0:T(128)S(1)} %convert_reduce_fusion.starts, s32[8]{0:T(128)} %first.5, s32[8]{0:T(128)} %second.5, s32[16]{0:T(128)} %target.5, f32[2304,128]{1,0:T(8,128)} %bitcast.33), custom_call_target="tpu_custom_call" | custom-call | flops 1000000000 | bytes 4000000 | tf_op jit(solution)/shard_map/pack_w/pallas_call | solution.py:243
  11.6 1.7 %collective-permute-done.26.refs_2_ = f32[2,48,512]{2,1,0:T(8,128)S(1)} collective-permute-done((f32[2,48,512]{2,1,0:T(8,128)S(1)}, f32[2,48,512]{2,1,0:T(8,128)S(1)}, u32[]{:S(2)}, u32[]{:S(2)}) %collective-permute-start.26) | collective-permute-done | bytes 196640 | tf_op jit(solution)/shard_map/ppermute | solution.py:260
  13.2 3.7 %collective-permute-start.28 = (f32[2,48,512]{2,1,0:T(8,128)S(1)}, f32[2,48,512]{2,1,0:T(8,128)S(1)}, u32[]{:S(2)}, u32[]{:S(2)}) collective-permute-start(f32[2,48,512]{2,1,0:T(8,128)S(1)} %collective-permute-done.26.refs_2_), channel_id=1, source_target_pairs={{0,56},{4,60},{8,0},{12,4},{16,8},{20,12},{24,16},{28,20},{32,24},... | collective-permute-start | bytes 589832 | tf_op jit(solution)/shard_map/ppermute | solution.py:260
  16.9 1.5 %collective-permute-start.38 = (f32[2,192,128]{2,1,0:T(8,128)S(1)}, f32[2,192,128]{2,1,0:T(8,128)S(1)}, u32[]{:S(2)}, u32[]{:S(2)}) collective-permute-start(f32[2,192,128]{2,1,0:T(8,128)S(1)} %get-tuple-element.208.refs_14_), channel_id=1, source_target_pairs={{0,64},{64,0},{128,192},{192,128},{1,65},{65,1},{129,193},{193,129... | collective-permute-start | bytes 589832 | tf_op jit(solution)/shard_map/ppermute | solution.py:270
  18.4 0.0 collective-permute-start.27
  18.4 1.8 %collective-permute-done.28.refs_4_ = f32[2,48,512]{2,1,0:T(8,128)S(1)} collective-permute-done((f32[2,48,512]{2,1,0:T(8,128)S(1)}, f32[2,48,512]{2,1,0:T(8,128)S(1)}, u32[]{:S(2)}, u32[]{:S(2)}) %collective-permute-start.28) | collective-permute-done | bytes 196640 | tf_op jit(solution)/shard_map/ppermute | solution.py:260
  20.2 3.7 %collective-permute-start.30 = (f32[2,48,512]{2,1,0:T(8,128)S(1)}, f32[2,48,512]{2,1,0:T(8,128)S(1)}, u32[]{:S(2)}, u32[]{:S(2)}) collective-permute-start(f32[2,48,512]{2,1,0:T(8,128)S(1)} %collective-permute-done.28.refs_4_), channel_id=1, source_target_pairs={{0,56},{4,60},{8,0},{12,4},{16,8},{20,12},{24,16},{28,20},{32,24},... | collective-permute-start | bytes 589832 | tf_op jit(solution)/shard_map/ppermute | solution.py:260
  23.9 0.0 collective-permute-done.38.refs_15_
  24.0 2.9 %collective-permute-start.39 = (f32[2,2,192,128]{3,2,1,0:T(8,128)S(1)}, f32[2,2,192,128]{3,2,1,0:T(8,128)S(1)}, u32[]{:S(2)}, u32[]{:S(2)}) collective-permute-start(f32[2,2,192,128]{3,2,1,0:T(8,128)S(1)} %pad_maximum_fusion.1), channel_id=1, source_target_pairs={{0,192},{64,128},{128,64},{192,0},{1,193},{65,129},{129,65},{193,1... | collective-permute-start | bytes 1179656 | tf_op jit(solution)/shard_map/ppermute | solution.py:271
  26.8 0.0 collective-permute-start.29
  26.8 0.0 collective-permute-start.31
  26.8 0.5 collective-permute-start.33
  27.3 0.1 collective-permute-start.32
  27.4 6.3 %collective-permute-done.29.refs_5_ = f32[2,48,512]{2,1,0:T(8,128)S(1)} collective-permute-done((f32[2,48,512]{2,1,0:T(8,128)S(1)}, f32[2,48,512]{2,1,0:T(8,128)S(1)}, u32[]{:S(2)}, u32[]{:S(2)}) %collective-permute-start.29) | collective-permute-done | bytes 196640 | tf_op jit(solution)/shard_map/ppermute | solution.py:260
  33.7 0.0 collective-permute-start.35
  33.7 0.0 copy-start.1
  33.7 0.0 copy-start.2
  33.8 0.0 collective-permute-done.31.refs_7_
  33.8 0.6 collective-permute-start.34
  34.4 0.0 collective-permute-done.32.refs_8_
  34.4 0.2 collective-permute-start.37
  34.6 0.0 collective-permute-done.39.refs_16_
  34.6 0.4 collective-permute-start.36
  35.0 0.2 collective-permute-done.35.refs_11_
  35.1 1.8 %collective-permute-start.40 = (f32[1,48,512]{2,1,0:T(8,128)S(1)}, f32[1,48,512]{2,1,0:T(8,128)S(1)}, u32[]{:S(2)}, u32[]{:S(2)}) collective-permute-start(f32[1,48,512]{2,1,0:T(8,128)S(1)} %slice.22), channel_id=1, source_target_pairs={{0,8},{4,12},{8,16},{12,20},{16,24},{20,28},{24,32},{28,36},{32,40... | collective-permute-start | bytes 294920 | tf_op jit(solution)/shard_map/ppermute | solution.py:260
  36.9 2.2 %collective-permute-done.41.refs_1_ = f32[1,48,512]{2,1,0:T(8,128)S(1)} collective-permute-done((f32[1,48,512]{2,1,0:T(8,128)S(1)}, f32[1,48,512]{2,1,0:T(8,128)S(1)}, u32[]{:S(2)}, u32[]{:S(2)}) %collective-permute-start.41) | collective-permute-done | bytes 98336 | tf_op jit(solution)/shard_map/ppermute | solution.py:260
  39.2 2.1 %collective-permute-done.40.refs_0_ = f32[1,48,512]{2,1,0:T(8,128)S(1)} collective-permute-done((f32[1,48,512]{2,1,0:T(8,128)S(1)}, f32[1,48,512]{2,1,0:T(8,128)S(1)}, u32[]{:S(2)}, u32[]{:S(2)}) %collective-permute-start.40) | collective-permute-done | bytes 98336 | tf_op jit(solution)/shard_map/ppermute | solution.py:260
  41.3 0.9 %place.5 = (f32[2,768,512]{2,1,0:T(8,128)S(1)}, f32[2,768,128]{2,1,0:T(8,128)S(1)}, f32[896,512]{1,0:T(8,128)S(1)}) custom-call(s32[8]{0:T(128)S(1)} %stack.75.pos, f32[2,48,512]{2,1,0:T(8,128)S(1)} %get-tuple-element.207.refs_0_, f32[2,48,512]{2,1,0:T(8,128)S(1)} %collective-permute-done.25.refs_1_, f32[2,48,512]{2,1,0:T(8,128)S(1)} %collective-permute-done.26.refs_2_, ...), custom_call_target="tpu_custom_call" | custom-call | bytes 7000000 | tf_op jit(solution)/shard_map/place/pallas_call | solution.py:272
  42.2 0.3 collective-permute-done.42.refs_2_
  42.6 4.3 %product.5 = (f32[2,768,512]{2,1,0:T(8,128)S(1)}, f32[896,512]{1,0:T(8,128)S(1)}, f32[96,512]{1,0:T(8,128)S(1)}, f32[96,512]{1,0:T(8,128)S(1)}, f32[96,512]{1,0:T(8,128)}, /*index=5*/f32[96,512]{1,0:T(8,128)}) custom-call(s32[8]{0:T(128)S(1)} %stack.75.pos, s32[16]{0:T(128)S(1)} %convert_reduce_fusion.starts, ...), custom_call_target="tpu_custom_call", output_to_operand_aliasing={{0}: (4, {}), {1}: (5, {})} | custom-call | tf_op jit(solution)/shard_map/product/pallas_call | solution.py:284
  46.9 0.2 collective-permute-start.44
  47.1 1.8 %collective-permute-start.45 = (f32[96,512]{1,0:T(8,128)S(1)}, f32[96,512]{1,0:T(8,128)S(1)}, u32[]{:S(2)}, u32[]{:S(2)}) collective-permute-start(f32[96,512]{1,0:T(8,128)S(1)} %get-tuple-element.214), channel_id=1, source_target_pairs={{0,3},{1,0},{2,1},{3,2},{4,7},{5,4},{6,5},{7,6},{8,11},{9,8},{10,9... | collective-permute-start | bytes 589832 | tf_op jit(solution)/shard_map/ppermute | solution.py:254
  48.9 1.4 %collective-permute-start.47 = (f32[96,512]{1,0:T(8,128)}, f32[96,512]{1,0:T(8,128)}, u32[]{:S(2)}, u32[]{:S(2)}) collective-permute-start(f32[96,512]{1,0:T(8,128)} %get-tuple-element.216), channel_id=1, source_target_pairs={{0,1},{1,2},{2,3},{3,0},{4,5},{5,6},{6,7},{7,4},{8,9},{9,10},{10,1... | collective-permute-start | bytes 589832 | tf_op jit(solution)/shard_map/ppermute | solution.py:254
  50.3 0.6 collective-permute-start.48
  50.9 3.7 %collective-permute-done.44.relay_up = f32[96,512]{1,0:T(8,128)S(1)} collective-permute-done((f32[96,512]{1,0:T(8,128)S(1)}, f32[96,512]{1,0:T(8,128)S(1)}, u32[]{:S(2)}, u32[]{:S(2)}) %collective-permute-start.44) | collective-permute-done | bytes 196640 | tf_op jit(solution)/shard_map/ppermute | solution.py:254
  54.6 1.4 %collective-permute-done.45.relay_down = f32[96,512]{1,0:T(8,128)S(1)} collective-permute-done((f32[96,512]{1,0:T(8,128)S(1)}, f32[96,512]{1,0:T(8,128)S(1)}, u32[]{:S(2)}, u32[]{:S(2)}) %collective-permute-start.45) | collective-permute-done | bytes 196640 | tf_op jit(solution)/shard_map/ppermute | solution.py:254
  56.1 1.4 %join.5 = (f32[96,512]{1,0:T(8,128)}, f32[96,512]{1,0:T(8,128)}) custom-call(s32[8]{0:T(128)S(1)} %stack.75.pos, f32[896,512]{1,0:T(8,128)S(1)} %get-tuple-element.212.total.refs_0_, f32[96,512]{1,0:T(8,128)S(1)} %collective-permute-done.44.relay_up, f32[96,512]{1,0:T(8,128)S(1)} %collective-permute-done.45.relay_down), custom_call_target="tpu_custom_call" | custom-call | tf_op jit(solution)/shard_map/join/pallas_call | solution.py:295
  57.5 0.3 collective-permute-start.46
  57.8 1.7 %collective-permute-start.49 = (f32[96,512]{1,0:T(8,128)}, f32[96,512]{1,0:T(8,128)}, u32[]{:S(2)}, u32[]{:S(2)}) collective-permute-start(f32[96,512]{1,0:T(8,128)} %get-tuple-element.218), channel_id=1, source_target_pairs={{0,3},{1,0},{2,1},{3,2},{4,7},{5,4},{6,5},{7,6},{8,11},{9,8},{10,9... | collective-permute-start | bytes 589832 | tf_op jit(solution)/shard_map/ppermute | solution.py:254
  61.4 2.0 %collective-permute-done.46.refs_1_ = f32[96,512]{1,0:T(8,128)} collective-permute-done((f32[96,512]{1,0:T(8,128)}, f32[96,512]{1,0:T(8,128)}, u32[]{:S(2)}, u32[]{:S(2)}) %collective-permute-start.46) | collective-permute-done | bytes 196640 | tf_op jit(solution)/shard_map/ppermute | solution.py:254
  63.5 1.6 %collective-permute-done.49.refs_4_ = f32[96,512]{1,0:T(8,128)} collective-permute-done((f32[96,512]{1,0:T(8,128)}, f32[96,512]{1,0:T(8,128)}, u32[]{:S(2)}, u32[]{:S(2)}) %collective-permute-start.49) | collective-permute-done | bytes 196640 | tf_op jit(solution)/shard_map/ppermute | solution.py:254
  65.0 3.7 %expand.5 = f32[1,192,1536]{2,1,0:T(8,128)} custom-call(s32[8]{0:T(128)S(1)} %stack.75.pos, s32[16]{0:T(128)S(1)} %convert_reduce_fusion.starts, s32[8]{0:T(128)S(1)} %copy-done, s32[16]{0:T(128)S(1)} %copy-done.1, bf16[512,1536]{1,0:T(8,128)(2,1)S(1)} %get-tuple-element.206.g_ref, f32[896,512]{1,0:T(8,128)S(1)} %get-tuple-element.212.total.refs_0_, ...), custom_call_target="tpu_custom_call" | custom-call | tf_op jit(solution)/shard_map/expand/pallas_call | solution.py:306
  68.7 0.8 %while.12 = (s32[]{:T(128)}, f32[1,192,1536]{2,1,0:T(8,128)}, s32[]{:T(128)}, s32[]{:T(128)}, s32[]{:T(128)}, /*index=5*/s32[]{:T(128)}, s32[]{:T(128)}, pred[]{...) while((s32[]{:T(128)}, f32[1,192,1536]{2,1,0:T(8,128)}, ...), condition=%wide.region_2.3_spmd, body=%wide.region_1.2_spmd.sunk | while | flops 1000098304 | bytes 33414708 | solution.py:334
  (21 shorter events, 0.1 us)
Async XLA Ops:
  3.2 10.1 %collective-permute-start.26 = (f32[2,48,512]{2,1,0:T(8,128)S(1)}, f32[2,48,512]{2,1,0:T(8,128)S(1)}, u32[]{:S(2)}, u32[]{:S(2)}) collective-permute-start(f32[2,48,512]{2,1,0:T(8,128)S(1)} %get-tuple-element.207.refs_0_), channel_id=1, source_target_pairs={{0,56},{4,60},{8,0},{12,4},{16,8},{20,12},{24,16},{28,20},{32,24},... | collective-permute-start | bytes 589832 | tf_op jit(solution)/shard_map/ppermute | solution.py:260
  9.1 9.3 %collective-permute-start.25 = (f32[2,48,512]{2,1,0:T(8,128)S(1)}, f32[2,48,512]{2,1,0:T(8,128)S(1)}, u32[]{:S(2)}, u32[]{:S(2)}) collective-permute-start(f32[2,48,512]{2,1,0:T(8,128)S(1)} %get-tuple-element.207.refs_0_), channel_id=1, source_target_pairs={{0,8},{4,12},{8,16},{12,20},{16,24},{20,28},{24,32},{28,36},{32,40... | collective-permute-start | bytes 589832 | tf_op jit(solution)/shard_map/ppermute | solution.py:260
  13.2 7.0 %collective-permute-start.28 = (f32[2,48,512]{2,1,0:T(8,128)S(1)}, f32[2,48,512]{2,1,0:T(8,128)S(1)}, u32[]{:S(2)}, u32[]{:S(2)}) collective-permute-start(f32[2,48,512]{2,1,0:T(8,128)S(1)} %collective-permute-done.26.refs_2_), channel_id=1, source_target_pairs={{0,56},{4,60},{8,0},{12,4},{16,8},{20,12},{24,16},{28,20},{32,24},... | collective-permute-start | bytes 589832 | tf_op jit(solution)/shard_map/ppermute | solution.py:260
  16.9 7.0 %collective-permute-start.38 = (f32[2,192,128]{2,1,0:T(8,128)S(1)}, f32[2,192,128]{2,1,0:T(8,128)S(1)}, u32[]{:S(2)}, u32[]{:S(2)}) collective-permute-start(f32[2,192,128]{2,1,0:T(8,128)S(1)} %get-tuple-element.208.refs_14_), channel_id=1, source_target_pairs={{0,64},{64,0},{128,192},{192,128},{1,65},{65,1},{129,193},{193,129... | collective-permute-start | bytes 589832 | tf_op jit(solution)/shard_map/ppermute | solution.py:270
  18.4 8.4 %collective-permute-start.27 = (f32[2,48,512]{2,1,0:T(8,128)S(1)}, f32[2,48,512]{2,1,0:T(8,128)S(1)}, u32[]{:S(2)}, u32[]{:S(2)}) collective-permute-start(f32[2,48,512]{2,1,0:T(8,128)S(1)} %collective-permute-done.25.refs_1_), channel_id=1, source_target_pairs={{0,8},{4,12},{8,16},{12,20},{16,24},{20,28},{24,32},{28,36},{32,40... | collective-permute-start | bytes 589832 | tf_op jit(solution)/shard_map/ppermute | solution.py:260
  20.2 7.1 %collective-permute-start.30 = (f32[2,48,512]{2,1,0:T(8,128)S(1)}, f32[2,48,512]{2,1,0:T(8,128)S(1)}, u32[]{:S(2)}, u32[]{:S(2)}) collective-permute-start(f32[2,48,512]{2,1,0:T(8,128)S(1)} %collective-permute-done.28.refs_4_), channel_id=1, source_target_pairs={{0,56},{4,60},{8,0},{12,4},{16,8},{20,12},{24,16},{28,20},{32,24},... | collective-permute-start | bytes 589832 | tf_op jit(solution)/shard_map/ppermute | solution.py:260
  24.0 10.6 %collective-permute-start.39 = (f32[2,2,192,128]{3,2,1,0:T(8,128)S(1)}, f32[2,2,192,128]{3,2,1,0:T(8,128)S(1)}, u32[]{:S(2)}, u32[]{:S(2)}) collective-permute-start(f32[2,2,192,128]{3,2,1,0:T(8,128)S(1)} %pad_maximum_fusion.1), channel_id=1, source_target_pairs={{0,192},{64,128},{128,64},{192,0},{1,193},{65,129},{129,65},{193,1... | collective-permute-start | bytes 1179656 | tf_op jit(solution)/shard_map/ppermute | solution.py:271
  26.8 6.9 %collective-permute-start.29 = (f32[2,48,512]{2,1,0:T(8,128)S(1)}, f32[2,48,512]{2,1,0:T(8,128)S(1)}, u32[]{:S(2)}, u32[]{:S(2)}) collective-permute-start(f32[2,48,512]{2,1,0:T(8,128)S(1)} %collective-permute-done.27.refs_3_), channel_id=1, source_target_pairs={{0,8},{4,12},{8,16},{12,20},{16,24},{20,28},{24,32},{28,36},{32,40... | collective-permute-start | bytes 589832 | tf_op jit(solution)/shard_map/ppermute | solution.py:260
  26.8 6.9 %collective-permute-start.31 = (f32[2,48,512]{2,1,0:T(8,128)S(1)}, f32[2,48,512]{2,1,0:T(8,128)S(1)}, u32[]{:S(2)}, u32[]{:S(2)}) collective-permute-start(f32[2,48,512]{2,1,0:T(8,128)S(1)} %get-tuple-element.207.refs_0_), channel_id=1, source_target_pairs={{0,4},{4,0},{8,12},{12,8},{16,20},{20,16},{24,28},{28,24},{32,36},... | collective-permute-start | bytes 589832 | tf_op jit(solution)/shard_map/ppermute | solution.py:257
  26.8 7.5 %collective-permute-start.33 = (f32[2,48,512]{2,1,0:T(8,128)S(1)}, f32[2,48,512]{2,1,0:T(8,128)S(1)}, u32[]{:S(2)}, u32[]{:S(2)}) collective-permute-start(f32[2,48,512]{2,1,0:T(8,128)S(1)} %collective-permute-done.26.refs_2_), channel_id=1, source_target_pairs={{0,4},{4,0},{8,12},{12,8},{16,20},{20,16},{24,28},{28,24},{32,36},... | collective-permute-start | bytes 589832 | tf_op jit(solution)/shard_map/ppermute | solution.py:257
  27.3 7.0 %collective-permute-start.32 = (f32[2,48,512]{2,1,0:T(8,128)S(1)}, f32[2,48,512]{2,1,0:T(8,128)S(1)}, u32[]{:S(2)}, u32[]{:S(2)}) collective-permute-start(f32[2,48,512]{2,1,0:T(8,128)S(1)} %collective-permute-done.25.refs_1_), channel_id=1, source_target_pairs={{0,4},{4,0},{8,12},{12,8},{16,20},{20,16},{24,28},{28,24},{32,36},... | collective-permute-start | bytes 589832 | tf_op jit(solution)/shard_map/ppermute | solution.py:257
  33.7 1.4 %collective-permute-start.35 = (f32[2,48,512]{2,1,0:T(8,128)S(1)}, f32[2,48,512]{2,1,0:T(8,128)S(1)}, u32[]{:S(2)}, u32[]{:S(2)}) collective-permute-start(f32[2,48,512]{2,1,0:T(8,128)S(1)} %collective-permute-done.28.refs_4_), channel_id=1, source_target_pairs={{0,4},{4,0},{8,12},{12,8},{16,20},{20,16},{24,28},{28,24},{32,36},... | collective-permute-start | bytes 589832 | tf_op jit(solution)/shard_map/ppermute | solution.py:257
  33.7 8.8 %copy-start.1 = (s32[16]{0:T(128)S(1)}, s32[16]{0:T(128)}, u32[]{:S(2)}) copy-start(s32[16]{0:T(128)} %target.5) | copy-start | bytes 196
  33.7 8.8 %copy-start.2 = (s32[8]{0:T(128)S(1)}, s32[8]{0:T(128)}, u32[]{:S(2)}) copy-start(s32[8]{0:T(128)} %second.5) | copy-start | bytes 100
  33.8 7.5 %collective-permute-start.34 = (f32[2,48,512]{2,1,0:T(8,128)S(1)}, f32[2,48,512]{2,1,0:T(8,128)S(1)}, u32[]{:S(2)}, u32[]{:S(2)}) collective-permute-start(f32[2,48,512]{2,1,0:T(8,128)S(1)} %collective-permute-done.27.refs_3_), channel_id=1, source_target_pairs={{0,4},{4,0},{8,12},{12,8},{16,20},{20,16},{24,28},{28,24},{32,36},... | collective-permute-start | bytes 589832 | tf_op jit(solution)/shard_map/ppermute | solution.py:257
  34.4 4.8 %collective-permute-start.41 = (f32[1,48,512]{2,1,0:T(8,128)S(1)}, f32[1,48,512]{2,1,0:T(8,128)S(1)}, u32[]{:S(2)}, u32[]{:S(2)}) collective-permute-start(f32[1,48,512]{2,1,0:T(8,128)S(1)} %slice.23), channel_id=1, source_target_pairs={{0,56},{4,60},{8,0},{12,4},{16,8},{20,12},{24,16},{28,20},{32,24},... | collective-permute-start | bytes 294920 | tf_op jit(solution)/shard_map/ppermute | solution.py:260
  34.4 6.9 %collective-permute-start.37 = (f32[2,48,512]{2,1,0:T(8,128)S(1)}, f32[2,48,512]{2,1,0:T(8,128)S(1)}, u32[]{:S(2)}, u32[]{:S(2)}) collective-permute-start(f32[2,48,512]{2,1,0:T(8,128)S(1)} %collective-permute-done.30.refs_6_), channel_id=1, source_target_pairs={{0,4},{4,0},{8,12},{12,8},{16,20},{20,16},{24,28},{28,24},{32,36},... | collective-permute-start | bytes 589832 | tf_op jit(solution)/shard_map/ppermute | solution.py:257
  34.6 6.7 %collective-permute-start.36 = (f32[2,48,512]{2,1,0:T(8,128)S(1)}, f32[2,48,512]{2,1,0:T(8,128)S(1)}, u32[]{:S(2)}, u32[]{:S(2)}) collective-permute-start(f32[2,48,512]{2,1,0:T(8,128)S(1)} %collective-permute-done.29.refs_5_), channel_id=1, source_target_pairs={{0,4},{4,0},{8,12},{12,8},{16,20},{20,16},{24,28},{28,24},{32,36},... | collective-permute-start | bytes 589832 | tf_op jit(solution)/shard_map/ppermute | solution.py:257
  35.1 6.1 %collective-permute-start.40 = (f32[1,48,512]{2,1,0:T(8,128)S(1)}, f32[1,48,512]{2,1,0:T(8,128)S(1)}, u32[]{:S(2)}, u32[]{:S(2)}) collective-permute-start(f32[1,48,512]{2,1,0:T(8,128)S(1)} %slice.22), channel_id=1, source_target_pairs={{0,8},{4,12},{8,16},{12,20},{16,24},{20,28},{24,32},{28,36},{32,40... | collective-permute-start | bytes 294920 | tf_op jit(solution)/shard_map/ppermute | solution.py:260
  39.2 3.0 %collective-permute-start.43 = (f32[1,48,512]{2,1,0:T(8,128)S(1)}, f32[1,48,512]{2,1,0:T(8,128)S(1)}, u32[]{:S(2)}, u32[]{:S(2)}) collective-permute-start(f32[1,48,512]{2,1,0:T(8,128)S(1)} %collective-permute-done.41.refs_1_), channel_id=1, source_target_pairs={{0,4},{4,0},{8,12},{12,8},{16,20},{20,16},{24,28},{28,24},{32,36},... | collective-permute-start | bytes 294920 | tf_op jit(solution)/shard_map/ppermute | solution.py:257
  41.3 1.3 %collective-permute-start.42 = (f32[1,48,512]{2,1,0:T(8,128)S(1)}, f32[1,48,512]{2,1,0:T(8,128)S(1)}, u32[]{:S(2)}, u32[]{:S(2)}) collective-permute-start(f32[1,48,512]{2,1,0:T(8,128)S(1)} %collective-permute-done.40.refs_0_), channel_id=1, source_target_pairs={{0,4},{4,0},{8,12},{12,8},{16,20},{20,16},{24,28},{28,24},{32,36},... | collective-permute-start | bytes 294920 | tf_op jit(solution)/shard_map/ppermute | solution.py:257
  46.9 18.1 %copy-start = (s32[8]{0:T(128)S(1)}, s32[8]{0:T(128)}, u32[]{:S(2)}) copy-start(s32[8]{0:T(128)} %first.5) | copy-start | bytes 100
  46.9 7.8 %collective-permute-start.44 = (f32[96,512]{1,0:T(8,128)S(1)}, f32[96,512]{1,0:T(8,128)S(1)}, u32[]{:S(2)}, u32[]{:S(2)}) collective-permute-start(f32[96,512]{1,0:T(8,128)S(1)} %get-tuple-element.213), channel_id=1, source_target_pairs={{0,1},{1,2},{2,3},{3,0},{4,5},{5,6},{6,7},{7,4},{8,9},{9,10},{10,1... | collective-permute-start | bytes 589832 | tf_op jit(solution)/shard_map/ppermute | solution.py:254
  47.1 9.0 %collective-permute-start.45 = (f32[96,512]{1,0:T(8,128)S(1)}, f32[96,512]{1,0:T(8,128)S(1)}, u32[]{:S(2)}, u32[]{:S(2)}) collective-permute-start(f32[96,512]{1,0:T(8,128)S(1)} %get-tuple-element.214), channel_id=1, source_target_pairs={{0,3},{1,0},{2,1},{3,2},{4,7},{5,4},{6,5},{7,6},{8,11},{9,8},{10,9... | collective-permute-start | bytes 589832 | tf_op jit(solution)/shard_map/ppermute | solution.py:254
  48.9 12.5 %collective-permute-start.47 = (f32[96,512]{1,0:T(8,128)}, f32[96,512]{1,0:T(8,128)}, u32[]{:S(2)}, u32[]{:S(2)}) collective-permute-start(f32[96,512]{1,0:T(8,128)} %get-tuple-element.216), channel_id=1, source_target_pairs={{0,1},{1,2},{2,3},{3,0},{4,5},{5,6},{6,7},{7,4},{8,9},{9,10},{10,1... | collective-permute-start | bytes 589832 | tf_op jit(solution)/shard_map/ppermute | solution.py:254
  50.3 11.1 %collective-permute-start.48 = (f32[96,512]{1,0:T(8,128)}, f32[96,512]{1,0:T(8,128)}, u32[]{:S(2)}, u32[]{:S(2)}) collective-permute-start(f32[96,512]{1,0:T(8,128)} %get-tuple-element.217), channel_id=1, source_target_pairs={{0,3},{1,0},{2,1},{3,2},{4,7},{5,4},{6,5},{7,6},{8,11},{9,8},{10,9... | collective-permute-start | bytes 589832 | tf_op jit(solution)/shard_map/ppermute | solution.py:254
  57.5 6.0 %collective-permute-start.46 = (f32[96,512]{1,0:T(8,128)}, f32[96,512]{1,0:T(8,128)}, u32[]{:S(2)}, u32[]{:S(2)}) collective-permute-start(f32[96,512]{1,0:T(8,128)} %get-tuple-element.215), channel_id=1, source_target_pairs={{0,1},{1,2},{2,3},{3,0},{4,5},{5,6},{6,7},{7,4},{8,9},{9,10},{10,1... | collective-permute-start | bytes 589832 | tf_op jit(solution)/shard_map/ppermute | solution.py:254
  57.8 7.2 %collective-permute-start.49 = (f32[96,512]{1,0:T(8,128)}, f32[96,512]{1,0:T(8,128)}, u32[]{:S(2)}, u32[]{:S(2)}) collective-permute-start(f32[96,512]{1,0:T(8,128)} %get-tuple-element.218), channel_id=1, source_target_pairs={{0,3},{1,0},{2,1},{3,2},{4,7},{5,4},{6,5},{7,6},{8,11},{9,8},{10,9... | collective-permute-start | bytes 589832 | tf_op jit(solution)/shard_map/ppermute | solution.py:254

commit v7 on v6

--- a/solution.py
+++ b/solution.py
@@ -249,6 +249,10 @@
         cost_estimate=pl.CostEstimate(flops=10**9, bytes_accessed=4 * 10**6, transcendentals=0),
         name="pack_w",
     )(pos, starts, first, second, target, integrals)
+
+    n_lanes, n_passes = (limit.reshape(()) for limit in limits)
+    passes = (n_lanes, n_passes, jnp.minimum(n_passes, 1), n_passes > 1)
+    w0, passes = lax.optimization_barrier((w0, passes))
 
     def along(x, axis, step):
         return lax.ppermute(x, axis, [(i, (i + step) % 4) for i in range(4)])
@@ -312,7 +316,7 @@
         compiler_params=params(),
         name="expand",
     )(pos, starts, first, target, hot, *sums, *more)
-    return out, limits
+    return out, passes
 
 
 def per_device(amplitudes, integrals, irrep_virtual, irrep_first, irrep_second, irrep_target):
@@ -329,9 +333,13 @@
         labels = (starts, irrep_first, irrep_second, irrep_target)
         return one_pass(position(n_lane, n_block), *labels, amplitudes, flat, w_rows, before)
 
-    out, limits = run(jnp.int32(0), jnp.int32(0), None)
-    n_lanes, n_passes = (limit.reshape(()) for limit in limits)
-    return lax.fori_loop(1, n_passes, lambda n, acc: run(n % n_lanes, n // n_lanes, acc)[0], out)
+    out, (n_lanes, n_passes, done, more) = run(jnp.int32(0), jnp.int32(0), None)
+
+    def further(state):
+        n, _, acc = state
+        return n + 1, n + 1 < n_passes, run(lax.rem(n, n_lanes), lax.div(n, n_lanes), acc)[0]
+
+    return lax.while_loop(lambda state: state[1], further, (done, more, out))[2]
 
 
 def solution(mesh):

time: 69.9 us -> 65.1 us (0.931)
  the two profiles are of different devices: /device:TPU:24 before, /device:TPU:32 now
where the time goes in v7:
time: 65.1 us; the launch traced here: 64.9 us
  starting transfers between devices  28.8 us (44%)
  waiting for transfers between devices  20.7 us (32%)
  Pallas kernels  12.8 us (20%)
  between operations  1.42 us (2%)
  other arithmetic  0.84 us (1%)
    ppermute x8, waiting for transfers between devices, ring(): return lax.ppermute(x, 'col', [(i, (i + 2 * step) % 16) for i in range(16)])  13.5 us
    ppermute x8, starting transfers between devices, ring(): return lax.ppermute(x, 'col', [(i, (i + 2 * step) % 16) for i in range(16)])  13 us
    ppermute x6, starting transfers between devices, along(): return lax.ppermute(x, axis, [(i, (i + step) % 4) for i in range(4)])  9.86 us
    ppermute x6, waiting for transfers between devices, along(): return lax.ppermute(x, axis, [(i, (i + step) % 4) for i in range(4)])  6.85 us
    pallas_call x1, Pallas kernels, one_pass(): pl.pallas_call(functools.partial(product_kernel, where), out_shape=(shape...  3.52 us
    pallas_call x1, Pallas kernels, one_pass(): pl.pallas_call(expand_kernel, out_shape=shape((1, b_local, x_local), F32)...  3.04 us
    ppermute x1, starting transfers between devices, one_pass(): lax.ppermute(jnp.stack([w0, pair]), 'row', [(i, 3 - i) for i in range(4)])  2.86 us
    pallas_call x1, Pallas kernels, one_pass(): pl.pallas_call(functools.partial(pack_w_kernel, x_local // first.shape[0]...  2.46 us
  transfers between devices with their start and end apart: 25, of which 11 were waited for; matrix products, arithmetic and copies ran while one was open for 0% of the time, Pallas kernels for 6%

profile of v7, /device:TPU:32, one launch (start us, length us, event | category | flops | bytes accessed | tf_op | source)
XLA Modules:
  0.0 64.9 jit_solution(18127176634514572370)
XLA Ops:
  0.0 0.8 %convert_reduce_fusion.starts = s32[16]{0:T(128)S(1)} fusion(s32[768]{0:T(1024)} %param.10), kind=kLoop, calls=%fused_computation.2 | loop fusion | flops 36848 | bytes 3136 | tf_op jit(solution)/shard_map/reduce_sum | solution.py:323
  0.8 0.1 stack.51.pos
  0.9 2.3 %pack_t.2 = (f32[2,48,512]{2,1,0:T(8,128)S(1)}, bf16[512,1536]{1,0:T(8,128)(2,1)S(1)}) custom-call(s32[8]{0:T(128)S(1)} %stack.51.pos, s32[16]{0:T(128)S(1)} %convert_reduce_fusion.starts, s32[8]{0:T(128)} %first.5, s32[8]{0:T(128)} %second.5, f32[2,48,1536]{2,1,0:T(8,128)} %t_ref.1), custom_call_target="tpu_custom_call" | custom-call | tf_op jit(solution)/shard_map/pack_t/pallas_call | solution.py:235
  3.2 2.0 %collective-permute-start.25 = (f32[2,48,512]{2,1,0:T(8,128)S(1)}, f32[2,48,512]{2,1,0:T(8,128)S(1)}, u32[]{:S(2)}, u32[]{:S(2)}) collective-permute-start(f32[2,48,512]{2,1,0:T(8,128)S(1)} %get-tuple-element.115.refs_0_), channel_id=1, source_target_pairs={{0,8},{4,12},{8,16},{12,20},{16,24},{20,28},{24,32},{28,36},{32,40... | collective-permute-start | bytes 589832 | tf_op jit(solution)/shard_map/ppermute | solution.py:264
  5.2 0.1 collective-permute-start.26
  5.3 2.5 %pack_w.2 = (f32[2,192,128]{2,1,0:T(8,128)S(1)}, s32[1]{0:T(128)}, s32[1]{0:T(128)}) custom-call(s32[8]{0:T(128)S(1)} %stack.51.pos, s32[16]{0:T(128)S(1)} %convert_reduce_fusion.starts, s32[8]{0:T(128)} %first.5, s32[8]{0:T(128)} %second.5, s32[16]{0:T(128)} %target.5, f32[2304,128]{1,0:T(8,128)} %bitcast.10.w_ref), custom_call_target="tpu_custom_call" | custom-call | flops 1000000000 | bytes 4000000 | tf_op jit(solution)/shard_map/pack_w/pallas_call | solution.py:243
  8.8 1.1 %collective-permute-done.25.refs_1_ = f32[2,48,512]{2,1,0:T(8,128)S(1)} collective-permute-done((f32[2,48,512]{2,1,0:T(8,128)S(1)}, f32[2,48,512]{2,1,0:T(8,128)S(1)}, u32[]{:S(2)}, u32[]{:S(2)}) %collective-permute-start.25) | collective-permute-done | bytes 196640 | tf_op jit(solution)/shard_map/ppermute | solution.py:264
  9.9 1.9 %collective-permute-start.27 = (f32[2,48,512]{2,1,0:T(8,128)S(1)}, f32[2,48,512]{2,1,0:T(8,128)S(1)}, u32[]{:S(2)}, u32[]{:S(2)}) collective-permute-start(f32[2,48,512]{2,1,0:T(8,128)S(1)} %collective-permute-done.25.refs_1_), channel_id=1, source_target_pairs={{0,8},{4,12},{8,16},{12,20},{16,24},{20,28},{24,32},{28,36},{32,40... | collective-permute-start | bytes 589832 | tf_op jit(solution)/shard_map/ppermute | solution.py:264
  11.8 1.5 %collective-permute-start.38 = (f32[2,192,128]{2,1,0:T(8,128)S(1)}, f32[2,192,128]{2,1,0:T(8,128)S(1)}, u32[]{:S(2)}, u32[]{:S(2)}) collective-permute-start(f32[2,192,128]{2,1,0:T(8,128)S(1)} %get-tuple-element.116.refs_14_), channel_id=1, source_target_pairs={{0,64},{64,0},{128,192},{192,128},{1,65},{65,1},{129,193},{193,129... | collective-permute-start | bytes 589832 | tf_op jit(solution)/shard_map/ppermute | solution.py:274
  13.3 0.0 collective-permute-done.26.refs_2_
  13.3 2.3 %collective-permute-start.28 = (f32[2,48,512]{2,1,0:T(8,128)S(1)}, f32[2,48,512]{2,1,0:T(8,128)S(1)}, u32[]{:S(2)}, u32[]{:S(2)}) collective-permute-start(f32[2,48,512]{2,1,0:T(8,128)S(1)} %collective-permute-done.26.refs_2_), channel_id=1, source_target_pairs={{0,56},{4,60},{8,0},{12,4},{16,8},{20,12},{24,16},{28,20},{32,24},... | collective-permute-start | bytes 589832 | tf_op jit(solution)/shard_map/ppermute | solution.py:264
  15.6 2.8 %collective-permute-done.27.refs_3_ = f32[2,48,512]{2,1,0:T(8,128)S(1)} collective-permute-done((f32[2,48,512]{2,1,0:T(8,128)S(1)}, f32[2,48,512]{2,1,0:T(8,128)S(1)}, u32[]{:S(2)}, u32[]{:S(2)}) %collective-permute-start.27) | collective-permute-done | bytes 196640 | tf_op jit(solution)/shard_map/ppermute | solution.py:264
  18.4 0.0 collective-permute-start.29
  18.4 0.0 collective-permute-done.38.refs_15_
  18.5 2.9 %collective-permute-start.39 = (f32[2,2,192,128]{3,2,1,0:T(8,128)S(1)}, f32[2,2,192,128]{3,2,1,0:T(8,128)S(1)}, u32[]{:S(2)}, u32[]{:S(2)}) collective-permute-start(f32[2,2,192,128]{3,2,1,0:T(8,128)S(1)} %pad_maximum_fusion.1), channel_id=1, source_target_pairs={{0,192},{64,128},{128,64},{192,0},{1,193},{65,129},{129,65},{193,1... | collective-permute-start | bytes 1179656 | tf_op jit(solution)/shard_map/ppermute | solution.py:275
  21.3 3.0 %collective-permute-start.30 = (f32[2,48,512]{2,1,0:T(8,128)S(1)}, f32[2,48,512]{2,1,0:T(8,128)S(1)}, u32[]{:S(2)}, u32[]{:S(2)}) collective-permute-start(f32[2,48,512]{2,1,0:T(8,128)S(1)} %collective-permute-done.28.refs_4_), channel_id=1, source_target_pairs={{0,56},{4,60},{8,0},{12,4},{16,8},{20,12},{24,16},{28,20},{32,24},... | collective-permute-start | bytes 589832 | tf_op jit(solution)/shard_map/ppermute | solution.py:264
  24.3 0.0 collective-permute-start.31
  24.3 0.5 collective-permute-start.32
  24.8 0.2 collective-permute-done.29.refs_5_
  25.0 2.9 %collective-permute-done.30.refs_6_ = f32[2,48,512]{2,1,0:T(8,128)S(1)} collective-permute-done((f32[2,48,512]{2,1,0:T(8,128)S(1)}, f32[2,48,512]{2,1,0:T(8,128)S(1)}, u32[]{:S(2)}, u32[]{:S(2)}) %collective-permute-start.30) | collective-permute-done | bytes 196640 | tf_op jit(solution)/shard_map/ppermute | solution.py:264
  27.9 0.0 copy-start.4
  27.9 0.0 copy-start.5
  27.9 0.0 collective-permute-done.31.refs_7_
  28.0 0.6 collective-permute-start.35
  28.5 3.7 %collective-permute-start.40 = (f32[1,48,512]{2,1,0:T(8,128)S(1)}, f32[1,48,512]{2,1,0:T(8,128)S(1)}, u32[]{:S(2)}, u32[]{:S(2)}) collective-permute-start(f32[1,48,512]{2,1,0:T(8,128)S(1)} %slice.16), channel_id=1, source_target_pairs={{0,8},{4,12},{8,16},{12,20},{16,24},{20,28},{24,32},{28,36},{32,40... | collective-permute-start | bytes 294920 | tf_op jit(solution)/shard_map/ppermute | solution.py:264
  32.2 0.0 collective-permute-done.33.refs_9_
  32.2 0.5 collective-permute-start.37
  32.8 0.0 collective-permute-done.34.refs_10_
  32.8 0.0 collective-permute-start.41
  32.8 1.8 %collective-permute-done.40.refs_0_ = f32[1,48,512]{2,1,0:T(8,128)S(1)} collective-permute-done((f32[1,48,512]{2,1,0:T(8,128)S(1)}, f32[1,48,512]{2,1,0:T(8,128)S(1)}, u32[]{:S(2)}, u32[]{:S(2)}) %collective-permute-start.40) | collective-permute-done | bytes 98336 | tf_op jit(solution)/shard_map/ppermute | solution.py:264
  34.6 4.8 %collective-permute-done.41.refs_1_ = f32[1,48,512]{2,1,0:T(8,128)S(1)} collective-permute-done((f32[1,48,512]{2,1,0:T(8,128)S(1)}, f32[1,48,512]{2,1,0:T(8,128)S(1)}, u32[]{:S(2)}, u32[]{:S(2)}) %collective-permute-start.41) | collective-permute-done | bytes 98336 | tf_op jit(solution)/shard_map/ppermute | solution.py:264
  39.3 0.9 %place.2 = (f32[2,768,512]{2,1,0:T(8,128)S(1)}, f32[2,768,128]{2,1,0:T(8,128)S(1)}, f32[896,512]{1,0:T(8,128)S(1)}) custom-call(s32[8]{0:T(128)S(1)} %stack.51.pos, f32[2,48,512]{2,1,0:T(8,128)S(1)} %get-tuple-element.115.refs_0_, f32[2,48,512]{2,1,0:T(8,128)S(1)} %collective-permute-done.25.refs_1_, f32[2,48,512]{2,1,0:T(8,128)S(1)} %collective-permute-done.26.refs_2_, ...), custom_call_target="tpu_custom_call" | custom-call | bytes 7000000 | tf_op jit(solution)/shard_map/place/pallas_call | solution.py:276
  40.3 0.3 collective-permute-done.43.refs_3_
  40.6 3.5 %product.2 = (f32[2,768,512]{2,1,0:T(8,128)S(1)}, f32[896,512]{1,0:T(8,128)S(1)}, f32[96,512]{1,0:T(8,128)S(1)}, f32[96,512]{1,0:T(8,128)S(1)}, f32[96,512]{1,0:T(8,128)S(1)}, /*index=5*/f32[96,512]{1,0:T(8,128)S(1)}) custom-call(s32[8]{0:T(128)S(1)} %stack.51.pos, s32[16]{0:T(128)S(1)} %convert_reduce_fusion.starts, ...), custom_call_target="tpu_custom_call", output_to_operand_aliasing={{0}: (4, {}), {1}: (5, {})} | custom-call | tf_op jit(solution)/shard_map/product/pallas_call | solution.py:288
  44.2 0.0 copy-start.3
  44.2 1.7 %collective-permute-start.44 = (f32[96,512]{1,0:T(8,128)S(1)}, f32[96,512]{1,0:T(8,128)S(1)}, u32[]{:S(2)}, u32[]{:S(2)}) collective-permute-start(f32[96,512]{1,0:T(8,128)S(1)} %get-tuple-element.121), channel_id=1, source_target_pairs={{0,1},{1,2},{2,3},{3,0},{4,5},{5,6},{6,7},{7,4},{8,9},{9,10},{10,1... | collective-permute-start | bytes 589832 | tf_op jit(solution)/shard_map/ppermute | solution.py:258
  45.8 1.7 %collective-permute-start.45 = (f32[96,512]{1,0:T(8,128)S(1)}, f32[96,512]{1,0:T(8,128)S(1)}, u32[]{:S(2)}, u32[]{:S(2)}) collective-permute-start(f32[96,512]{1,0:T(8,128)S(1)} %get-tuple-element.122), channel_id=1, source_target_pairs={{0,3},{1,0},{2,1},{3,2},{4,7},{5,4},{6,5},{7,6},{8,11},{9,8},{10,9... | collective-permute-start | bytes 589832 | tf_op jit(solution)/shard_map/ppermute | solution.py:258
  47.5 0.4 collective-permute-start.47
  47.9 2.9 %collective-permute-start.48 = (f32[96,512]{1,0:T(8,128)S(1)}, f32[96,512]{1,0:T(8,128)S(1)}, u32[]{:S(2)}, u32[]{:S(2)}) collective-permute-start(f32[96,512]{1,0:T(8,128)S(1)} %get-tuple-element.125), channel_id=1, source_target_pairs={{0,3},{1,0},{2,1},{3,2},{4,7},{5,4},{6,5},{7,6},{8,11},{9,8},{10,9... | collective-permute-start | bytes 589832 | tf_op jit(solution)/shard_map/ppermute | solution.py:258
  50.7 2.5 %collective-permute-done.44.relay_up = f32[96,512]{1,0:T(8,128)S(1)} collective-permute-done((f32[96,512]{1,0:T(8,128)S(1)}, f32[96,512]{1,0:T(8,128)S(1)}, u32[]{:S(2)}, u32[]{:S(2)}) %collective-permute-start.44) | collective-permute-done | bytes 196640 | tf_op jit(solution)/shard_map/ppermute | solution.py:258
  53.2 0.4 collective-permute-done.45.relay_down
  53.6 0.6 join.2
  54.2 1.6 %collective-permute-start.46 = (f32[96,512]{1,0:T(8,128)S(1)}, f32[96,512]{1,0:T(8,128)S(1)}, u32[]{:S(2)}, u32[]{:S(2)}) collective-permute-start(f32[96,512]{1,0:T(8,128)S(1)} %get-tuple-element.123), channel_id=1, source_target_pairs={{0,1},{1,2},{2,3},{3,0},{4,5},{5,6},{6,7},{7,4},{8,9},{9,10},{10,1... | collective-permute-start | bytes 589832 | tf_op jit(solution)/shard_map/ppermute | solution.py:258
  55.8 1.7 %collective-permute-start.49 = (f32[96,512]{1,0:T(8,128)S(1)}, f32[96,512]{1,0:T(8,128)S(1)}, u32[]{:S(2)}, u32[]{:S(2)}) collective-permute-start(f32[96,512]{1,0:T(8,128)S(1)} %get-tuple-element.126), channel_id=1, source_target_pairs={{0,3},{1,0},{2,1},{3,2},{4,7},{5,4},{6,5},{7,6},{8,11},{9,8},{10,9... | collective-permute-start | bytes 589832 | tf_op jit(solution)/shard_map/ppermute | solution.py:258
  57.5 3.6 %collective-permute-done.46.refs_1_ = f32[96,512]{1,0:T(8,128)S(1)} collective-permute-done((f32[96,512]{1,0:T(8,128)S(1)}, f32[96,512]{1,0:T(8,128)S(1)}, u32[]{:S(2)}, u32[]{:S(2)}) %collective-permute-start.46) | collective-permute-done | bytes 196640 | tf_op jit(solution)/shard_map/ppermute | solution.py:258
  61.2 0.3 collective-permute-done.49.refs_4_
  61.5 3.0 %expand.2 = f32[1,192,1536]{2,1,0:T(8,128)} custom-call(s32[8]{0:T(128)S(1)} %stack.51.pos, s32[16]{0:T(128)S(1)} %convert_reduce_fusion.starts, s32[8]{0:T(128)S(1)} %copy-done.3, s32[16]{0:T(128)S(1)} %copy-done.5, bf16[512,1536]{1,0:T(8,128)(2,1)S(1)} %get-tuple-element.114.g_ref, f32[896,512]{1,0:T(8,128)S(1)} %get-tuple-element.120.total.refs_0_, ...), custom_call_target="tpu_custom_call" | custom-call | tf_op jit(solution)/shard_map/expand/pallas_call | solution.py:310
  64.5 0.2 while.12
  (21 shorter events, 0.1 us)
Async XLA Ops:
  3.2 6.7 %collective-permute-start.25 = (f32[2,48,512]{2,1,0:T(8,128)S(1)}, f32[2,48,512]{2,1,0:T(8,128)S(1)}, u32[]{:S(2)}, u32[]{:S(2)}) collective-permute-start(f32[2,48,512]{2,1,0:T(8,128)S(1)} %get-tuple-element.115.refs_0_), channel_id=1, source_target_pairs={{0,8},{4,12},{8,16},{12,20},{16,24},{20,28},{24,32},{28,36},{32,40... | collective-permute-start | bytes 589832 | tf_op jit(solution)/shard_map/ppermute | solution.py:264
  5.2 8.1 %collective-permute-start.26 = (f32[2,48,512]{2,1,0:T(8,128)S(1)}, f32[2,48,512]{2,1,0:T(8,128)S(1)}, u32[]{:S(2)}, u32[]{:S(2)}) collective-permute-start(f32[2,48,512]{2,1,0:T(8,128)S(1)} %get-tuple-element.115.refs_0_), channel_id=1, source_target_pairs={{0,56},{4,60},{8,0},{12,4},{16,8},{20,12},{24,16},{28,20},{32,24},... | collective-permute-start | bytes 589832 | tf_op jit(solution)/shard_map/ppermute | solution.py:264
  9.9 8.5 %collective-permute-start.27 = (f32[2,48,512]{2,1,0:T(8,128)S(1)}, f32[2,48,512]{2,1,0:T(8,128)S(1)}, u32[]{:S(2)}, u32[]{:S(2)}) collective-permute-start(f32[2,48,512]{2,1,0:T(8,128)S(1)} %collective-permute-done.25.refs_1_), channel_id=1, source_target_pairs={{0,8},{4,12},{8,16},{12,20},{16,24},{20,28},{24,32},{28,36},{32,40... | collective-permute-start | bytes 589832 | tf_op jit(solution)/shard_map/ppermute | solution.py:264
  11.8 6.6 %collective-permute-start.38 = (f32[2,192,128]{2,1,0:T(8,128)S(1)}, f32[2,192,128]{2,1,0:T(8,128)S(1)}, u32[]{:S(2)}, u32[]{:S(2)}) collective-permute-start(f32[2,192,128]{2,1,0:T(8,128)S(1)} %get-tuple-element.116.refs_14_), channel_id=1, source_target_pairs={{0,64},{64,0},{128,192},{192,128},{1,65},{65,1},{129,193},{193,129... | collective-permute-start | bytes 589832 | tf_op jit(solution)/shard_map/ppermute | solution.py:274
  13.3 8.0 %collective-permute-start.28 = (f32[2,48,512]{2,1,0:T(8,128)S(1)}, f32[2,48,512]{2,1,0:T(8,128)S(1)}, u32[]{:S(2)}, u32[]{:S(2)}) collective-permute-start(f32[2,48,512]{2,1,0:T(8,128)S(1)} %collective-permute-done.26.refs_2_), channel_id=1, source_target_pairs={{0,56},{4,60},{8,0},{12,4},{16,8},{20,12},{24,16},{28,20},{32,24},... | collective-permute-start | bytes 589832 | tf_op jit(solution)/shard_map/ppermute | solution.py:264
  18.4 6.6 %collective-permute-start.29 = (f32[2,48,512]{2,1,0:T(8,128)S(1)}, f32[2,48,512]{2,1,0:T(8,128)S(1)}, u32[]{:S(2)}, u32[]{:S(2)}) collective-permute-start(f32[2,48,512]{2,1,0:T(8,128)S(1)} %collective-permute-done.27.refs_3_), channel_id=1, source_target_pairs={{0,8},{4,12},{8,16},{12,20},{16,24},{20,28},{24,32},{28,36},{32,40... | collective-permute-start | bytes 589832 | tf_op jit(solution)/shard_map/ppermute | solution.py:264
  18.5 13.8 %collective-permute-start.39 = (f32[2,2,192,128]{3,2,1,0:T(8,128)S(1)}, f32[2,2,192,128]{3,2,1,0:T(8,128)S(1)}, u32[]{:S(2)}, u32[]{:S(2)}) collective-permute-start(f32[2,2,192,128]{3,2,1,0:T(8,128)S(1)} %pad_maximum_fusion.1), channel_id=1, source_target_pairs={{0,192},{64,128},{128,64},{192,0},{1,193},{65,129},{129,65},{193,1... | collective-permute-start | bytes 1179656 | tf_op jit(solution)/shard_map/ppermute | solution.py:275
  21.3 6.6 %collective-permute-start.30 = (f32[2,48,512]{2,1,0:T(8,128)S(1)}, f32[2,48,512]{2,1,0:T(8,128)S(1)}, u32[]{:S(2)}, u32[]{:S(2)}) collective-permute-start(f32[2,48,512]{2,1,0:T(8,128)S(1)} %collective-permute-done.28.refs_4_), channel_id=1, source_target_pairs={{0,56},{4,60},{8,0},{12,4},{16,8},{20,12},{24,16},{28,20},{32,24},... | collective-permute-start | bytes 589832 | tf_op jit(solution)/shard_map/ppermute | solution.py:264
  24.3 3.7 %collective-permute-start.31 = (f32[2,48,512]{2,1,0:T(8,128)S(1)}, f32[2,48,512]{2,1,0:T(8,128)S(1)}, u32[]{:S(2)}, u32[]{:S(2)}) collective-permute-start(f32[2,48,512]{2,1,0:T(8,128)S(1)} %get-tuple-element.115.refs_0_), channel_id=1, source_target_pairs={{0,4},{4,0},{8,12},{12,8},{16,20},{20,16},{24,28},{28,24},{32,36},... | collective-permute-start | bytes 589832 | tf_op jit(solution)/shard_map/ppermute | solution.py:261
  24.3 4.3 %collective-permute-start.32 = (f32[2,48,512]{2,1,0:T(8,128)S(1)}, f32[2,48,512]{2,1,0:T(8,128)S(1)}, u32[]{:S(2)}, u32[]{:S(2)}) collective-permute-start(f32[2,48,512]{2,1,0:T(8,128)S(1)} %collective-permute-done.25.refs_1_), channel_id=1, source_target_pairs={{0,4},{4,0},{8,12},{12,8},{16,20},{20,16},{24,28},{28,24},{32,36},... | collective-permute-start | bytes 589832 | tf_op jit(solution)/shard_map/ppermute | solution.py:261
  25.0 7.2 %collective-permute-start.33 = (f32[2,48,512]{2,1,0:T(8,128)S(1)}, f32[2,48,512]{2,1,0:T(8,128)S(1)}, u32[]{:S(2)}, u32[]{:S(2)}) collective-permute-start(f32[2,48,512]{2,1,0:T(8,128)S(1)} %collective-permute-done.26.refs_2_), channel_id=1, source_target_pairs={{0,4},{4,0},{8,12},{12,8},{16,20},{20,16},{24,28},{28,24},{32,36},... | collective-permute-start | bytes 589832 | tf_op jit(solution)/shard_map/ppermute | solution.py:261
  27.9 4.9 %collective-permute-start.34 = (f32[2,48,512]{2,1,0:T(8,128)S(1)}, f32[2,48,512]{2,1,0:T(8,128)S(1)}, u32[]{:S(2)}, u32[]{:S(2)}) collective-permute-start(f32[2,48,512]{2,1,0:T(8,128)S(1)} %collective-permute-done.27.refs_3_), channel_id=1, source_target_pairs={{0,4},{4,0},{8,12},{12,8},{16,20},{20,16},{24,28},{28,24},{32,36},... | collective-permute-start | bytes 589832 | tf_op jit(solution)/shard_map/ppermute | solution.py:261
  27.9 12.7 %copy-start.4 = (s32[8]{0:T(128)S(1)}, s32[8]{0:T(128)}, u32[]{:S(2)}) copy-start(s32[8]{0:T(128)} %second.5) | copy-start | bytes 100
  27.9 12.7 %copy-start.5 = (s32[16]{0:T(128)S(1)}, s32[16]{0:T(128)}, u32[]{:S(2)}) copy-start(s32[16]{0:T(128)} %target.5) | copy-start | bytes 196
  28.0 11.4 %collective-permute-start.35 = (f32[2,48,512]{2,1,0:T(8,128)S(1)}, f32[2,48,512]{2,1,0:T(8,128)S(1)}, u32[]{:S(2)}, u32[]{:S(2)}) collective-permute-start(f32[2,48,512]{2,1,0:T(8,128)S(1)} %collective-permute-done.28.refs_4_), channel_id=1, source_target_pairs={{0,4},{4,0},{8,12},{12,8},{16,20},{20,16},{24,28},{28,24},{32,36},... | collective-permute-start | bytes 589832 | tf_op jit(solution)/shard_map/ppermute | solution.py:261
  28.5 6.0 %collective-permute-start.40 = (f32[1,48,512]{2,1,0:T(8,128)S(1)}, f32[1,48,512]{2,1,0:T(8,128)S(1)}, u32[]{:S(2)}, u32[]{:S(2)}) collective-permute-start(f32[1,48,512]{2,1,0:T(8,128)S(1)} %slice.16), channel_id=1, source_target_pairs={{0,8},{4,12},{8,16},{12,20},{16,24},{20,28},{24,32},{28,36},{32,40... | collective-permute-start | bytes 294920 | tf_op jit(solution)/shard_map/ppermute | solution.py:264
  32.2 7.1 %collective-permute-start.36 = (f32[2,48,512]{2,1,0:T(8,128)S(1)}, f32[2,48,512]{2,1,0:T(8,128)S(1)}, u32[]{:S(2)}, u32[]{:S(2)}) collective-permute-start(f32[2,48,512]{2,1,0:T(8,128)S(1)} %collective-permute-done.29.refs_5_), channel_id=1, source_target_pairs={{0,4},{4,0},{8,12},{12,8},{16,20},{20,16},{24,28},{28,24},{32,36},... | collective-permute-start | bytes 589832 | tf_op jit(solution)/shard_map/ppermute | solution.py:261
  32.2 7.1 %collective-permute-start.37 = (f32[2,48,512]{2,1,0:T(8,128)S(1)}, f32[2,48,512]{2,1,0:T(8,128)S(1)}, u32[]{:S(2)}, u32[]{:S(2)}) collective-permute-start(f32[2,48,512]{2,1,0:T(8,128)S(1)} %collective-permute-done.30.refs_6_), channel_id=1, source_target_pairs={{0,4},{4,0},{8,12},{12,8},{16,20},{20,16},{24,28},{28,24},{32,36},... | collective-permute-start | bytes 589832 | tf_op jit(solution)/shard_map/ppermute | solution.py:261
  32.8 6.6 %collective-permute-start.41 = (f32[1,48,512]{2,1,0:T(8,128)S(1)}, f32[1,48,512]{2,1,0:T(8,128)S(1)}, u32[]{:S(2)}, u32[]{:S(2)}) collective-permute-start(f32[1,48,512]{2,1,0:T(8,128)S(1)} %slice.17), channel_id=1, source_target_pairs={{0,56},{4,60},{8,0},{12,4},{16,8},{20,12},{24,16},{28,20},{32,24},... | collective-permute-start | bytes 294920 | tf_op jit(solution)/shard_map/ppermute | solution.py:264
  34.6 5.7 %collective-permute-start.42 = (f32[1,48,512]{2,1,0:T(8,128)S(1)}, f32[1,48,512]{2,1,0:T(8,128)S(1)}, u32[]{:S(2)}, u32[]{:S(2)}) collective-permute-start(f32[1,48,512]{2,1,0:T(8,128)S(1)} %collective-permute-done.40.refs_0_), channel_id=1, source_target_pairs={{0,4},{4,0},{8,12},{12,8},{16,20},{20,16},{24,28},{28,24},{32,36},... | collective-permute-start | bytes 294920 | tf_op jit(solution)/shard_map/ppermute | solution.py:261
  39.3 1.3 %collective-permute-start.43 = (f32[1,48,512]{2,1,0:T(8,128)S(1)}, f32[1,48,512]{2,1,0:T(8,128)S(1)}, u32[]{:S(2)}, u32[]{:S(2)}) collective-permute-start(f32[1,48,512]{2,1,0:T(8,128)S(1)} %collective-permute-done.41.refs_1_), channel_id=1, source_target_pairs={{0,4},{4,0},{8,12},{12,8},{16,20},{20,16},{24,28},{28,24},{32,36},... | collective-permute-start | bytes 294920 | tf_op jit(solution)/shard_map/ppermute | solution.py:261
  44.2 17.3 %copy-start.3 = (s32[8]{0:T(128)S(1)}, s32[8]{0:T(128)}, u32[]{:S(2)}) copy-start(s32[8]{0:T(128)} %first.5) | copy-start | bytes 100
  44.2 9.1 %collective-permute-start.44 = (f32[96,512]{1,0:T(8,128)S(1)}, f32[96,512]{1,0:T(8,128)S(1)}, u32[]{:S(2)}, u32[]{:S(2)}) collective-permute-start(f32[96,512]{1,0:T(8,128)S(1)} %get-tuple-element.121), channel_id=1, source_target_pairs={{0,1},{1,2},{2,3},{3,0},{4,5},{5,6},{6,7},{7,4},{8,9},{9,10},{10,1... | collective-permute-start | bytes 589832 | tf_op jit(solution)/shard_map/ppermute | solution.py:258
  45.8 7.8 %collective-permute-start.45 = (f32[96,512]{1,0:T(8,128)S(1)}, f32[96,512]{1,0:T(8,128)S(1)}, u32[]{:S(2)}, u32[]{:S(2)}) collective-permute-start(f32[96,512]{1,0:T(8,128)S(1)} %get-tuple-element.122), channel_id=1, source_target_pairs={{0,3},{1,0},{2,1},{3,2},{4,7},{5,4},{6,5},{7,6},{8,11},{9,8},{10,9... | collective-permute-start | bytes 589832 | tf_op jit(solution)/shard_map/ppermute | solution.py:258
  47.5 10.0 %collective-permute-start.47 = (f32[96,512]{1,0:T(8,128)S(1)}, f32[96,512]{1,0:T(8,128)S(1)}, u32[]{:S(2)}, u32[]{:S(2)}) collective-permute-start(f32[96,512]{1,0:T(8,128)S(1)} %get-tuple-element.124), channel_id=1, source_target_pairs={{0,1},{1,2},{2,3},{3,0},{4,5},{5,6},{6,7},{7,4},{8,9},{9,10},{10,1... | collective-permute-start | bytes 589832 | tf_op jit(solution)/shard_map/ppermute | solution.py:258
  47.9 9.7 %collective-permute-start.48 = (f32[96,512]{1,0:T(8,128)S(1)}, f32[96,512]{1,0:T(8,128)S(1)}, u32[]{:S(2)}, u32[]{:S(2)}) collective-permute-start(f32[96,512]{1,0:T(8,128)S(1)} %get-tuple-element.125), channel_id=1, source_target_pairs={{0,3},{1,0},{2,1},{3,2},{4,7},{5,4},{6,5},{7,6},{8,11},{9,8},{10,9... | collective-permute-start | bytes 589832 | tf_op jit(solution)/shard_map/ppermute | solution.py:258
  54.2 7.0 %collective-permute-start.46 = (f32[96,512]{1,0:T(8,128)S(1)}, f32[96,512]{1,0:T(8,128)S(1)}, u32[]{:S(2)}, u32[]{:S(2)}) collective-permute-start(f32[96,512]{1,0:T(8,128)S(1)} %get-tuple-element.123), channel_id=1, source_target_pairs={{0,1},{1,2},{2,3},{3,0},{4,5},{5,6},{6,7},{7,4},{8,9},{9,10},{10,1... | collective-permute-start | bytes 589832 | tf_op jit(solution)/shard_map/ppermute | solution.py:258
  55.8 5.7 %collective-permute-start.49 = (f32[96,512]{1,0:T(8,128)S(1)}, f32[96,512]{1,0:T(8,128)S(1)}, u32[]{:S(2)}, u32[]{:S(2)}) collective-permute-start(f32[96,512]{1,0:T(8,128)S(1)} %get-tuple-element.126), channel_id=1, source_target_pairs={{0,3},{1,0},{2,1},{3,2},{4,7},{5,4},{6,5},{7,6},{8,11},{9,8},{10,9... | collective-permute-start | bytes 589832 | tf_op jit(solution)/shard_map/ppermute | solution.py:258

commit v8 on v7

--- a/solution.py
+++ b/solution.py
@@ -70,9 +70,10 @@
         keep = (label ^ second[pos[2] * k_local + k]) == s
         parts.extend(two_terms(jnp.where(keep, t_ref[k], 0.0)))
     stacked = jnp.concatenate(parts, 0)
-    for n in range(LANES // 128):
-        lanes = slice(n * 128, n * 128 + 128)
-        rows = n * 128 + lax.broadcasted_iota(I32, (128, x_local), 0)
+    width = 256
+    for n in range(LANES // width):
+        lanes = slice(n * width, n * width + width)
+        rows = n * width + lax.broadcasted_iota(I32, (width, x_local), 0)
         hot = jnp.where(rows == place, 1.0, 0.0).astype(BF16)
         g_ref[lanes, :] = hot
         packed = nt(stacked, hot)
@@ -252,7 +253,6 @@
 
     n_lanes, n_passes = (limit.reshape(()) for limit in limits)
     passes = (n_lanes, n_passes, jnp.minimum(n_passes, 1), n_passes > 1)
-    w0, passes = lax.optimization_barrier((w0, passes))
 
     def along(x, axis, step):
         return lax.ppermute(x, axis, [(i, (i + step) % 4) for i in range(4)])
@@ -272,6 +272,7 @@
     for (far, _), piece in list(got.items()):
         got[far, True] = swap(piece)
     pair = lax.ppermute(w0, "row", [(i, i ^ 1) for i in range(4)])
+    pair, passes = lax.optimization_barrier((pair, passes))
     far = lax.ppermute(jnp.stack([w0, pair]), "row", [(i, 3 - i) for i in range(4)])
     t_all, w_all, total = pl.pallas_call(
         functools.partial(place_kernel, list(got)),

time: 65.1 us -> 65 us (level)
  no operation moved by 1% of the time
where the time goes in v8:
time: 65 us; the launch traced here: 64.9 us
  starting transfers between devices  28.9 us (44%)
  waiting for transfers between devices  20.7 us (32%)
  Pallas kernels  12.7 us (20%)
  between operations  1.44 us (2%)
  other arithmetic  0.83 us (1%)
    ppermute x8, waiting for transfers between devices, ring(): return lax.ppermute(x, 'col', [(i, (i + 2 * step) % 16) for i in range(16)])  13.4 us
    ppermute x8, starting transfers between devices, ring(): return lax.ppermute(x, 'col', [(i, (i + 2 * step) % 16) for i in range(16)])  13 us
    ppermute x6, starting transfers between devices, along(): return lax.ppermute(x, axis, [(i, (i + step) % 4) for i in range(4)])  9.86 us
    ppermute x6, waiting for transfers between devices, along(): return lax.ppermute(x, axis, [(i, (i + step) % 4) for i in range(4)])  6.86 us
    pallas_call x1, Pallas kernels, one_pass(): pl.pallas_call(functools.partial(product_kernel, where), out_shape=(shape...  3.51 us
    pallas_call x1, Pallas kernels, one_pass(): pl.pallas_call(expand_kernel, out_shape=shape((1, b_local, x_local), F32)...  3.04 us
    ppermute x1, starting transfers between devices, one_pass(): lax.ppermute(jnp.stack([w0, pair]), 'row', [(i, 3 - i) for i in range(4)])  2.85 us
    pallas_call x1, Pallas kernels, one_pass(): pl.pallas_call(functools.partial(pack_w_kernel, x_local // first.shape[0]...  2.46 us
  transfers between devices with their start and end apart: 25, of which 11 were waited for; matrix products, arithmetic and copies ran while one was open for 0% of the time, Pallas kernels for 6%

profile of v8, /device:TPU:32, one launch (start us, length us, event | category | flops | bytes accessed | tf_op | source)
XLA Modules:
  0.0 64.9 jit_solution(11225710647627060657)
XLA Ops:
  0.0 0.8 %convert_reduce_fusion.starts = s32[16]{0:T(128)S(1)} fusion(s32[768]{0:T(1024)} %param.10), kind=kLoop, calls=%fused_computation.2 | loop fusion | flops 36848 | bytes 3136 | tf_op jit(solution)/shard_map/reduce_sum | solution.py:324
  0.8 0.1 stack.51.pos
  0.9 2.2 %pack_t.2 = (f32[2,48,512]{2,1,0:T(8,128)S(1)}, bf16[512,1536]{1,0:T(8,128)(2,1)S(1)}) custom-call(s32[8]{0:T(128)S(1)} %stack.51.pos, s32[16]{0:T(128)S(1)} %convert_reduce_fusion.starts, s32[8]{0:T(128)} %first.5, s32[8]{0:T(128)} %second.5, f32[2,48,1536]{2,1,0:T(8,128)} %t_ref.1), custom_call_target="tpu_custom_call" | custom-call | tf_op jit(solution)/shard_map/pack_t/pallas_call | solution.py:236
  3.1 2.0 %collective-permute-start.26 = (f32[2,48,512]{2,1,0:T(8,128)S(1)}, f32[2,48,512]{2,1,0:T(8,128)S(1)}, u32[]{:S(2)}, u32[]{:S(2)}) collective-permute-start(f32[2,48,512]{2,1,0:T(8,128)S(1)} %get-tuple-element.115.refs_0_), channel_id=1, source_target_pairs={{0,8},{4,12},{8,16},{12,20},{16,24},{20,28},{24,32},{28,36},{32,40... | collective-permute-start | bytes 589832 | tf_op jit(solution)/shard_map/ppermute | solution.py:264
  5.1 0.1 collective-permute-start.27
  5.2 2.5 %pack_w.2 = (f32[2,192,128]{2,1,0:T(8,128)S(1)}, s32[1]{0:T(128)}, s32[1]{0:T(128)}) custom-call(s32[8]{0:T(128)S(1)} %stack.51.pos, s32[16]{0:T(128)S(1)} %convert_reduce_fusion.starts, s32[8]{0:T(128)} %first.5, s32[8]{0:T(128)} %second.5, s32[16]{0:T(128)} %target.5, f32[2304,128]{1,0:T(8,128)} %bitcast.10.w_ref), custom_call_target="tpu_custom_call" | custom-call | flops 1000000000 | bytes 4000000 | tf_op jit(solution)/shard_map/pack_w/pallas_call | solution.py:244
  7.7 1.6 %collective-permute-start.25 = (f32[2,192,128]{2,1,0:T(8,128)S(1)}, f32[2,192,128]{2,1,0:T(8,128)S(1)}, u32[]{:S(2)}, u32[]{:S(2)}) collective-permute-start(f32[2,192,128]{2,1,0:T(8,128)S(1)} %get-tuple-element.109.refs_14_), channel_id=1, source_target_pairs={{0,64},{64,0},{128,192},{192,128},{1,65},{65,1},{129,193},{193,129... | collective-permute-start | bytes 589832 | tf_op jit(solution)/shard_map/ppermute | solution.py:274
  9.3 0.6 collective-permute-done.26.refs_1_
  9.8 1.9 %collective-permute-start.28 = (f32[2,48,512]{2,1,0:T(8,128)S(1)}, f32[2,48,512]{2,1,0:T(8,128)S(1)}, u32[]{:S(2)}, u32[]{:S(2)}) collective-permute-start(f32[2,48,512]{2,1,0:T(8,128)S(1)} %collective-permute-done.26.refs_1_), channel_id=1, source_target_pairs={{0,8},{4,12},{8,16},{12,20},{16,24},{20,28},{24,32},{28,36},{32,40... | collective-permute-start | bytes 589832 | tf_op jit(solution)/shard_map/ppermute | solution.py:264
  11.7 2.3 %collective-permute-start.29 = (f32[2,48,512]{2,1,0:T(8,128)S(1)}, f32[2,48,512]{2,1,0:T(8,128)S(1)}, u32[]{:S(2)}, u32[]{:S(2)}) collective-permute-start(f32[2,48,512]{2,1,0:T(8,128)S(1)} %collective-permute-done.27.refs_2_), channel_id=1, source_target_pairs={{0,56},{4,60},{8,0},{12,4},{16,8},{20,12},{24,16},{28,20},{32,24},... | collective-permute-start | bytes 589832 | tf_op jit(solution)/shard_map/ppermute | solution.py:264
  15.2 3.2 %collective-permute-done.28.refs_3_ = f32[2,48,512]{2,1,0:T(8,128)S(1)} collective-permute-done((f32[2,48,512]{2,1,0:T(8,128)S(1)}, f32[2,48,512]{2,1,0:T(8,128)S(1)}, u32[]{:S(2)}, u32[]{:S(2)}) %collective-permute-start.28) | collective-permute-done | bytes 196640 | tf_op jit(solution)/shard_map/ppermute | solution.py:264
  18.4 0.0 collective-permute-start.30
  18.4 2.8 %collective-permute-start.39 = (f32[2,2,192,128]{3,2,1,0:T(8,128)S(1)}, f32[2,2,192,128]{3,2,1,0:T(8,128)S(1)}, u32[]{:S(2)}, u32[]{:S(2)}) collective-permute-start(f32[2,2,192,128]{3,2,1,0:T(8,128)S(1)} %pad_maximum_fusion.1), channel_id=1, source_target_pairs={{0,192},{64,128},{128,64},{192,0},{1,193},{65,129},{129,65},{193,1... | collective-permute-start | bytes 1179656 | tf_op jit(solution)/shard_map/ppermute | solution.py:276
  21.2 0.0 collective-permute-done.29.refs_4_
  21.2 3.0 %collective-permute-start.31 = (f32[2,48,512]{2,1,0:T(8,128)S(1)}, f32[2,48,512]{2,1,0:T(8,128)S(1)}, u32[]{:S(2)}, u32[]{:S(2)}) collective-permute-start(f32[2,48,512]{2,1,0:T(8,128)S(1)} %collective-permute-done.29.refs_4_), channel_id=1, source_target_pairs={{0,56},{4,60},{8,0},{12,4},{16,8},{20,12},{24,16},{28,20},{32,24},... | collective-permute-start | bytes 589832 | tf_op jit(solution)/shard_map/ppermute | solution.py:264
  24.2 0.5 collective-permute-start.33
  24.7 0.3 collective-permute-done.30.refs_5_
  25.0 0.0 collective-permute-start.34
  25.0 2.9 %collective-permute-done.31.refs_6_ = f32[2,48,512]{2,1,0:T(8,128)S(1)} collective-permute-done((f32[2,48,512]{2,1,0:T(8,128)S(1)}, f32[2,48,512]{2,1,0:T(8,128)S(1)}, u32[]{:S(2)}, u32[]{:S(2)}) %collective-permute-start.31) | collective-permute-done | bytes 196640 | tf_op jit(solution)/shard_map/ppermute | solution.py:264
  27.9 0.0 copy-start.4
  27.9 0.0 copy-start.5
  27.9 0.6 collective-permute-start.36
  28.5 0.0 collective-permute-done.33.refs_8_
  28.5 3.7 %collective-permute-start.40 = (f32[1,48,512]{2,1,0:T(8,128)S(1)}, f32[1,48,512]{2,1,0:T(8,128)S(1)}, u32[]{:S(2)}, u32[]{:S(2)}) collective-permute-start(f32[1,48,512]{2,1,0:T(8,128)S(1)} %slice.16), channel_id=1, source_target_pairs={{0,8},{4,12},{8,16},{12,20},{16,24},{20,28},{24,32},{28,36},{32,40... | collective-permute-start | bytes 294920 | tf_op jit(solution)/shard_map/ppermute | solution.py:264
  32.2 0.0 collective-permute-done.34.refs_9_
  32.2 0.0 collective-permute-start.37
  32.2 0.0 collective-permute-done.39.refs_16_
  32.2 0.5 collective-permute-start.38
  32.7 0.0 collective-permute-start.41
  32.7 1.8 %collective-permute-done.40.refs_0_ = f32[1,48,512]{2,1,0:T(8,128)S(1)} collective-permute-done((f32[1,48,512]{2,1,0:T(8,128)S(1)}, f32[1,48,512]{2,1,0:T(8,128)S(1)}, u32[]{:S(2)}, u32[]{:S(2)}) %collective-permute-start.40) | collective-permute-done | bytes 98336 | tf_op jit(solution)/shard_map/ppermute | solution.py:264
  34.5 4.8 %collective-permute-done.41.refs_1_ = f32[1,48,512]{2,1,0:T(8,128)S(1)} collective-permute-done((f32[1,48,512]{2,1,0:T(8,128)S(1)}, f32[1,48,512]{2,1,0:T(8,128)S(1)}, u32[]{:S(2)}, u32[]{:S(2)}) %collective-permute-start.41) | collective-permute-done | bytes 98336 | tf_op jit(solution)/shard_map/ppermute | solution.py:264
  39.3 0.9 %place.2 = (f32[2,768,512]{2,1,0:T(8,128)S(1)}, f32[2,768,128]{2,1,0:T(8,128)S(1)}, f32[896,512]{1,0:T(8,128)S(1)}) custom-call(s32[8]{0:T(128)S(1)} %stack.51.pos, f32[2,48,512]{2,1,0:T(8,128)S(1)} %get-tuple-element.115.refs_0_, f32[2,48,512]{2,1,0:T(8,128)S(1)} %collective-permute-done.26.refs_1_, f32[2,48,512]{2,1,0:T(8,128)S(1)} %collective-permute-done.27.refs_2_, ...), custom_call_target="tpu_custom_call" | custom-call | bytes 7000000 | tf_op jit(solution)/shard_map/place/pallas_call | solution.py:277
  40.2 0.3 collective-permute-done.43.refs_3_
  40.6 3.5 %product.2 = (f32[2,768,512]{2,1,0:T(8,128)S(1)}, f32[896,512]{1,0:T(8,128)S(1)}, f32[96,512]{1,0:T(8,128)S(1)}, f32[96,512]{1,0:T(8,128)S(1)}, f32[96,512]{1,0:T(8,128)S(1)}, /*index=5*/f32[96,512]{1,0:T(8,128)S(1)}) custom-call(s32[8]{0:T(128)S(1)} %stack.51.pos, s32[16]{0:T(128)S(1)} %convert_reduce_fusion.starts, ...), custom_call_target="tpu_custom_call", output_to_operand_aliasing={{0}: (4, {}), {1}: (5, {})} | custom-call | tf_op jit(solution)/shard_map/product/pallas_call | solution.py:289
  44.1 0.0 copy-start.3
  44.1 1.7 %collective-permute-start.44 = (f32[96,512]{1,0:T(8,128)S(1)}, f32[96,512]{1,0:T(8,128)S(1)}, u32[]{:S(2)}, u32[]{:S(2)}) collective-permute-start(f32[96,512]{1,0:T(8,128)S(1)} %get-tuple-element.121), channel_id=1, source_target_pairs={{0,1},{1,2},{2,3},{3,0},{4,5},{5,6},{6,7},{7,4},{8,9},{9,10},{10,1... | collective-permute-start | bytes 589832 | tf_op jit(solution)/shard_map/ppermute | solution.py:258
  45.7 1.7 %collective-permute-start.45 = (f32[96,512]{1,0:T(8,128)S(1)}, f32[96,512]{1,0:T(8,128)S(1)}, u32[]{:S(2)}, u32[]{:S(2)}) collective-permute-start(f32[96,512]{1,0:T(8,128)S(1)} %get-tuple-element.122), channel_id=1, source_target_pairs={{0,3},{1,0},{2,1},{3,2},{4,7},{5,4},{6,5},{7,6},{8,11},{9,8},{10,9... | collective-permute-start | bytes 589832 | tf_op jit(solution)/shard_map/ppermute | solution.py:258
  47.4 0.4 collective-permute-start.47
  47.8 2.9 %collective-permute-start.48 = (f32[96,512]{1,0:T(8,128)S(1)}, f32[96,512]{1,0:T(8,128)S(1)}, u32[]{:S(2)}, u32[]{:S(2)}) collective-permute-start(f32[96,512]{1,0:T(8,128)S(1)} %get-tuple-element.125), channel_id=1, source_target_pairs={{0,3},{1,0},{2,1},{3,2},{4,7},{5,4},{6,5},{7,6},{8,11},{9,8},{10,9... | collective-permute-start | bytes 589832 | tf_op jit(solution)/shard_map/ppermute | solution.py:258
  50.6 2.5 %collective-permute-done.44.relay_up = f32[96,512]{1,0:T(8,128)S(1)} collective-permute-done((f32[96,512]{1,0:T(8,128)S(1)}, f32[96,512]{1,0:T(8,128)S(1)}, u32[]{:S(2)}, u32[]{:S(2)}) %collective-permute-start.44) | collective-permute-done | bytes 196640 | tf_op jit(solution)/shard_map/ppermute | solution.py:258
  53.2 0.4 collective-permute-done.45.relay_down
  53.5 0.6 join.2
  54.1 1.6 %collective-permute-start.46 = (f32[96,512]{1,0:T(8,128)S(1)}, f32[96,512]{1,0:T(8,128)S(1)}, u32[]{:S(2)}, u32[]{:S(2)}) collective-permute-start(f32[96,512]{1,0:T(8,128)S(1)} %get-tuple-element.123), channel_id=1, source_target_pairs={{0,1},{1,2},{2,3},{3,0},{4,5},{5,6},{6,7},{7,4},{8,9},{9,10},{10,1... | collective-permute-start | bytes 589832 | tf_op jit(solution)/shard_map/ppermute | solution.py:258
  55.7 1.7 %collective-permute-start.49 = (f32[96,512]{1,0:T(8,128)S(1)}, f32[96,512]{1,0:T(8,128)S(1)}, u32[]{:S(2)}, u32[]{:S(2)}) collective-permute-start(f32[96,512]{1,0:T(8,128)S(1)} %get-tuple-element.126), channel_id=1, source_target_pairs={{0,3},{1,0},{2,1},{3,2},{4,7},{5,4},{6,5},{7,6},{8,11},{9,8},{10,9... | collective-permute-start | bytes 589832 | tf_op jit(solution)/shard_map/ppermute | solution.py:258
  57.4 3.6 %collective-permute-done.46.refs_1_ = f32[96,512]{1,0:T(8,128)S(1)} collective-permute-done((f32[96,512]{1,0:T(8,128)S(1)}, f32[96,512]{1,0:T(8,128)S(1)}, u32[]{:S(2)}, u32[]{:S(2)}) %collective-permute-start.46) | collective-permute-done | bytes 196640 | tf_op jit(solution)/shard_map/ppermute | solution.py:258
  61.1 0.3 collective-permute-done.49.refs_4_
  61.4 3.0 %expand.2 = f32[1,192,1536]{2,1,0:T(8,128)} custom-call(s32[8]{0:T(128)S(1)} %stack.51.pos, s32[16]{0:T(128)S(1)} %convert_reduce_fusion.starts, s32[8]{0:T(128)S(1)} %copy-done.3, s32[16]{0:T(128)S(1)} %copy-done.5, bf16[512,1536]{1,0:T(8,128)(2,1)S(1)} %get-tuple-element.114.g_ref, f32[896,512]{1,0:T(8,128)S(1)} %get-tuple-element.120.total.refs_0_, ...), custom_call_target="tpu_custom_call" | custom-call | tf_op jit(solution)/shard_map/expand/pallas_call | solution.py:311
  64.5 0.2 while.12
  (21 shorter events, 0.1 us)
Async XLA Ops:
  3.1 6.7 %collective-permute-start.26 = (f32[2,48,512]{2,1,0:T(8,128)S(1)}, f32[2,48,512]{2,1,0:T(8,128)S(1)}, u32[]{:S(2)}, u32[]{:S(2)}) collective-permute-start(f32[2,48,512]{2,1,0:T(8,128)S(1)} %get-tuple-element.115.refs_0_), channel_id=1, source_target_pairs={{0,8},{4,12},{8,16},{12,20},{16,24},{20,28},{24,32},{28,36},{32,40... | collective-permute-start | bytes 589832 | tf_op jit(solution)/shard_map/ppermute | solution.py:264
  5.1 6.6 %collective-permute-start.27 = (f32[2,48,512]{2,1,0:T(8,128)S(1)}, f32[2,48,512]{2,1,0:T(8,128)S(1)}, u32[]{:S(2)}, u32[]{:S(2)}) collective-permute-start(f32[2,48,512]{2,1,0:T(8,128)S(1)} %get-tuple-element.115.refs_0_), channel_id=1, source_target_pairs={{0,56},{4,60},{8,0},{12,4},{16,8},{20,12},{24,16},{28,20},{32,24},... | collective-permute-start | bytes 589832 | tf_op jit(solution)/shard_map/ppermute | solution.py:264
  7.7 7.5 %collective-permute-start.25 = (f32[2,192,128]{2,1,0:T(8,128)S(1)}, f32[2,192,128]{2,1,0:T(8,128)S(1)}, u32[]{:S(2)}, u32[]{:S(2)}) collective-permute-start(f32[2,192,128]{2,1,0:T(8,128)S(1)} %get-tuple-element.109.refs_14_), channel_id=1, source_target_pairs={{0,64},{64,0},{128,192},{192,128},{1,65},{65,1},{129,193},{193,129... | collective-permute-start | bytes 589832 | tf_op jit(solution)/shard_map/ppermute | solution.py:274
  9.8 8.5 %collective-permute-start.28 = (f32[2,48,512]{2,1,0:T(8,128)S(1)}, f32[2,48,512]{2,1,0:T(8,128)S(1)}, u32[]{:S(2)}, u32[]{:S(2)}) collective-permute-start(f32[2,48,512]{2,1,0:T(8,128)S(1)} %collective-permute-done.26.refs_1_), channel_id=1, source_target_pairs={{0,8},{4,12},{8,16},{12,20},{16,24},{20,28},{24,32},{28,36},{32,40... | collective-permute-start | bytes 589832 | tf_op jit(solution)/shard_map/ppermute | solution.py:264
  11.7 9.5 %collective-permute-start.29 = (f32[2,48,512]{2,1,0:T(8,128)S(1)}, f32[2,48,512]{2,1,0:T(8,128)S(1)}, u32[]{:S(2)}, u32[]{:S(2)}) collective-permute-start(f32[2,48,512]{2,1,0:T(8,128)S(1)} %collective-permute-done.27.refs_2_), channel_id=1, source_target_pairs={{0,56},{4,60},{8,0},{12,4},{16,8},{20,12},{24,16},{28,20},{32,24},... | collective-permute-start | bytes 589832 | tf_op jit(solution)/shard_map/ppermute | solution.py:264
  18.4 6.6 %collective-permute-start.30 = (f32[2,48,512]{2,1,0:T(8,128)S(1)}, f32[2,48,512]{2,1,0:T(8,128)S(1)}, u32[]{:S(2)}, u32[]{:S(2)}) collective-permute-start(f32[2,48,512]{2,1,0:T(8,128)S(1)} %collective-permute-done.28.refs_3_), channel_id=1, source_target_pairs={{0,8},{4,12},{8,16},{12,20},{16,24},{20,28},{24,32},{28,36},{32,40... | collective-permute-start | bytes 589832 | tf_op jit(solution)/shard_map/ppermute | solution.py:264
  18.4 13.8 %collective-permute-start.39 = (f32[2,2,192,128]{3,2,1,0:T(8,128)S(1)}, f32[2,2,192,128]{3,2,1,0:T(8,128)S(1)}, u32[]{:S(2)}, u32[]{:S(2)}) collective-permute-start(f32[2,2,192,128]{3,2,1,0:T(8,128)S(1)} %pad_maximum_fusion.1), channel_id=1, source_target_pairs={{0,192},{64,128},{128,64},{192,0},{1,193},{65,129},{129,65},{193,1... | collective-permute-start | bytes 1179656 | tf_op jit(solution)/shard_map/ppermute | solution.py:276
  21.2 6.6 %collective-permute-start.31 = (f32[2,48,512]{2,1,0:T(8,128)S(1)}, f32[2,48,512]{2,1,0:T(8,128)S(1)}, u32[]{:S(2)}, u32[]{:S(2)}) collective-permute-start(f32[2,48,512]{2,1,0:T(8,128)S(1)} %collective-permute-done.29.refs_4_), channel_id=1, source_target_pairs={{0,56},{4,60},{8,0},{12,4},{16,8},{20,12},{24,16},{28,20},{32,24},... | collective-permute-start | bytes 589832 | tf_op jit(solution)/shard_map/ppermute | solution.py:264
  24.2 3.7 %collective-permute-start.32 = (f32[2,48,512]{2,1,0:T(8,128)S(1)}, f32[2,48,512]{2,1,0:T(8,128)S(1)}, u32[]{:S(2)}, u32[]{:S(2)}) collective-permute-start(f32[2,48,512]{2,1,0:T(8,128)S(1)} %get-tuple-element.115.refs_0_), channel_id=1, source_target_pairs={{0,4},{4,0},{8,12},{12,8},{16,20},{20,16},{24,28},{28,24},{32,36},... | collective-permute-start | bytes 589832 | tf_op jit(solution)/shard_map/ppermute | solution.py:261
  24.2 4.3 %collective-permute-start.33 = (f32[2,48,512]{2,1,0:T(8,128)S(1)}, f32[2,48,512]{2,1,0:T(8,128)S(1)}, u32[]{:S(2)}, u32[]{:S(2)}) collective-permute-start(f32[2,48,512]{2,1,0:T(8,128)S(1)} %collective-permute-done.26.refs_1_), channel_id=1, source_target_pairs={{0,4},{4,0},{8,12},{12,8},{16,20},{20,16},{24,28},{28,24},{32,36},... | collective-permute-start | bytes 589832 | tf_op jit(solution)/shard_map/ppermute | solution.py:261
  25.0 7.2 %collective-permute-start.34 = (f32[2,48,512]{2,1,0:T(8,128)S(1)}, f32[2,48,512]{2,1,0:T(8,128)S(1)}, u32[]{:S(2)}, u32[]{:S(2)}) collective-permute-start(f32[2,48,512]{2,1,0:T(8,128)S(1)} %collective-permute-done.27.refs_2_), channel_id=1, source_target_pairs={{0,4},{4,0},{8,12},{12,8},{16,20},{20,16},{24,28},{28,24},{32,36},... | collective-permute-start | bytes 589832 | tf_op jit(solution)/shard_map/ppermute | solution.py:261
  27.8 4.9 %collective-permute-start.35 = (f32[2,48,512]{2,1,0:T(8,128)S(1)}, f32[2,48,512]{2,1,0:T(8,128)S(1)}, u32[]{:S(2)}, u32[]{:S(2)}) collective-permute-start(f32[2,48,512]{2,1,0:T(8,128)S(1)} %collective-permute-done.28.refs_3_), channel_id=1, source_target_pairs={{0,4},{4,0},{8,12},{12,8},{16,20},{20,16},{24,28},{28,24},{32,36},... | collective-permute-start | bytes 589832 | tf_op jit(solution)/shard_map/ppermute | solution.py:261
  27.9 12.7 %copy-start.4 = (s32[8]{0:T(128)S(1)}, s32[8]{0:T(128)}, u32[]{:S(2)}) copy-start(s32[8]{0:T(128)} %second.5) | copy-start | bytes 100
  27.9 12.7 %copy-start.5 = (s32[16]{0:T(128)S(1)}, s32[16]{0:T(128)}, u32[]{:S(2)}) copy-start(s32[16]{0:T(128)} %target.5) | copy-start | bytes 196
  27.9 11.4 %collective-permute-start.36 = (f32[2,48,512]{2,1,0:T(8,128)S(1)}, f32[2,48,512]{2,1,0:T(8,128)S(1)}, u32[]{:S(2)}, u32[]{:S(2)}) collective-permute-start(f32[2,48,512]{2,1,0:T(8,128)S(1)} %collective-permute-done.29.refs_4_), channel_id=1, source_target_pairs={{0,4},{4,0},{8,12},{12,8},{16,20},{20,16},{24,28},{28,24},{32,36},... | collective-permute-start | bytes 589832 | tf_op jit(solution)/shard_map/ppermute | solution.py:261
  28.5 6.0 %collective-permute-start.40 = (f32[1,48,512]{2,1,0:T(8,128)S(1)}, f32[1,48,512]{2,1,0:T(8,128)S(1)}, u32[]{:S(2)}, u32[]{:S(2)}) collective-permute-start(f32[1,48,512]{2,1,0:T(8,128)S(1)} %slice.16), channel_id=1, source_target_pairs={{0,8},{4,12},{8,16},{12,20},{16,24},{20,28},{24,32},{28,36},{32,40... | collective-permute-start | bytes 294920 | tf_op jit(solution)/shard_map/ppermute | solution.py:264
  32.2 7.1 %collective-permute-start.37 = (f32[2,48,512]{2,1,0:T(8,128)S(1)}, f32[2,48,512]{2,1,0:T(8,128)S(1)}, u32[]{:S(2)}, u32[]{:S(2)}) collective-permute-start(f32[2,48,512]{2,1,0:T(8,128)S(1)} %collective-permute-done.30.refs_5_), channel_id=1, source_target_pairs={{0,4},{4,0},{8,12},{12,8},{16,20},{20,16},{24,28},{28,24},{32,36},... | collective-permute-start | bytes 589832 | tf_op jit(solution)/shard_map/ppermute | solution.py:261
  32.2 7.1 %collective-permute-start.38 = (f32[2,48,512]{2,1,0:T(8,128)S(1)}, f32[2,48,512]{2,1,0:T(8,128)S(1)}, u32[]{:S(2)}, u32[]{:S(2)}) collective-permute-start(f32[2,48,512]{2,1,0:T(8,128)S(1)} %collective-permute-done.31.refs_6_), channel_id=1, source_target_pairs={{0,4},{4,0},{8,12},{12,8},{16,20},{20,16},{24,28},{28,24},{32,36},... | collective-permute-start | bytes 589832 | tf_op jit(solution)/shard_map/ppermute | solution.py:261
  32.7 6.6 %collective-permute-start.41 = (f32[1,48,512]{2,1,0:T(8,128)S(1)}, f32[1,48,512]{2,1,0:T(8,128)S(1)}, u32[]{:S(2)}, u32[]{:S(2)}) collective-permute-start(f32[1,48,512]{2,1,0:T(8,128)S(1)} %slice.17), channel_id=1, source_target_pairs={{0,56},{4,60},{8,0},{12,4},{16,8},{20,12},{24,16},{28,20},{32,24},... | collective-permute-start | bytes 294920 | tf_op jit(solution)/shard_map/ppermute | solution.py:264
  34.5 5.7 %collective-permute-start.42 = (f32[1,48,512]{2,1,0:T(8,128)S(1)}, f32[1,48,512]{2,1,0:T(8,128)S(1)}, u32[]{:S(2)}, u32[]{:S(2)}) collective-permute-start(f32[1,48,512]{2,1,0:T(8,128)S(1)} %collective-permute-done.40.refs_0_), channel_id=1, source_target_pairs={{0,4},{4,0},{8,12},{12,8},{16,20},{20,16},{24,28},{28,24},{32,36},... | collective-permute-start | bytes 294920 | tf_op jit(solution)/shard_map/ppermute | solution.py:261
  39.3 1.3 %collective-permute-start.43 = (f32[1,48,512]{2,1,0:T(8,128)S(1)}, f32[1,48,512]{2,1,0:T(8,128)S(1)}, u32[]{:S(2)}, u32[]{:S(2)}) collective-permute-start(f32[1,48,512]{2,1,0:T(8,128)S(1)} %collective-permute-done.41.refs_1_), channel_id=1, source_target_pairs={{0,4},{4,0},{8,12},{12,8},{16,20},{20,16},{24,28},{28,24},{32,36},... | collective-permute-start | bytes 294920 | tf_op jit(solution)/shard_map/ppermute | solution.py:261
  44.1 17.3 %copy-start.3 = (s32[8]{0:T(128)S(1)}, s32[8]{0:T(128)}, u32[]{:S(2)}) copy-start(s32[8]{0:T(128)} %first.5) | copy-start | bytes 100
  44.1 9.1 %collective-permute-start.44 = (f32[96,512]{1,0:T(8,128)S(1)}, f32[96,512]{1,0:T(8,128)S(1)}, u32[]{:S(2)}, u32[]{:S(2)}) collective-permute-start(f32[96,512]{1,0:T(8,128)S(1)} %get-tuple-element.121), channel_id=1, source_target_pairs={{0,1},{1,2},{2,3},{3,0},{4,5},{5,6},{6,7},{7,4},{8,9},{9,10},{10,1... | collective-permute-start | bytes 589832 | tf_op jit(solution)/shard_map/ppermute | solution.py:258
  45.7 7.8 %collective-permute-start.45 = (f32[96,512]{1,0:T(8,128)S(1)}, f32[96,512]{1,0:T(8,128)S(1)}, u32[]{:S(2)}, u32[]{:S(2)}) collective-permute-start(f32[96,512]{1,0:T(8,128)S(1)} %get-tuple-element.122), channel_id=1, source_target_pairs={{0,3},{1,0},{2,1},{3,2},{4,7},{5,4},{6,5},{7,6},{8,11},{9,8},{10,9... | collective-permute-start | bytes 589832 | tf_op jit(solution)/shard_map/ppermute | solution.py:258
  47.4 10.0 %collective-permute-start.47 = (f32[96,512]{1,0:T(8,128)S(1)}, f32[96,512]{1,0:T(8,128)S(1)}, u32[]{:S(2)}, u32[]{:S(2)}) collective-permute-start(f32[96,512]{1,0:T(8,128)S(1)} %get-tuple-element.124), channel_id=1, source_target_pairs={{0,1},{1,2},{2,3},{3,0},{4,5},{5,6},{6,7},{7,4},{8,9},{9,10},{10,1... | collective-permute-start | bytes 589832 | tf_op jit(solution)/shard_map/ppermute | solution.py:258
  47.8 9.7 %collective-permute-start.48 = (f32[96,512]{1,0:T(8,128)S(1)}, f32[96,512]{1,0:T(8,128)S(1)}, u32[]{:S(2)}, u32[]{:S(2)}) collective-permute-start(f32[96,512]{1,0:T(8,128)S(1)} %get-tuple-element.125), channel_id=1, source_target_pairs={{0,3},{1,0},{2,1},{3,2},{4,7},{5,4},{6,5},{7,6},{8,11},{9,8},{10,9... | collective-permute-start | bytes 589832 | tf_op jit(solution)/shard_map/ppermute | solution.py:258
  54.1 7.0 %collective-permute-start.46 = (f32[96,512]{1,0:T(8,128)S(1)}, f32[96,512]{1,0:T(8,128)S(1)}, u32[]{:S(2)}, u32[]{:S(2)}) collective-permute-start(f32[96,512]{1,0:T(8,128)S(1)} %get-tuple-element.123), channel_id=1, source_target_pairs={{0,1},{1,2},{2,3},{3,0},{4,5},{5,6},{6,7},{7,4},{8,9},{9,10},{10,1... | collective-permute-start | bytes 589832 | tf_op jit(solution)/shard_map/ppermute | solution.py:258
  55.7 5.7 %collective-permute-start.49 = (f32[96,512]{1,0:T(8,128)S(1)}, f32[96,512]{1,0:T(8,128)S(1)}, u32[]{:S(2)}, u32[]{:S(2)}) collective-permute-start(f32[96,512]{1,0:T(8,128)S(1)} %get-tuple-element.126), channel_id=1, source_target_pairs={{0,3},{1,0},{2,1},{3,2},{4,7},{5,4},{6,5},{7,6},{8,11},{9,8},{10,9... | collective-permute-start | bytes 589832 | tf_op jit(solution)/shard_map/ppermute | solution.py:258
